TPU v7x, 32 devices: a whole 2x2x4 slice. The times are simulated.
32 devices in a mesh: dp: 8 (over z, y), tp: 4 (over x, core).
Axes of the slice: x: 2, y: 2, z: 4, core: 2. Of those that a mesh axis runs over, the one named last changes fastest.
Arguments:
- inputs: bfloat16 [16384, 2048], P(('dp', 'tp')), may hold values from -6 to 6
- sentence_ids: int32 [32, 512], P(('dp', 'tp')), may hold values from 0 to 3, never falling along the last dimension, each value on 1 to 192 neighbouring positions
- start_states: float32 [128, 2048], P(('dp', 'tp')), may hold values from -5 to 5
- ln_gain: float32 [2048], replicated, may hold values from 0.1 to 1.9
- ln_bias: float32 [2048], replicated, may hold values from -3 to 3
- weight: bfloat16 [6144, 2048], P('tp'), may hold values from -0.125 to 0.125
- gate_bias: float32 [2, 2048], replicated, may hold values from -2 to 4
- out_grad: bfloat16 [16384, 2048], P(('dp', 'tp')), may hold values from -6 to 6
Outputs:
- output: bfloat16 [16384, 2048], P(('dp', 'tp'))
- final_states: float32 [128, 2048], P(('dp', 'tp'))
- input_grad: float32 [16384, 2048], P(('dp', 'tp'))
- weight_grad: float32 [6144, 2048], P('tp')
- gate_bias_grad: float32 [2, 2048], replicated
- ln_gain_grad: float32 [2048], replicated
- ln_bias_grad: float32 [2048], replicated
- start_grad: float32 [128, 2048], P(('dp', 'tp'))
Inputs may be any that keep to these rules, and one draw needn't show every extreme that they name: `sentence_ids`: each row holds the sentence ids of one device's tokens in order: never falling, every id of 0 to 3 present, each sentence 1 to 192 tokens and some sentence exactly 192.
All inputs are finite; a program needn't handle non-finite values.
Results may differ from a plain program's by a relative error of at most 0.006.
Values may be sent and summed in bfloat16 or wider, within the bound.
No kernel may reach another device: no remote copies, remote signals or barrier semaphores. Data moves between devices by JAX's collectives and lax.ppermute only.
A program may use at most 256 MiB of HBM per device.

v0:
```python
import jax
import jax.numpy as jnp
from jax import lax
from jax.sharding import PartitionSpec as P

SENT_DEV = 4


def link(first, second):
    first_decay, first_value = first
    second_decay, second_value = second
    return (first_decay * second_decay, second_decay * first_value + second_value)


def local(inputs, sentence_ids, start_states, ln_gain, ln_bias, weight, gate_bias, out_grad):
    width = inputs.shape[1]
    signal = inputs.astype(jnp.float32)
    centred = signal - jnp.mean(signal, axis=1, keepdims=True)
    rstd = lax.rsqrt(jnp.mean(centred * centred, axis=1, keepdims=True) + 1e-05)
    scaled_in = centred * rstd
    normed = scaled_in * ln_gain + ln_bias
    normed_low = normed.astype(jnp.bfloat16)
    contract_last = (((1,), (1,)), ((), ()))
    contract_first = (((0,), (0,)), ((), ()))
    streams = lax.dot_general(
        normed_low,
        lax.all_gather(weight, "tp", axis=0, tiled=True),
        contract_last,
        preferred_element_type=jnp.float32,
    ).astype(jnp.bfloat16)
    stream_vals = streams.astype(jnp.float32)
    candidate = stream_vals[:, :width]
    forget = jax.nn.sigmoid(stream_vals[:, width : 2 * width] + gate_bias[0])
    reset = jax.nn.sigmoid(stream_vals[:, 2 * width :] + gate_bias[1])
    seg_row = sentence_ids[0]
    first_mask = jnp.concatenate([jnp.ones((1,), bool), seg_row[1:] != seg_row[:-1]])[:, None]
    last_mask = jnp.concatenate([seg_row[:-1] != seg_row[1:], jnp.ones((1,), bool)])[:, None]
    table = (seg_row[:, None] == jnp.arange(SENT_DEV, dtype=jnp.int32)[None, :]).astype(jnp.float32)
    begin = jnp.dot(table, start_states, precision=lax.Precision.HIGHEST)
    zeros_like = jnp.zeros_like(forget)
    decay = jnp.where(first_mask, zeros_like, forget)
    drive = (1.0 - forget) * candidate + jnp.where(first_mask, forget * begin, zeros_like)
    unused, cells = lax.associative_scan(link, (decay, drive), axis=0)
    output = (signal + reset * cells + (1.0 - reset) * normed).astype(jnp.bfloat16)
    picker = table * last_mask.astype(jnp.float32)
    final_states = lax.dot_general(picker, cells, contract_first, precision=lax.Precision.HIGHEST)
    outer = out_grad.astype(jnp.float32)
    shifted = jnp.concatenate([jnp.zeros((1, width), jnp.float32), cells[:-1]], axis=0)
    previous = jnp.where(first_mask, begin, shifted)
    reset_pre_grad = outer * (cells - normed) * reset * (1.0 - reset)
    direct = outer * reset
    next_decay = jnp.concatenate([decay[1:], jnp.zeros((1, width), jnp.float32)], axis=0)
    unused_back, carry_grad = lax.associative_scan(link, (next_decay, direct), reverse=True, axis=0)
    candidate_grad = carry_grad * (1.0 - forget)
    forget_pre_grad = carry_grad * (previous - candidate) * forget * (1.0 - forget)
    start_terms = jnp.where(first_mask, forget * carry_grad, zeros_like)
    start_grad = lax.dot_general(
        table, start_terms, contract_first, precision=lax.Precision.HIGHEST
    )
    stream_grads = jnp.concatenate(
        [candidate_grad, forget_pre_grad, reset_pre_grad], axis=1
    ).astype(jnp.bfloat16)
    bias_part = jnp.stack([jnp.sum(forget_pre_grad, axis=0), jnp.sum(reset_pre_grad, axis=0)])
    columns = stream_grads
    projected_grad = jnp.dot(
        columns,
        lax.all_gather(weight, "tp", axis=0, tiled=True),
        preferred_element_type=jnp.float32,
    )
    columns = stream_grads
    weight_part = lax.psum_scatter(
        lax.dot_general(columns, normed_low, contract_first, preferred_element_type=jnp.float32),
        "tp",
        scatter_dimension=0,
        tiled=True,
    )
    normed_grad = projected_grad + outer * (1.0 - reset)
    gain_part = jnp.sum(normed_grad * scaled_in, axis=0)
    shift_part = jnp.sum(normed_grad, axis=0)
    scaled_grad = normed_grad * ln_gain
    input_grad = (
        rstd
        * (
            scaled_grad
            - jnp.mean(scaled_grad, axis=1, keepdims=True)
            - scaled_in * jnp.mean(scaled_grad * scaled_in, axis=1, keepdims=True)
        )
        + outer
    )
    weight_grad = lax.psum(weight_part, "dp")
    bias_grad, gain_grad, shift_grad = lax.psum((bias_part, gain_part, shift_part), ("dp", "tp"))
    return (
        output,
        final_states,
        input_grad,
        weight_grad,
        bias_grad,
        gain_grad,
        shift_grad,
        start_grad,
    )


def solution(mesh):
    placed = (
        P(("dp", "tp"), None),
        P(("dp", "tp"), None),
        P(("dp", "tp"), None),
        P(),
        P(),
        P("tp", None),
        P(),
        P(("dp", "tp"), None),
    )
    return jax.shard_map(
        local,
        mesh=mesh,
        in_specs=placed,
        out_specs=(
            P(("dp", "tp"), None),
            P(("dp", "tp"), None),
            P(("dp", "tp"), None),
            P("tp", None),
            P(),
            P(),
            P(),
            P(("dp", "tp"), None),
        ),
        check_vma=False,
    )
```

profile of v0, /device:TPU:0, one launch (start us, length us, event | category | flops | bytes accessed | tf_op | source)
XLA Modules:
  0.0 1565.2 jit_solution(1547898737292328093)
XLA Ops:
  10.5 156.7 %all-gather.2.cloned.1.call-done = bf16[6144,2048]{1,0:T(8,128)(2,1)} async-done(((bf16[1536,2048]{1,0:T(8,128)(2,1)}), bf16[6144,2048]{1,0:T(8,128)(2,1)}) %all-gather.2.cloned.1.call-update) | async-done | bytes 25165840 | tf_op jit(solution)/shard_map/all_gather | solution.py:27
  167.2 19.4 %fusion = f32[512,6144]{1,0:T(8,128)} fusion(bf16[6144,2048]{1,0:T(8,128)(2,1)} %all-gather.2.cloned.1.call-done, bf16[512,2048]{1,0:T(8,128)(2,1)S(1)} %copy-done.4, f32[2048]{0:T(1024)S(1)} %copy-done.30, f32[2048]{0:T(1024)S(1)} %copy-done.20, f32[512]{0:T(512)S(1)} %add_rsqrt_fusion, f32[512]{0:T(512)S(1)} %broadcast_multiply_fusion.2), kind=kOutput, calls=%fused_computation.1 | convolution fusion | flops 12897484800 | bytes 39866368 | tf_op jit(solution)/shard_map/dot_general | solution.py:25
  195.2 9.8 slice.477
  205.0 9.8 slice.473
  214.8 10.1 slice.472
  229.8 9.8 slice.549
  239.6 9.8 slice.542
  249.4 9.8 slice.540
  260.1 10.0 slice.537
  270.2 9.8 slice.475
  280.0 9.8 slice.474
  402.9 16.5 %pad.128 = f32[512,2048]{1,0:T(8,128)} pad(f32[256,2048]{1,0:T(8,128)} %pad_maximum_fusion.3, f32[]{:T(128)} %constant.15.clone.1), padding=0_1_1x0_0_0 | pad | bytes 6291460 | tf_op jit(solution)/shard_map/pad | solution.py:43
  419.3 16.6 %pad.129 = f32[512,2048]{1,0:T(8,128)} pad(f32[256,2048]{1,0:T(8,128)} %add.338, f32[]{:T(128)} %constant.15.clone.1), padding=1_0_1x0_0_0 | pad | bytes 6291460 | tf_op jit(solution)/shard_map/pad | solution.py:43
  453.2 9.8 slice.610
  463.1 9.9 slice.546
  472.9 9.8 slice.544
  482.8 16.7 %slice.550 = f32[256,2048]{1,0:T(8,128)} reverse(f32[256,2048]{1,0:T(8,128)} %slice.549), dimensions={0} | reverse | bytes 4194304 | tf_op jit(solution)/shard_map/slice | solution.py:53
  499.4 16.7 %slice.543 = f32[256,2048]{1,0:T(8,128)} reverse(f32[256,2048]{1,0:T(8,128)} %slice.542), dimensions={0} | reverse | bytes 4194304 | tf_op jit(solution)/shard_map/slice | solution.py:53
  516.2 16.6 %slice.545 = f32[256,2048]{1,0:T(8,128)} reverse(f32[256,2048]{1,0:T(8,128)} %slice.544), dimensions={0} | reverse | bytes 4194304 | tf_op jit(solution)/shard_map/slice | solution.py:53
  532.8 16.7 %slice.547 = f32[256,2048]{1,0:T(8,128)} reverse(f32[256,2048]{1,0:T(8,128)} %slice.546), dimensions={0} | reverse | bytes 4194304 | tf_op jit(solution)/shard_map/slice | solution.py:53
  617.8 17.0 %slice.541 = f32[255,2048]{1,0:T(8,128)} reverse(f32[255,2048]{1,0:T(8,128)} %slice.540), dimensions={0} | reverse | bytes 4177920 | tf_op jit(solution)/shard_map/slice | solution.py:53
  634.8 17.1 %slice.611 = f32[255,2048]{1,0:T(8,128)} reverse(f32[255,2048]{1,0:T(8,128)} %slice.610), dimensions={0} | reverse | bytes 4177920 | tf_op jit(solution)/shard_map/slice | solution.py:53
  692.3 16.6 %pad.146 = f32[512,2048]{1,0:T(8,128)} pad(f32[256,2048]{1,0:T(8,128)} %pad_maximum_fusion.4, f32[]{:T(128)} %constant.15.clone.1), padding=0_1_1x0_0_0 | pad | bytes 6291460 | tf_op jit(solution)/shard_map/pad | solution.py:53
  708.9 16.5 %pad.147 = f32[512,2048]{1,0:T(8,128)} pad(f32[256,2048]{1,0:T(8,128)} %add.366, f32[]{:T(128)} %constant.15.clone.1), padding=1_0_1x0_0_0 | pad | bytes 6291460 | tf_op jit(solution)/shard_map/pad | solution.py:53
  732.0 32.6 %rev.2 = f32[512,2048]{1,0:T(8,128)} reverse(f32[512,2048]{1,0:T(8,128)} %add.368), dimensions={0} | reverse | bytes 8388608 | tf_op jit(solution)/shard_map/rev | solution.py:53
  764.7 10.8 fusion.71
  775.5 24.6 %fusion.32 = f32[6144,2048]{1,0:T(8,128)} fusion(bf16[512,2048]{1,0:T(8,128)(2,1)} %get-tuple-element.20, bf16[512,2048]{1,0:T(8,128)(2,1)} %get-tuple-element.18, bf16[512,2048]{1,0:T(8,128)(2,1)} %get-tuple-element.22, bf16[512,2048]{1,0:T(8,128)(2,1)S(1)} %copy-done.4, f32[2048]{0:T(1024)S(1)} %copy-done.32, f32[2048]{0:T(1024)S(1)} %copy-done.20, ...), kind=kOutput, calls=%fused_computation.48 | convolution fusion | flops 12910067712 | bytes 58740736 | tf_op jit(solution)/shard_map/dot_general | solution.py:72
  800.2 346.6 %reduce-scatter.2.cloned.1.call-done = f32[1536,2048]{1,0:T(8,128)} async-done(((f32[6144,2048]{1,0:T(8,128)}), f32[1536,2048]{1,0:T(8,128)}) %reduce-scatter.2.cloned.1.call-update) | async-done | bytes 12582928 | tf_op jit(solution)/shard_map/reduce_scatter | solution.py:71
  1147.6 27.8 %fusion.16 = (f32[2048]{0:T(1024)S(1)}, f32[512]{0:T(512)S(1)}, f32[512]{0:T(512)S(1)}, f32[2048]{0:T(1024)S(1)}, f32[512,2048]{1,0:T(8,128)}) fusion(bf16[512,2048]{1,0:T(8,128)(2,1)S(1)} %copy-done.4, f32[512]{0:T(512)S(1)} %copy-done.28, f32[512]{0:T(512)S(1)} %copy-done.23, f32[2048]{0:T(1024)S(1)} %copy-done.20, f32[2048]{0:T(1024)S(1)} %bitcast.12, ...), kind=kOutput, calls=%fused_computation.25 | convolution fusion | flops 12922646528 | bytes 44081152 | tf_op jit(solution)/shard_map/dot_general | solution.py:65
  1175.4 43.3 %all-reduce.38 = (f32[2,2048]{1,0:T(2,128)}, f32[2048]{0:T(1024)}, f32[2048]{0:T(1024)}) all-reduce(f32[2,2048]{1,0:T(2,128)S(1)} %pad_maximum_fusion.19, f32[2048]{0:T(1024)S(1)} %get-tuple-element.8, f32[2048]{0:T(1024)S(1)} %get-tuple-element.11), channel_id=1, replica_groups=mesh['dp'=8,'tp'=4] {'dp','tp'}, use_global_device_ids=true, to_apply=%region_8.9 | all-reduce | flops 8192 | bytes 65536 | tf_op jit(solution)/shard_map/psum | solution.py:91
  1233.7 313.0 %all-reduce.41.cloned.1.call-done = f32[1536,2048]{1,0:T(8,128)} async-done(((f32[1536,2048]{1,0:T(8,128)}), f32[1536,2048]{1,0:T(8,128)}) %all-reduce.41.cloned.1.call-update) | async-done | bytes 12582928 | tf_op jit(solution)/shard_map/psum | solution.py:90
  1546.7 11.5 copy.17
  (285 shorter events, 278.2 us)
Async XLA Ops:
  7.2 179.4 %copy-start = (f32[4,2048]{1,0:T(4,128)S(1)}, f32[4,2048]{1,0:T(4,128)}, u32[]{:S(2)}) copy-start(f32[4,2048]{1,0:T(4,128)} %param.10) | copy-start | bytes 98308
  7.2 159.9 %copy-start.20 = (f32[2048]{0:T(1024)S(1)}, f32[2048]{0:T(1024)}, u32[]{:S(2)}) copy-start(f32[2048]{0:T(1024)} %param.11) | copy-start | bytes 24580
  7.2 159.9 %copy-start.30 = (f32[2048]{0:T(1024)S(1)}, f32[2048]{0:T(1024)}, u32[]{:S(2)}) copy-start(f32[2048]{0:T(1024)} %param.12) | copy-start | bytes 24580
  7.2 159.9 %all-gather.2.cloned.1.call-start = ((), (), s32[]{:S(2)}) async-start(), calls=%async_computation.1 | async-start | bytes 31457280 | tf_op jit(solution)/shard_map/all_gather | solution.py:27
  8.0 1138.8 %reduce-scatter.2.cloned.1.call-start = ((), (), s32[]{:S(2)}) async-start(), calls=%async_computation.2 | async-start | bytes 62914560 | tf_op jit(solution)/shard_map/reduce_scatter | solution.py:71
  8.8 177.8 %copy-start.34 = (pred[512]{0:T(512)(128)(4,1)}, pred[512]{0:T(512)(128)(4,1)S(1)}, u32[]{:S(2)}) copy-start(pred[512]{0:T(512)(128)(4,1)S(1)} %pad_add_fusion.2) | copy-start | bytes 1540
  9.2 177.4 %copy-start.22 = (f32[512]{0:T(512)}, f32[512]{0:T(512)S(1)}, u32[]{:S(2)}) copy-start(f32[512]{0:T(512)S(1)} %broadcast_multiply_fusion.2) | copy-start | bytes 6148
  9.9 176.7 %copy-start.26 = (f32[512]{0:T(512)}, f32[512]{0:T(512)S(1)}, u32[]{:S(2)}) copy-start(f32[512]{0:T(512)S(1)} %add_rsqrt_fusion) | copy-start | bytes 6148
  355.5 7.0 copy-start.19
  379.4 9.8 copy-start.15
  393.9 4.0 copy-start.6
  393.9 4.0 copy-start.8
  394.0 4.9 copy-start.11
  436.0 6.9 copy-start.2
  436.0 6.9 copy-start.3
  436.0 8.0 copy-start.13
  436.0 8.0 copy-start.21
  436.0 8.0 copy-start.23
  436.0 8.0 copy-start.27
  436.0 8.0 copy-start.31
  634.8 17.5 %copy-start.18 = (f32[15,2048]{1,0:T(8,128)S(1)}, f32[15,2048]{1,0:T(8,128)}, u32[]{:S(2)}) copy-start(f32[15,2048]{1,0:T(8,128)} %slice.569) | copy-start | bytes 368644
  668.8 9.8 copy-start.16
  683.4 4.1 copy-start.7
  683.4 4.1 copy-start.9
  683.4 4.9 copy-start.12
  732.0 32.6 %copy-start.35 = (pred[512]{0:T(512)(128)(4,1)S(1)}, pred[512]{0:T(512)(128)(4,1)}, u32[]{:S(2)}) copy-start(pred[512]{0:T(512)(128)(4,1)} %copy-done.34) | copy-start | bytes 1540
  764.7 10.8 copy-start.32
  800.1 746.5 %all-reduce.41.cloned.1.call-start = ((), (), s32[]{:S(2)}) async-start(), calls=%async_computation.3 | async-start | bytes 25165824 | tf_op jit(solution)/shard_map/psum | solution.py:90
  1147.6 71.2 %copy-start.25 = (s32[1,512]{1,0:T(1,128)S(1)}, s32[1,512]{1,0:T(1,128)}, u32[]{:S(2)}) copy-start(s32[1,512]{1,0:T(1,128)} %param.9) | copy-start | bytes 6148
  1218.8 6.6 copy-start.14
  1218.8 6.6 copy-start.17
  1546.7 11.6 copy-start.1
  (7 other events, 11.8 us)
Sparse Core Ops, SparseCore 0:
  9.6 157.4 all-gather.1
  800.3 346.4 reduce-scatter.1
  1150.9 395.7 all-reduce.40
where the time goes:
time: 1590 us; the launch traced here: 1570 us
  waiting for transfers between devices  817 us (51%)
  local copies, waits for them, and re-layouts  495 us (31%)
  other arithmetic  102 us (6%)
  matrix products  92.1 us (6%)
  blocking collectives  43.3 us (3%)
    reduce_scatter x1, waiting for transfers between devices, local(): lax.psum_scatter(lax.dot_general(columns, normed_low, contract_first, pre...  347 us
    psum x1, waiting for transfers between devices, local(): weight_grad = lax.psum(weight_part, 'dp')  313 us
    slice x59, local copies, waits for them, and re-layouts, local(): lax.associative_scan(link, (next_decay, direct), reverse=True, axis=0)  214 us
    all_gather x1, waiting for transfers between devices, local(): lax.all_gather(weight, 'tp', axis=0, tiled=True)  157 us
    slice x53, local copies, waits for them, and re-layouts, local(): unused, cells = lax.associative_scan(link, (decay, drive), axis=0)  117 us
    pad x16, local copies, waits for them, and re-layouts, local(): lax.associative_scan(link, (next_decay, direct), reverse=True, axis=0)  54.8 us
    pad x16, local copies, waits for them, and re-layouts, local(): unused, cells = lax.associative_scan(link, (decay, drive), axis=0)  54.5 us
    psum x1, blocking collectives, local(): lax.psum((bias_part, gain_part, shift_part), ('dp', 'tp'))  43.3 us
  transfers between devices with their start and end apart: 3, of which 3 were waited for; matrix products, arithmetic and copies ran while one was open for 3% of the time, Pallas kernels for 0%

commit v1 on v0

v1 whole, which is shorter than its diff:
```python
import functools

import jax
import jax.numpy as jnp
from jax import lax
from jax.experimental import pallas as pl
from jax.experimental.pallas import tpu as pltpu
from jax.sharding import PartitionSpec as P

BF = jnp.bfloat16
F32 = jnp.float32
SENT = 4
TP = 4
TILE = 256
SEG = 8
EPS = 1e-05
CHUNKS = 2
RING = 8

CORE, XSIDE, DIAG = 1, 2, 3
KIND_OF = ((0, 1, 2), (1, 0, 2), (2, 0, 1), (2, 1, 0))


def after(value, earlier):
    return lax.optimization_barrier((value, earlier))[0]


def swap(value, by):
    return lax.ppermute(value, "tp", [(t, t ^ by) for t in range(TP)])


def block_kernel(
    sc, x_ref, xcol_ref, og_ref, st_ref, gain_ref, bias_ref, gcol_ref, bcol_ref, gb_ref, w0_ref, w1_ref, w2_ref,
    n_ref, mean_ref, rstd_ref, out_ref, sg_ref, ex_ref, ends_ref, bsum_ref,
    s_sc, f_sc, d_sc, r_sc, dir_sc, prev_sc, a_sc, b_sc, row_sc,
):
    tok = x_ref.shape[0]
    seg = tok // SEG
    pad = seg + 1
    wide = x_ref.shape[1]

    @pl.when(pl.program_id(0) == 0)
    def _():
        def norm_rows(i, carry):
            rows = pl.ds(pl.multiple_of(i * 32, 32), 32)
            v = x_ref[rows, :].astype(F32)
            mean = jnp.sum(v, axis=1, keepdims=True) * (1.0 / wide)
            cen = v - mean
            rstd = lax.rsqrt(jnp.sum(cen * cen, axis=1, keepdims=True) * (1.0 / wide) + EPS)
            n_ref[rows, :] = (cen * rstd * gain_ref[...] + bias_ref[...]).astype(BF)
            mean_ref[rows, :] = jnp.broadcast_to(mean, (32, 128))
            rstd_ref[rows, :] = jnp.broadcast_to(rstd, (32, 128))
            return carry

        lax.fori_loop(0, tok // 32, norm_rows, 0)

    for kind, w_ref in enumerate((w0_ref, w1_ref, w2_ref)):
        s_sc[kind] = lax.dot_general(
            n_ref[...], w_ref[...], (((1,), (1,)), ((), ())), preferred_element_type=F32
        ).astype(BF)
    kc, kf, kr = sc[1], sc[2], sc[3]
    lanes = [(n, slice(128 * n, 128 * n + 128)) for n in range(TILE // 128)]

    def place(token):
        return pl.ds(token + token // seg, 1)

    def gates(i, carry):
        rows = pl.ds(pl.multiple_of(i * seg, seg), seg)
        at = pl.ds(i * pad, seg)
        for n, cols in lanes:
            cand = s_sc[kc, rows, cols].astype(F32)
            fg = jax.nn.sigmoid(s_sc[kf, rows, cols].astype(F32) + gb_ref[0:1, cols])
            rs = jax.nn.sigmoid(s_sc[kr, rows, cols].astype(F32) + gb_ref[1:2, cols])
            f_sc[n, at, :] = fg
            r_sc[n, rows, :] = rs
            d_sc[n, at, :] = (1.0 - fg) * cand
            dir_sc[n, at, :] = og_ref[rows, cols].astype(F32) * rs
        return carry

    lax.fori_loop(0, SEG, gates, 0)
    for s in range(SENT):
        at = place(sc[4 + s])
        for n, cols in lanes:
            fg = f_sc[n, at, :]
            row_sc[s : s + 1, cols] = fg
            d_sc[n, at, :] = d_sc[n, at, :] + fg * st_ref[s : s + 1, cols]
            f_sc[n, at, :] = jnp.zeros_like(fg)

    def at_step(i):
        return pl.ds(i, SEG, stride=pad)

    ones = jnp.ones((SEG, 128), F32)
    zeros = jnp.zeros((SEG, 128), F32)

    def scan_step(i, carries):
        new = []
        j = seg - 1 - i
        for (n, cols), (c, a, g, b, nd) in zip(lanes, carries):
            fw = f_sc[n, at_step(i), :]
            c = fw * c + d_sc[n, at_step(i), :]
            a = fw * a
            d_sc[n, at_step(i), :] = c
            a_sc[n, at_step(i), :] = a
            g = dir_sc[n, at_step(j), :] + nd * g
            b = nd * b
            dir_sc[n, at_step(j), :] = g
            b_sc[n, at_step(j), :] = b
            new.append((c, a, g, b, f_sc[n, at_step(j), :]))
        return tuple(new)

    begin = []
    for n, cols in lanes:
        first_decay = f_sc[n, at_step(0), :]
        begin.append((zeros, ones, zeros, ones, jnp.concatenate([first_decay[1:], zeros[:1]], axis=0)))
    into = []
    for c, a, g, b, _ in lax.fori_loop(0, seg, scan_step, tuple(begin), unroll=8):
        carry_f = [zeros[:1]]
        for s in range(SEG - 1):
            carry_f.append(a[s : s + 1] * carry_f[-1] + c[s : s + 1])
        carry_b = [zeros[:1]]
        for s in range(SEG - 1, 0, -1):
            carry_b.append(b[s : s + 1] * carry_b[-1] + g[s : s + 1])
        into.append((jnp.concatenate(carry_f, axis=0), jnp.concatenate(carry_b[::-1], axis=0)))

    def fix_step(i, before):
        new = []
        for (n, cols), (into_f, into_b), last in zip(lanes, into, before):
            cell = d_sc[n, at_step(i), :] + a_sc[n, at_step(i), :] * into_f
            d_sc[n, at_step(i), :] = cell
            prev_sc[n, at_step(i), :] = last
            dir_sc[n, at_step(i), :] = dir_sc[n, at_step(i), :] + b_sc[n, at_step(i), :] * into_b
            new.append(cell)
        return tuple(new)

    lax.fori_loop(0, seg, fix_step, tuple(v[0] for v in into), unroll=8)
    for s in range(SENT):
        at = place(sc[4 + s])
        for n, cols in lanes:
            fg = row_sc[s : s + 1, cols]
            f_sc[n, at, :] = fg
            prev_sc[n, at, :] = st_ref[s : s + 1, cols]
            ends_ref[s : s + 1, cols] = d_sc[n, place(sc[5 + s] - 1), :]
            ends_ref[SENT + s : SENT + s + 1, cols] = fg * dir_sc[n, at, :]

    def grads(i, carry):
        rows = pl.ds(pl.multiple_of(i * seg, seg), seg)
        at = pl.ds(i * pad, seg)
        new = []
        for (n, cols), (fsum, rsum) in zip(lanes, carry):
            sig = xcol_ref[rows, cols].astype(F32)
            outer = og_ref[rows, cols].astype(F32)
            normed = (sig - mean_ref[rows, :]) * rstd_ref[rows, :] * gcol_ref[:, cols] + bcol_ref[:, cols]
            cand = s_sc[kc, rows, cols].astype(F32)
            fg, rs, cell, cg = f_sc[n, at, :], r_sc[n, rows, :], d_sc[n, at, :], dir_sc[n, at, :]
            keep = 1.0 - rs
            out_ref[rows, cols] = (sig + rs * cell + keep * normed).astype(BF)
            pass_on = outer * keep
            ex_ref[rows, cols] = pass_on.astype(BF)
            rpg = pass_on * (cell - normed) * rs
            cng = cg * (1.0 - fg)
            fpg = cng * (prev_sc[n, at, :] - cand) * fg
            sg_ref[kc, rows, cols] = cng.astype(BF)
            sg_ref[kf, rows, cols] = fpg.astype(BF)
            sg_ref[kr, rows, cols] = rpg.astype(BF)
            fsum = fsum + jnp.sum(fpg.reshape(seg // 8, 8, 128), axis=0)
            rsum = rsum + jnp.sum(rpg.reshape(seg // 8, 8, 128), axis=0)
            new.append((fsum, rsum))
        return tuple(new)

    sums = lax.fori_loop(0, SEG, grads, ((zeros, zeros),) * len(lanes))
    for (n, cols), (fsum, rsum) in zip(lanes, sums):
        bsum_ref[0:1, cols] = jnp.sum(fsum, axis=0, keepdims=True)
        bsum_ref[1:2, cols] = jnp.sum(rsum, axis=0, keepdims=True)
        bsum_ref[2:8, cols] = jnp.zeros((6, 128), F32)


def run_block(scal, x, og, st, gain, bias, gate_bias, weight, w_core, w_x):
    tok, wide = x.shape
    own = wide // TP
    steps = own // TILE
    per = steps
    col = lambda k, sc: (0, sc[0] * per + k)
    tile = lambda k, sc: (0, k)
    whole = lambda k, sc: (0, 0)
    spec = pl.BlockSpec
    f32 = lambda *s: jax.ShapeDtypeStruct(s, F32)
    b16 = lambda *s: jax.ShapeDtypeStruct(s, BF)
    return pl.pallas_call(
        block_kernel,
        name="block",
        grid_spec=pltpu.PrefetchScalarGridSpec(
            num_scalar_prefetch=1,
            grid=(steps,),
            in_specs=[
                spec((tok, wide), whole),
                spec((tok, TILE), col),
                spec((tok, TILE), tile),
                spec((SENT, TILE), tile),
                spec((1, wide), whole),
                spec((1, wide), whole),
                spec((1, TILE), col),
                spec((1, TILE), col),
                spec((2, TILE), col),
                spec((TILE, wide), lambda k, sc: (sc[9] * per + k, 0)),
                spec((TILE, wide), lambda k, sc: (k, 0)),
                spec((TILE, wide), lambda k, sc: (k, 0)),
            ],
            out_specs=[
                spec((tok, wide), whole),
                spec((tok, 128), whole),
                spec((tok, 128), whole),
                spec((tok, TILE), tile),
                spec((3, tok, TILE), lambda k, sc: (0, 0, k)),
                spec((tok, TILE), tile),
                spec((8, TILE), tile),
                spec((8, TILE), tile),
            ],
            scratch_shapes=[pltpu.VMEM((3, tok, TILE), BF)] + [pltpu.VMEM((TILE // 128, tok + SEG, 128), F32)] * 7
            + [pltpu.VMEM((8, TILE), F32)],
        ),
        out_shape=[
            b16(tok, wide), f32(tok, 128), f32(tok, 128), b16(tok, own), b16(3, tok, own), b16(tok, own),
            f32(8, own), f32(8, own),
        ],
        cost_estimate=pl.CostEstimate(flops=18 * tok * wide * own, transcendentals=0, bytes_accessed=16 << 20),
    )(scal, x, x, og, st, gain, bias, gain, bias, gate_bias, weight, w_core, w_x)


def weight_kernel(*refs):
    sg, nl, out_ref = refs[:4], refs[4:8], refs[8]
    total = None
    for a, b in zip(sg, nl):
        part = lax.dot_general(a[0], b[...], (((0,), (0,)), ((), ())), preferred_element_type=F32)
        total = part if total is None else total + part
    out_ref[...] = total.astype(BF).reshape(out_ref.shape)


def run_weight(sgs, nls, chunk, shards):
    tok, own = sgs[0].shape[1:]
    wide = nls[0].shape[1]
    cols = wide // CHUNKS
    m = 256
    rows = own // shards
    return pl.pallas_call(
        weight_kernel,
        name="weight_grad",
        grid=(3, own // m),
        in_specs=[pl.BlockSpec((1, tok, m), lambda k, h: (k, 0, h))] * 4
        + [pl.BlockSpec((tok, cols), lambda k, h: (0, chunk))] * 4,
        out_specs=pl.BlockSpec((m // rows, 1, rows, cols), lambda k, h: (h, k, 0, 0)),
        out_shape=jax.ShapeDtypeStruct((shards, 3, rows, cols), BF),
        cost_estimate=pl.CostEstimate(flops=32 * tok * own * cols, transcendentals=0, bytes_accessed=16 << 20),
    )(*sgs, *nls)


def input_kernel(sc, sg_ref, w0_ref, w1_ref, w2_ref, ex_ref, x_ref, mean_ref, rstd_ref, p_ref, sum_ref):
    total = None
    for kind, w_ref in enumerate((w0_ref, w1_ref, w2_ref)):
        part = jnp.dot(sg_ref[kind], w_ref[...], preferred_element_type=F32)
        total = part if total is None else total + part
    mine = (pl.program_id(0) == sc[0]).astype(F32)
    total = total + ex_ref[...].astype(F32) * mine
    scaled = (x_ref[...].astype(F32) - mean_ref[:, 0:1]) * rstd_ref[:, 0:1]
    p_ref[...] = total.astype(BF)
    sum_ref[0:1, :] = jnp.sum(total * scaled, axis=0, keepdims=True)
    sum_ref[1:2, :] = jnp.sum(total, axis=0, keepdims=True)
    sum_ref[2:8, :] = jnp.zeros((6, total.shape[1]), F32)


def run_input(scal, sg, weight, w_core, w_x, ex, x, mean, rstd):
    tok, wide = x.shape
    own = wide // TP
    spec = pl.BlockSpec
    return pl.pallas_call(
        input_kernel,
        name="input_grad",
        grid_spec=pltpu.PrefetchScalarGridSpec(
            num_scalar_prefetch=1,
            grid=(TP,),
            in_specs=[
                spec((3, tok, own), lambda n, sc: (0, 0, 0)),
                spec((own, own), lambda n, sc: (sc[9], n)),
                spec((own, own), lambda n, sc: (0, n)),
                spec((own, own), lambda n, sc: (0, n)),
                spec((tok, own), lambda n, sc: (0, 0)),
                spec((tok, own), lambda n, sc: (0, n)),
                spec((tok, 128), lambda n, sc: (0, 0)),
                spec((tok, 128), lambda n, sc: (0, 0)),
            ],
            out_specs=[
                spec((tok, own), lambda n, sc: (0, n)),
                spec((8, own), lambda n, sc: (0, n)),
            ],
        ),
        out_shape=[jax.ShapeDtypeStruct((tok, wide), BF), jax.ShapeDtypeStruct((8, wide), F32)],
        cost_estimate=pl.CostEstimate(flops=8 * tok * own * wide, transcendentals=0, bytes_accessed=16 << 20),
    )(scal, sg, weight, w_core, w_x, ex, x, mean, rstd)


def add(*parts):
    total = parts[0].astype(F32)
    for part in parts[1:]:
        total = total + part.astype(F32)
    return total.astype(BF)


def pick(value, index):
    return lax.dynamic_index_in_dim(value, index, axis=0, keepdims=False)


def ring_device(p):
    return 2 * p if p < 4 else 2 * (7 - p) + 1


def ring_place(d):
    z, y = d // 2, d % 2
    return jnp.where(y == 0, z, 7 - z)


def around(value, step_of):
    pairs = []
    for p in range(RING):
        for t in range(TP):
            to = (p + step_of(t & 1)) % RING
            pairs.append((ring_device(p) * TP + t, ring_device(to) * TP + t))
    return lax.ppermute(value, ("dp", "tp"), pairs)


def gather_plane(part, p):
    ahead, behind = [part], [part]
    for k in range(4):
        ahead.append(around(ahead[-1], lambda core: 1))
        if k < 3:
            behind.append(around(behind[-1], lambda core: -1))
    by_offset = [part] + behind[1:] + ahead[:0:-1]
    return jnp.roll(jnp.stack(by_offset), p, axis=0)


def opposite(core):
    return 1 - 2 * core


def ring_sum(grad, shards, units):
    piece = pick(grad, shards[1])
    for k in range(RING - 1):
        piece = add(around(piece, opposite), pick(grad, shards[(2 + k) % RING]))
    pieces = [units(piece)]
    for k in range(RING - 1):
        pieces.append(around(pieces[-1], opposite))
    return pieces


def place_kernel(sc, *refs):
    pieces, out_ref = refs[:RING], refs[-1]
    for k in range(RING):

        @pl.when(pl.program_id(0) == k)
        def _(k=k):
            for kind in range(3):
                out_ref[sc[RING + kind], 0] = pieces[k][kind].astype(F32)


def place_pieces(where, pieces, chunk, before):
    _, rows, cols = pieces[0].shape
    shape = jax.ShapeDtypeStruct((3, RING, rows, cols * CHUNKS), F32)
    held = [] if before is None else [before]
    return pl.pallas_call(
        place_kernel,
        name="place",
        grid_spec=pltpu.PrefetchScalarGridSpec(
            num_scalar_prefetch=1,
            grid=(RING,),
            in_specs=[pl.BlockSpec((3, rows, cols), lambda k, sc: (0, 0, 0))] * RING
            + [pl.BlockSpec(memory_space=pl.ANY)] * len(held),
            out_specs=pl.BlockSpec((3, 1, rows, cols), lambda k, sc: (0, sc[k], 0, chunk)),
        ),
        out_shape=shape,
        input_output_aliases={1 + RING: 0} if held else {},
    )(where, *pieces, *held)


def sum_all(value, sizes):
    for axis in ("tp", "dp"):
        size = sizes[axis]
        if size & (size - 1):
            value = lax.psum(value, axis)
            continue
        bit = 1
        while bit < size:
            value = value + lax.ppermute(value, axis, [(i, i ^ bit) for i in range(size)])
            bit *= 2
    return value


def local(sizes, inputs, sentence_ids, start_states, ln_gain, ln_bias, weight, gate_bias, out_grad):
    tok, wide = inputs.shape
    own = wide // TP
    t = lax.axis_index("tp")
    d = lax.axis_index("dp")
    core = t & 1
    stay_at = 2 * core
    x_at = 2 - stay_at

    def columns(value, index):
        return lax.dynamic_slice_in_dim(value, index * own, own, axis=1)

    dp = sizes["dp"]
    ringed = dp == RING
    if ringed:
        p = ring_place(d)
        shards = (p - opposite(core) * jnp.arange(RING, dtype=jnp.int32)) % RING
        part = own // RING
        w_part = swap(lax.dynamic_slice_in_dim(weight, x_at * own + p * part, part, axis=0), XSIDE)
        w_x = gather_plane(w_part, p).reshape(own, wide)
    else:
        w_part = swap(lax.dynamic_slice_in_dim(weight, x_at * own, own, axis=0), XSIDE)
        w_x = w_part
    w_core = swap(weight[own : 2 * own], CORE)

    firsts = jnp.sum(sentence_ids[0][None, :] < jnp.arange(SENT, dtype=jnp.int32)[:, None], axis=1)
    small = jnp.concatenate(
        [start_states, jnp.zeros((SENT, wide), F32) + firsts.astype(F32)[:, None]], axis=0
    )
    smalls = [columns(small, t)] + [swap(columns(small, t ^ by), by) for by in (CORE, XSIDE, DIAG)]
    x_core = swap(inputs, CORE)
    x_side = swap(after(inputs, w_part), XSIDE)
    x_diag = swap(x_side, CORE)
    xs = [inputs, x_core, x_side, x_diag]
    ogs = [columns(out_grad, t), swap(columns(out_grad, t ^ CORE), CORE)]
    ogs += [swap(after(columns(out_grad, t ^ by), x_side), by) for by in (XSIDE, DIAG)]

    table = jnp.asarray(KIND_OF, jnp.int32)[t]
    scals = [
        jnp.concatenate(
            [
                t[None].astype(jnp.int32),
                table,
                part[SENT:, 0].astype(jnp.int32),
                jnp.full((1,), tok, jnp.int32),
                stay_at[None].astype(jnp.int32),
            ]
        )
        for part in smalls
    ]
    gain, bias = ln_gain[None], ln_bias[None]
    done = [
        run_block(scals[i], xs[i], ogs[i], smalls[i][:SENT], gain, bias, gate_bias, weight, w_core, w_x)
        for i in range(4)
    ]
    nls, means, rstds, outs, sgs, exs, ends, bsums = [list(v) for v in zip(*done)]

    def units(piece):
        return jnp.stack([piece[0], swap(piece[1], CORE), swap(piece[2], XSIDE)])

    if ringed:
        kinds = jnp.stack([stay_at, jnp.ones_like(core), x_at])
        where = jnp.concatenate([shards, kinds]).astype(jnp.int32)
        grads = [run_weight(sgs, nls, n, RING) for n in range(CHUNKS)]
        pieces = [ring_sum(grad, shards, units) for grad in grads]
        weight_grad = None
        for n in range(CHUNKS):
            weight_grad = place_pieces(where, pieces[n], n, weight_grad)
        weight_grad = weight_grad.reshape(3 * own, wide)
    else:
        chunks = []
        for n in range(CHUNKS):
            whole = lax.psum(run_weight(sgs, nls, n, RING).astype(F32), "dp").astype(BF)
            chunks.append(units(jnp.swapaxes(whole, 0, 1)).reshape(3, own, -1))
        rows = jnp.concatenate(chunks, axis=2).astype(F32)
        weight_grad = jnp.where(core == 0, rows, rows[::-1]).reshape(3 * own, wide)

    parts = [None] * 4
    norm_sum = None
    for i in (3, 2, 1, 0):
        parts[i], sums = run_input(
            scals[i], sgs[i], weight, w_core, w_x, exs[i], xs[i], means[i], rstds[i]
        )
        norm_sum = sums if norm_sum is None else norm_sum + sums
    to_x = add(parts[2], swap(parts[3], CORE))
    normed_grad = parts[0].astype(F32) + swap(parts[1], CORE).astype(F32) + swap(to_x, XSIDE).astype(F32)
    rstd = rstds[0][:, :1]
    scaled_in = (inputs.astype(F32) - means[0][:, :1]) * rstd
    scaled_grad = normed_grad * ln_gain
    input_grad = (
        rstd
        * (
            scaled_grad
            - jnp.mean(scaled_grad, axis=1, keepdims=True)
            - scaled_in * jnp.mean(scaled_grad * scaled_in, axis=1, keepdims=True)
        )
        + out_grad.astype(F32)
    )

    def collect(mine):
        whole = jnp.zeros((mine[0].shape[0], wide), mine[0].dtype)
        got = [mine[0]] + [swap(mine[by], by) for by in (CORE, XSIDE, DIAG)]
        for by in range(4):
            whole = lax.dynamic_update_slice_in_dim(whole, got[by], (t ^ by) * own, axis=1)
        return whole

    output = collect(outs)
    tails = collect(ends)
    bias_sum = bsums[0] + bsums[1] + bsums[2] + bsums[3]
    spread = lax.dynamic_update_slice_in_dim(jnp.zeros((2, wide), F32), bias_sum[:2], t * own, axis=1)
    sums = sum_all(jnp.concatenate([spread, norm_sum[:2]], axis=0), sizes)
    return (
        output, tails[:SENT], input_grad, weight_grad, sums[:2], sums[2], sums[3], tails[SENT:],
    )


def solution(mesh):
    rows = P(("dp", "tp"), None)
    sizes = dict(mesh.shape)
    return jax.shard_map(
        functools.partial(local, sizes),
        mesh=mesh,
        in_specs=(rows, rows, rows, P(), P(), P("tp", None), P(), rows),
        out_specs=(rows, rows, rows, P("tp", None), P(), P(), P(), rows),
        check_vma=False,
    )
```

time: 1590 us -> 422 us (0.27); the launches traced: 1570 us -> 420 us
  waiting for transfers between devices: 817 us -> 148 us
  local copies, waits for them, and re-layouts: 495 us -> 26 us
  Pallas kernels: 0 us -> 140 us
  matrix products: 92.1 us -> 0 us
  other arithmetic: 102 us -> 31.7 us
  starting transfers between devices: 0.12 us -> 57.8 us
  blocking collectives: 43.3 us -> 0 us
    reduce_scatter x1 -> x0, waiting for transfers between devices: 347 us -> none  [local(): lax.psum_scatter(lax.dot_general(columns, normed_low, contract_first, pre...]
    slice x114 -> x12, local copies, waits for them, and re-layouts: 334 us -> 10.5 us  [the longest x4 4.53 us: local(): smalls[i][:SENT]]
    psum x1 -> x0, waiting for transfers between devices: 313 us -> none  [local(): weight_grad = lax.psum(weight_part, 'dp')]
    all_gather x1 -> x0, waiting for transfers between devices: 157 us -> none  [local(): lax.all_gather(weight, 'tp', axis=0, tiled=True)]
    ppermute x0 -> x64, waiting for transfers between devices: none -> 148 us  [the longest x35 75.3 us: around(): return lax.ppermute(value, ('dp', 'tp'), pairs)]
    pallas_call x0 -> x12, Pallas kernels: none -> 140 us  [the longest x4 67.1 us: run_block(): pl.pallas_call(block_kernel, name='block', grid_spec=pltpu.PrefetchScalar...]
    pad x32 -> x0, local copies, waits for them, and re-layouts: 109 us -> none  [the longest x16 54.8 us: local(): lax.associative_scan(link, (next_decay, direct), reverse=True, axis=0)]
    dot_general x6 -> x0, matrix products: 92.1 us -> none  [the longest x1 27.8 us: local(): jnp.dot(columns, lax.all_gather(weight, 'tp', axis=0, tiled=True), prefer...]
  transfers between devices with their start and end apart: 3 -> 64, of which waited for: 3 -> 30; matrix products, arithmetic and copies ran while one was open for 3% -> 12% of each run, Pallas kernels for 0% -> 25%
where the time goes in v1:
time: 422 us; the launch traced here: 420 us
  waiting for transfers between devices  148 us (35%)
  Pallas kernels  140 us (33%)
  starting transfers between devices  57.8 us (14%)
  other arithmetic  31.7 us (8%)
  local copies, waits for them, and re-layouts  26 us (6%)
  between operations  16.7 us (4%)
    ppermute x35, waiting for transfers between devices, around(): return lax.ppermute(value, ('dp', 'tp'), pairs)  75.3 us
    pallas_call x4, Pallas kernels, run_block(): pl.pallas_call(block_kernel, name='block', grid_spec=pltpu.PrefetchScalar...  67.1 us
    ppermute x24, waiting for transfers between devices, swap(): return lax.ppermute(value, 'tp', [(t, t ^ by) for t in range(TP)])  65.8 us
    ppermute x35, starting transfers between devices, around(): return lax.ppermute(value, ('dp', 'tp'), pairs)  39.2 us
    pallas_call x4, Pallas kernels, run_input(): pl.pallas_call(input_kernel, name='input_grad', grid_spec=pltpu.PrefetchS...  37 us
    pallas_call x2, Pallas kernels, run_weight(): pl.pallas_call(weight_kernel, name='weight_grad', grid=(3, own // m), in_...  22.7 us
    convert_element_type x15, other arithmetic, add(): return total.astype(BF)  17.6 us
    ppermute x24, starting transfers between devices, swap(): return lax.ppermute(value, 'tp', [(t, t ^ by) for t in range(TP)])  13.9 us
  transfers between devices with their start and end apart: 64, of which 30 were waited for; matrix products, arithmetic and copies ran while one was open for 12% of the time, Pallas kernels for 25%

profile of v1, /device:TPU:0, one launch (start us, length us, event | category | flops | bytes accessed | tf_op | source)
XLA Modules:
  0.0 420.3 jit_solution(14756656516009782808)
XLA Ops:
  8.9 2.8 constant_dynamic-slice_fusion
  22.4 3.2 slice.106
  41.8 6.7 %collective-permute-done.5 = bf16[64,2048]{1,0:T(8,128)(2,1)S(1)} collective-permute-done((bf16[64,2048]{1,0:T(8,128)(2,1)S(1)}, bf16[64,2048]{1,0:T(8,128)(2,1)S(1)}, u32[]{:S(2)}, u32[]{:S(2)}) %collective-permute-start.5) | collective-permute-done | bytes 262176 | tf_op jit(solution)/shard_map/ppermute | solution.py:326
  50.5 5.8 %collective-permute-done.6 = bf16[64,2048]{1,0:T(8,128)(2,1)S(1)} collective-permute-done((bf16[64,2048]{1,0:T(8,128)(2,1)S(1)}, bf16[64,2048]{1,0:T(8,128)(2,1)S(1)}, u32[]{:S(2)}, u32[]{:S(2)}) %collective-permute-start.6) | collective-permute-done | bytes 262176 | tf_op jit(solution)/shard_map/ppermute | solution.py:326
  58.4 4.9 %collective-permute-done.7 = bf16[64,2048]{1,0:T(8,128)(2,1)S(1)} collective-permute-done((bf16[64,2048]{1,0:T(8,128)(2,1)S(1)}, bf16[64,2048]{1,0:T(8,128)(2,1)S(1)}, u32[]{:S(2)}, u32[]{:S(2)}) %collective-permute-start.7) | collective-permute-done | bytes 262176 | tf_op jit(solution)/shard_map/ppermute | solution.py:326
  66.2 4.8 %collective-permute-done.8 = bf16[64,2048]{1,0:T(8,128)(2,1)S(1)} collective-permute-done((bf16[64,2048]{1,0:T(8,128)(2,1)S(1)}, bf16[64,2048]{1,0:T(8,128)(2,1)S(1)}, u32[]{:S(2)}, u32[]{:S(2)}) %collective-permute-start.8) | collective-permute-done | bytes 262176 | tf_op jit(solution)/shard_map/ppermute | solution.py:326
  72.9 16.7 %block.4 = (bf16[512,2048]{1,0:T(8,128)(2,1)}, f32[512,128]{1,0:T(8,128)}, f32[512,128]{1,0:T(8,128)}, bf16[512,512]{1,0:T(8,128)(2,1)}, bf16[3,512,512]{2,1,0:T...) custom-call(s32[10]{0:T(128)} %concatenate.27.sc, bf16[512,2048]{1,0:T(8,128)(2,1)} %x_ref.3, ...), custom_call_target="tpu_custom_call" | custom-call | flops 9663676416 | bytes 16777216 | tf_op jit(solution)/shard_map/block/pallas_call | solution.py:188
  89.6 19.3 %collective-permute-done.14.x_ref.xcol_ref = bf16[512,2048]{1,0:T(8,128)(2,1)} collective-permute-done((bf16[512,2048]{1,0:T(8,128)(2,1)S(1)}, bf16[512,2048]{1,0:T(8,128)(2,1)}, u32[]{:S(2)}, u32[]{:S(2)}) %collective-permute-start.14) | collective-permute-done | bytes 2097184 | tf_op jit(solution)/shard_map/ppermute | solution.py:29
  108.9 16.6 %block.5 = (bf16[512,2048]{1,0:T(8,128)(2,1)}, f32[512,128]{1,0:T(8,128)}, f32[512,128]{1,0:T(8,128)}, bf16[512,512]{1,0:T(8,128)(2,1)}, bf16[3,512,512]{2,1,0:T...) custom-call(s32[10]{0:T(128)} %concatenate.29.sc, ...), custom_call_target="tpu_custom_call" | custom-call | flops 9663676416 | bytes 16777216 | tf_op jit(solution)/shard_map/block/pallas_call | solution.py:188
  125.7 9.2 %input_grad.5 = (bf16[512,2048]{1,0:T(8,128)(2,1)}, f32[8,2048]{1,0:T(8,128)}) custom-call(s32[10]{0:T(128)} %concatenate.29.sc, bf16[3,512,512]{2,1,0:T(8,128)(2,1)} %get-tuple-element.67.sg_ref.refs_1_, bf16[1536,2048]{1,0:T(8,128)(2,1)} %w0_ref.15, bf16[512,2048]{1,0:T(8,128)(2,1)} %collective-permute-done.w1_ref, bf16[512,2048]{1,0:T(8,128)(2,1)} %bitcast.105, ...), custom_call_target="tpu_custom_call" | custom-call | flops 4294967296 | bytes 16777216 | tf_op jit(solution)/shard_map/input_grad/pallas_call | solution.py:274
  134.9 9.2 %input_grad.4 = (bf16[512,2048]{1,0:T(8,128)(2,1)}, f32[8,2048]{1,0:T(8,128)}) custom-call(s32[10]{0:T(128)} %concatenate.27.sc, bf16[3,512,512]{2,1,0:T(8,128)(2,1)} %get-tuple-element.63.sg_ref.refs_0_, bf16[1536,2048]{1,0:T(8,128)(2,1)} %w0_ref.15, bf16[512,2048]{1,0:T(8,128)(2,1)} %collective-permute-done.w1_ref, bf16[512,2048]{1,0:T(8,128)(2,1)} %bitcast.106, ...), custom_call_target="tpu_custom_call" | custom-call | flops 4294967296 | bytes 16777216 | tf_op jit(solution)/shard_map/input_grad/pallas_call | solution.py:274
  146.4 16.8 %block.6 = (bf16[512,2048]{1,0:T(8,128)(2,1)}, f32[512,128]{1,0:T(8,128)}, f32[512,128]{1,0:T(8,128)}, bf16[512,512]{1,0:T(8,128)(2,1)}, bf16[3,512,512]{2,1,0:T...) custom-call(s32[10]{0:T(128)} %concatenate.30.sc, ...), custom_call_target="tpu_custom_call" | custom-call | flops 9663676416 | bytes 16777216 | tf_op jit(solution)/shard_map/block/pallas_call | solution.py:188
  164.0 17.0 %block.7 = (bf16[512,2048]{1,0:T(8,128)(2,1)}, f32[512,128]{1,0:T(8,128)}, f32[512,128]{1,0:T(8,128)}, bf16[512,512]{1,0:T(8,128)(2,1)}, bf16[3,512,512]{2,1,0:T...) custom-call(s32[10]{0:T(128)} %concatenate.31.sc, ...), custom_call_target="tpu_custom_call" | custom-call | flops 9663676416 | bytes 16777216 | tf_op jit(solution)/shard_map/block/pallas_call | solution.py:188
  181.0 11.3 %weight_grad.3 = bf16[8,3,64,1024]{3,2,1,0:T(8,128)(2,1)} custom-call(bf16[3,512,512]{2,1,0:T(8,128)(2,1)} %get-tuple-element.63.sg_ref.refs_0_, bf16[3,512,512]{2,1,0:T(8,128)(2,1)} %get-tuple-element.67.sg_ref.refs_1_, bf16[3,512,512]{2,1,0:T(8,128)(2,1)} %get-tuple-element.72.sg_ref.refs_2_, bf16[3,512,512]{2,1,0:T(8,128)(2,1)} %get-tuple-element.77.sg_ref.refs_3_, ...), custom_call_target="tpu_custom_call" | custom-call | flops 8589934592 | bytes 16777216 | tf_op jit(solution)/shard_map/weight_grad/pallas_call | solution.py:244
  195.2 11.3 %weight_grad.2 = bf16[8,3,64,1024]{3,2,1,0:T(8,128)(2,1)} custom-call(bf16[3,512,512]{2,1,0:T(8,128)(2,1)} %get-tuple-element.63.sg_ref.refs_0_, bf16[3,512,512]{2,1,0:T(8,128)(2,1)} %get-tuple-element.67.sg_ref.refs_1_, bf16[3,512,512]{2,1,0:T(8,128)(2,1)} %get-tuple-element.72.sg_ref.refs_2_, bf16[3,512,512]{2,1,0:T(8,128)(2,1)} %get-tuple-element.77.sg_ref.refs_3_, ...), custom_call_target="tpu_custom_call" | custom-call | flops 8589934592 | bytes 16777216 | tf_op jit(solution)/shard_map/weight_grad/pallas_call | solution.py:244
  212.6 9.5 %input_grad.6 = (bf16[512,2048]{1,0:T(8,128)(2,1)}, f32[8,2048]{1,0:T(8,128)}) custom-call(s32[10]{0:T(128)} %concatenate.30.sc, bf16[3,512,512]{2,1,0:T(8,128)(2,1)} %get-tuple-element.72.sg_ref.refs_2_, bf16[1536,2048]{1,0:T(8,128)(2,1)} %w0_ref.15, bf16[512,2048]{1,0:T(8,128)(2,1)} %collective-permute-done.w1_ref, bf16[512,2048]{1,0:T(8,128)(2,1)} %bitcast.109, ...), custom_call_target="tpu_custom_call" | custom-call | flops 4294967296 | bytes 16777216 | tf_op jit(solution)/shard_map/input_grad/pallas_call | solution.py:274
  227.2 9.1 %input_grad.7 = (bf16[512,2048]{1,0:T(8,128)(2,1)}, f32[8,2048]{1,0:T(8,128)}) custom-call(s32[10]{0:T(128)} %concatenate.31.sc, bf16[3,512,512]{2,1,0:T(8,128)(2,1)} %get-tuple-element.77.sg_ref.refs_3_, bf16[1536,2048]{1,0:T(8,128)(2,1)} %w0_ref.15, bf16[512,2048]{1,0:T(8,128)(2,1)} %collective-permute-done.w1_ref, bf16[512,2048]{1,0:T(8,128)(2,1)} %bitcast.110, ...), custom_call_target="tpu_custom_call" | custom-call | flops 4294967296 | bytes 16777216 | tf_op jit(solution)/shard_map/input_grad/pallas_call | solution.py:274
  240.7 4.6 %collective-permute-done.29 = bf16[3,64,1024]{2,1,0:T(8,128)(2,1)S(1)} collective-permute-done((bf16[3,64,1024]{2,1,0:T(8,128)(2,1)S(1)}, bf16[3,64,1024]{2,1,0:T(8,128)(2,1)S(1)}, u32[]{:S(2)}, u32[]{:S(2)}) %collective-permute-start.29) | collective-permute-done | bytes 393248 | tf_op jit(solution)/shard_map/ppermute | solution.py:326
  246.0 3.6 collective-permute-done.46
  254.4 4.1 collective-permute-done.47
  264.1 3.4 collective-permute-done.48
  280.1 4.4 %collective-permute-done.33 = bf16[3,64,1024]{2,1,0:T(8,128)(2,1)S(1)} collective-permute-done((bf16[3,64,1024]{2,1,0:T(8,128)(2,1)S(1)}, bf16[3,64,1024]{2,1,0:T(8,128)(2,1)S(1)}, u32[]{:S(2)}, u32[]{:S(2)}) %collective-permute-start.33) | collective-permute-done | bytes 393248 | tf_op jit(solution)/shard_map/ppermute | solution.py:326
  297.2 5.1 %collective-permute-done.52.refs_1_ = bf16[3,64,1024]{2,1,0:T(8,128)(2,1)S(1)} collective-permute-done((bf16[3,64,1024]{2,1,0:T(8,128)(2,1)S(1)}, bf16[3,64,1024]{2,1,0:T(8,128)(2,1)S(1)}, u32[]{:S(2)}, u32[]{:S(2)}) %collective-permute-start.52) | collective-permute-done | bytes 393248 | tf_op jit(solution)/shard_map/ppermute | solution.py:326
  303.9 2.6 collective-permute-done.36.refs_1_
  308.2 42.7 %collective-permute-done.16 = bf16[512,512]{1,0:T(8,128)(2,1)S(1)} collective-permute-done((bf16[512,512]{1,0:T(8,128)(2,1)S(1)}, bf16[512,512]{1,0:T(8,128)(2,1)S(1)}, u32[]{:S(2)}, u32[]{:S(2)}) %collective-permute-start.16) | collective-permute-done | bytes 524320 | tf_op jit(solution)/shard_map/ppermute | solution.py:29
  354.9 3.1 collective-permute-done.23
  359.5 3.3 collective-permute-done.63
  366.2 4.4 %collective-permute-done.54.refs_3_ = bf16[3,64,1024]{2,1,0:T(8,128)(2,1)S(1)} collective-permute-done((bf16[3,64,1024]{2,1,0:T(8,128)(2,1)S(1)}, bf16[3,64,1024]{2,1,0:T(8,128)(2,1)S(1)}, u32[]{:S(2)}, u32[]{:S(2)}) %collective-permute-start.54) | collective-permute-done | bytes 393248 | tf_op jit(solution)/shard_map/ppermute | solution.py:326
  380.7 2.6 collective-permute-done.39.refs_4_
  401.7 3.8 convert_add_fusion
  406.3 6.6 %place.2.refs_8_ = f32[3,8,64,2048]{3,2,1,0:T(8,128)} custom-call(s32[11]{0:T(128)} %pad_add_fusion.sc, bf16[3,64,1024]{2,1,0:T(8,128)(2,1)} %copy-done.7, bf16[3,64,1024]{2,1,0:T(8,128)(2,1)} %copy-done.10, bf16[3,64,1024]{2,1,0:T(8,128)(2,1)} %copy-done.11, bf16[3,64,1024]{2,1,0:T(8,128)(2,1)} %copy-done.12, bf16[3,64,1024]{2,1,0:T(8,128)(2,1)} %copy-done.13, ...), custom_call_target="tpu_custom_call" | custom-call | tf_op jit(solution)/shard_map/place/pallas_call | solution.py:367
  413.7 6.6 %place.3 = f32[3,8,64,2048]{3,2,1,0:T(8,128)} custom-call(s32[11]{0:T(128)} %pad_add_fusion.sc, bf16[3,64,1024]{2,1,0:T(8,128)(2,1)} %copy-done.8, bf16[3,64,1024]{2,1,0:T(8,128)(2,1)} %copy-done.17, bf16[3,64,1024]{2,1,0:T(8,128)(2,1)} %copy-done.18, bf16[3,64,1024]{2,1,0:T(8,128)(2,1)} %copy-done.19, ...), custom_call_target="tpu_custom_call", output_to_operand_aliasing={{}: (9, {})} | custom-call | tf_op jit(solution)/shard_map/place/pallas_call | solution.py:367
  (269 shorter events, 128.5 us)
Async XLA Ops:
  2.4 28.5 %collective-permute-start.17 = (f32[8,512]{1,0:T(8,128)S(1)}, f32[8,512]{1,0:T(8,128)}, u32[]{:S(2)}, u32[]{:S(2)}) collective-permute-start(f32[8,512]{1,0:T(8,128)S(1)} %get-tuple-element.108), channel_id=1, source_target_pairs={{0,3},{1,2},{2,1},{3,0},{4,7},{5,6},{6,5},{7,4},{8,11},{9,10},{10,... | collective-permute-start | bytes 49160 | tf_op jit(solution)/shard_map/ppermute | solution.py:29
  4.9 27.3 %collective-permute-start.13 = (f32[8,512]{1,0:T(8,128)S(1)}, f32[8,512]{1,0:T(8,128)}, u32[]{:S(2)}, u32[]{:S(2)}) collective-permute-start(f32[8,512]{1,0:T(8,128)S(1)} %get-tuple-element.109), channel_id=1, source_target_pairs={{0,2},{1,3},{2,0},{3,1},{4,6},{5,7},{6,4},{7,5},{8,10},{9,11},{10,... | collective-permute-start | bytes 49160 | tf_op jit(solution)/shard_map/ppermute | solution.py:29
  5.5 28.9 %collective-permute-start.9 = (f32[8,512]{1,0:T(8,128)S(1)}, f32[8,512]{1,0:T(8,128)}, u32[]{:S(2)}, u32[]{:S(2)}) collective-permute-start(f32[8,512]{1,0:T(8,128)S(1)} %get-tuple-element.110), channel_id=1, source_target_pairs={{0,1},{1,0},{2,3},{3,2},{4,5},{5,4},{6,7},{7,6},{8,9},{9,8},{10,11... | collective-permute-start | bytes 49160 | tf_op jit(solution)/shard_map/ppermute | solution.py:29
  7.2 32.6 %collective-permute-start.1 = (bf16[64,2048]{1,0:T(8,128)(2,1)}, bf16[64,2048]{1,0:T(8,128)(2,1)S(1)}, u32[]{:S(2)}, u32[]{:S(2)}) collective-permute-start(bf16[64,2048]{1,0:T(8,128)(2,1)} %constant_dynamic-slice_fusion.7), channel_id=1, source_target_pairs={{0,2},{1,3},{2,0},{3,1},{4,6},{5,7},{6,4},{7,5},{8,10},{9,11},{10,... | collective-permute-start | bytes 786440 | tf_op jit(solution)/shard_map/ppermute | solution.py:29
  11.7 97.2 %collective-permute-start.11 = (bf16[512,512]{1,0:T(8,128)(2,1)}, bf16[512,512]{1,0:T(8,128)(2,1)}, u32[]{:S(2)}, u32[]{:S(2)}) collective-permute-start(bf16[512,512]{1,0:T(8,128)(2,1)} %get-tuple-element.98), channel_id=1, source_target_pairs={{0,1},{1,0},{2,3},{3,2},{4,5},{5,4},{6,7},{7,6},{8,9},{9,8},{10,11... | collective-permute-start | bytes 1572872 | tf_op jit(solution)/shard_map/ppermute | solution.py:29
  30.9 42.0 %collective-permute-start = (bf16[512,2048]{1,0:T(8,128)(2,1)}, bf16[512,2048]{1,0:T(8,128)(2,1)}, u32[]{:S(2)}, u32[]{:S(2)}) collective-permute-start(bf16[512,2048]{1,0:T(8,128)(2,1)} %slice.106), channel_id=1, source_target_pairs={{0,1},{1,0},{2,3},{3,2},{4,5},{5,4},{6,7},{7,6},{8,9},{9,8},{10,11... | collective-permute-start | bytes 6291464 | tf_op jit(solution)/shard_map/ppermute | solution.py:29
  32.2 76.7 %collective-permute-start.10 = (bf16[512,2048]{1,0:T(8,128)(2,1)S(1)}, bf16[512,2048]{1,0:T(8,128)(2,1)}, u32[]{:S(2)}, u32[]{:S(2)}) collective-permute-start(bf16[512,2048]{1,0:T(8,128)(2,1)S(1)} %copy-done), channel_id=1, source_target_pairs={{0,1},{1,0},{2,3},{3,2},{4,5},{5,4},{6,7},{7,6},{8,9},{9,8},{10,11... | collective-permute-start | bytes 6291464 | tf_op jit(solution)/shard_map/ppermute | solution.py:29
  63.3 45.6 %collective-permute-start.14 = (bf16[512,2048]{1,0:T(8,128)(2,1)S(1)}, bf16[512,2048]{1,0:T(8,128)(2,1)}, u32[]{:S(2)}, u32[]{:S(2)}) collective-permute-start(bf16[512,2048]{1,0:T(8,128)(2,1)S(1)} %copy-done), channel_id=1, source_target_pairs={{0,2},{1,3},{2,0},{3,1},{4,6},{5,7},{6,4},{7,5},{8,10},{9,11},{10,... | collective-permute-start | bytes 6291464 | tf_op jit(solution)/shard_map/ppermute | solution.py:29
  108.9 54.3 %collective-permute-start.18 = (bf16[512,2048]{1,0:T(8,128)(2,1)}, bf16[512,2048]{1,0:T(8,128)(2,1)}, u32[]{:S(2)}, u32[]{:S(2)}) collective-permute-start(bf16[512,2048]{1,0:T(8,128)(2,1)} %collective-permute-done.14.x_ref.xcol_ref), channel_id=1, source_target_pairs={{0,1},{1,0},{2,3},{3,2},{4,5},{5,4},{6,7},{7,6},{8,9},{9,8},{10,11... | collective-permute-start | bytes 6291464 | tf_op jit(solution)/shard_map/ppermute | solution.py:29
  125.5 20.0 %collective-permute-start.15 = (bf16[512,512]{1,0:T(8,128)(2,1)S(1)}, bf16[512,512]{1,0:T(8,128)(2,1)S(1)}, u32[]{:S(2)}, u32[]{:S(2)}) collective-permute-start(bf16[512,512]{1,0:T(8,128)(2,1)S(1)} %get-tuple-element.54), channel_id=1, source_target_pairs={{0,2},{1,3},{2,0},{3,1},{4,6},{5,7},{6,4},{7,5},{8,10},{9,11},{10,... | collective-permute-start | bytes 1572872 | tf_op jit(solution)/shard_map/ppermute | solution.py:29
  144.1 19.1 %collective-permute-start.19 = (bf16[512,512]{1,0:T(8,128)(2,1)S(1)}, bf16[512,512]{1,0:T(8,128)(2,1)S(1)}, u32[]{:S(2)}, u32[]{:S(2)}) collective-permute-start(bf16[512,512]{1,0:T(8,128)(2,1)S(1)} %get-tuple-element.56), channel_id=1, source_target_pairs={{0,3},{1,2},{2,1},{3,0},{4,7},{5,6},{6,5},{7,4},{8,11},{9,10},{10,... | collective-permute-start | bytes 1572872 | tf_op jit(solution)/shard_map/ppermute | solution.py:29
  193.3 15.8 %collective-permute-start.43 = (bf16[3,64,1024]{2,1,0:T(8,128)(2,1)S(1)}, bf16[3,64,1024]{2,1,0:T(8,128)(2,1)S(1)}, u32[]{:S(2)}, u32[]{:S(2)}) collective-permute-start(bf16[3,64,1024]{2,1,0:T(8,128)(2,1)S(1)} %dynamic-slice_bitcast_fusion), channel_id=1, source_target_pairs={{0,8},{1,5},{2,10},{3,7},{8,16},{9,1},{10,18},{11,3},{16,24},{17,9... | collective-permute-start | bytes 1179656 | tf_op jit(solution)/shard_map/ppermute | solution.py:326
  207.5 14.6 %collective-permute-start.27 = (bf16[3,64,1024]{2,1,0:T(8,128)(2,1)S(1)}, bf16[3,64,1024]{2,1,0:T(8,128)(2,1)}, u32[]{:S(2)}, u32[]{:S(2)}) collective-permute-start(bf16[3,64,1024]{2,1,0:T(8,128)(2,1)S(1)} %dynamic-slice_bitcast_fusion.1), channel_id=1, source_target_pairs={{0,8},{1,5},{2,10},{3,7},{8,16},{9,1},{10,18},{11,3},{16,24},{17,9... | collective-permute-start | bytes 1179656 | tf_op jit(solution)/shard_map/ppermute | solution.py:326
  211.0 13.8 %collective-permute-start.44 = (bf16[3,64,1024]{2,1,0:T(8,128)(2,1)}, bf16[3,64,1024]{2,1,0:T(8,128)(2,1)}, u32[]{:S(2)}, u32[]{:S(2)}) collective-permute-start(bf16[3,64,1024]{2,1,0:T(8,128)(2,1)} %fusion.6), channel_id=1, source_target_pairs={{0,8},{1,5},{2,10},{3,7},{8,16},{9,1},{10,18},{11,3},{16,24},{17,9... | collective-permute-start | bytes 1179656 | tf_op jit(solution)/shard_map/ppermute | solution.py:326
  223.2 13.2 %collective-permute-start.28 = (bf16[3,64,1024]{2,1,0:T(8,128)(2,1)S(1)}, bf16[3,64,1024]{2,1,0:T(8,128)(2,1)}, u32[]{:S(2)}, u32[]{:S(2)}) collective-permute-start(bf16[3,64,1024]{2,1,0:T(8,128)(2,1)S(1)} %fusion.13), channel_id=1, source_target_pairs={{0,8},{1,5},{2,10},{3,7},{8,16},{9,1},{10,18},{11,3},{16,24},{17,9... | collective-permute-start | bytes 1179656 | tf_op jit(solution)/shard_map/ppermute | solution.py:326
  226.8 11.3 %collective-permute-start.45 = (bf16[3,64,1024]{2,1,0:T(8,128)(2,1)}, bf16[3,64,1024]{2,1,0:T(8,128)(2,1)}, u32[]{:S(2)}, u32[]{:S(2)}) collective-permute-start(bf16[3,64,1024]{2,1,0:T(8,128)(2,1)} %fusion.5), channel_id=1, source_target_pairs={{0,8},{1,5},{2,10},{3,7},{8,16},{9,1},{10,18},{11,3},{16,24},{17,9... | collective-permute-start | bytes 1179656 | tf_op jit(solution)/shard_map/ppermute | solution.py:326
  236.4 49.2 %collective-permute-start.25 = (bf16[512,2048]{1,0:T(8,128)(2,1)}, bf16[512,2048]{1,0:T(8,128)(2,1)}, u32[]{:S(2)}, u32[]{:S(2)}) collective-permute-start(bf16[512,2048]{1,0:T(8,128)(2,1)} %get-tuple-element.81), channel_id=1, source_target_pairs={{0,1},{1,0},{2,3},{3,2},{4,5},{5,4},{6,7},{7,6},{8,9},{9,8},{10,11... | collective-permute-start | bytes 6291464 | tf_op jit(solution)/shard_map/ppermute | solution.py:29
  239.3 10.3 %collective-permute-start.46 = (bf16[3,64,1024]{2,1,0:T(8,128)(2,1)S(1)}, bf16[3,64,1024]{2,1,0:T(8,128)(2,1)S(1)}, u32[]{:S(2)}, u32[]{:S(2)}) collective-permute-start(bf16[3,64,1024]{2,1,0:T(8,128)(2,1)S(1)} %fusion.4), channel_id=1, source_target_pairs={{0,8},{1,5},{2,10},{3,7},{8,16},{9,1},{10,18},{11,3},{16,24},{17,9... | collective-permute-start | bytes 1179656 | tf_op jit(solution)/shard_map/ppermute | solution.py:326
  260.2 9.7 %collective-permute-start.59 = (f32[4,2048]{1,0:T(4,128)S(1)}, f32[4,2048]{1,0:T(4,128)S(1)}, u32[]{:S(2)}, u32[]{:S(2)}) collective-permute-start(f32[4,2048]{1,0:T(4,128)S(1)} %pad_maximum_fusion.3), channel_id=1, source_target_pairs={{0,1},{1,0},{2,3},{3,2},{4,5},{5,4},{6,7},{7,6},{8,9},{9,8},{10,11... | collective-permute-start | bytes 98312 | tf_op jit(solution)/shard_map/ppermute | solution.py:390
  263.6 11.9 %collective-permute-start.32 = (bf16[3,64,1024]{2,1,0:T(8,128)(2,1)}, bf16[3,64,1024]{2,1,0:T(8,128)(2,1)}, u32[]{:S(2)}, u32[]{:S(2)}) collective-permute-start(bf16[3,64,1024]{2,1,0:T(8,128)(2,1)} %fusion.9), channel_id=1, source_target_pairs={{0,8},{1,5},{2,10},{3,7},{8,16},{9,1},{10,18},{11,3},{16,24},{17,9... | collective-permute-start | bytes 1179656 | tf_op jit(solution)/shard_map/ppermute | solution.py:326
  273.3 19.9 %collective-permute-start.12 = (bf16[512,512]{1,0:T(8,128)(2,1)}, bf16[512,512]{1,0:T(8,128)(2,1)S(1)}, u32[]{:S(2)}, u32[]{:S(2)}) collective-permute-start(bf16[512,512]{1,0:T(8,128)(2,1)} %get-tuple-element.52), channel_id=1, source_target_pairs={{0,1},{1,0},{2,3},{3,2},{4,5},{5,4},{6,7},{7,6},{8,9},{9,8},{10,11... | collective-permute-start | bytes 1572872 | tf_op jit(solution)/shard_map/ppermute | solution.py:29
  278.6 9.5 %collective-permute-start.51 = (bf16[64,1024]{1,0:T(8,128)(2,1)S(1)}, bf16[64,1024]{1,0:T(8,128)(2,1)S(1)}, u32[]{:S(2)}, u32[]{:S(2)}) collective-permute-start(bf16[64,1024]{1,0:T(8,128)(2,1)S(1)} %get-tuple-element.101), channel_id=1, source_target_pairs={{0,2},{1,3},{2,0},{3,1},{4,6},{5,7},{6,4},{7,5},{8,10},{9,11},{10,... | collective-permute-start | bytes 393224 | tf_op jit(solution)/shard_map/ppermute | solution.py:29
  288.7 96.2 %collective-permute-start.24 = (bf16[512,2048]{1,0:T(8,128)(2,1)S(1)}, bf16[512,2048]{1,0:T(8,128)(2,1)S(1)}, u32[]{:S(2)}, u32[]{:S(2)}) collective-permute-start(bf16[512,2048]{1,0:T(8,128)(2,1)S(1)} %copy-done.28), channel_id=1, source_target_pairs={{0,1},{1,0},{2,3},{3,2},{4,5},{5,4},{6,7},{7,6},{8,9},{9,8},{10,11... | collective-permute-start | bytes 6291464 | tf_op jit(solution)/shard_map/ppermute | solution.py:29
  292.3 92.5 %collective-permute-start.26 = (bf16[512,2048]{1,0:T(8,128)(2,1)S(1)}, bf16[512,2048]{1,0:T(8,128)(2,1)S(1)}, u32[]{:S(2)}, u32[]{:S(2)}) collective-permute-start(bf16[512,2048]{1,0:T(8,128)(2,1)S(1)} %add_convert_fusion), channel_id=1, source_target_pairs={{0,2},{1,3},{2,0},{3,1},{4,6},{5,7},{6,4},{7,5},{8,10},{9,11},{10,... | collective-permute-start | bytes 6291464 | tf_op jit(solution)/shard_map/ppermute | solution.py:29
  293.2 57.7 %collective-permute-start.16 = (bf16[512,512]{1,0:T(8,128)(2,1)S(1)}, bf16[512,512]{1,0:T(8,128)(2,1)S(1)}, u32[]{:S(2)}, u32[]{:S(2)}) collective-permute-start(bf16[512,512]{1,0:T(8,128)(2,1)S(1)} %copy-done.30), channel_id=1, source_target_pairs={{0,2},{1,3},{2,0},{3,1},{4,6},{5,7},{6,4},{7,5},{8,10},{9,11},{10,... | collective-permute-start | bytes 1572872 | tf_op jit(solution)/shard_map/ppermute | solution.py:29
  296.1 10.4 %collective-permute-start.36 = (bf16[3,64,1024]{2,1,0:T(8,128)(2,1)S(1)}, bf16[3,64,1024]{2,1,0:T(8,128)(2,1)S(1)}, u32[]{:S(2)}, u32[]{:S(2)}) collective-permute-start(bf16[3,64,1024]{2,1,0:T(8,128)(2,1)S(1)} %pad_maximum_fusion.refs_0_), channel_id=1, source_target_pairs={{0,8},{1,5},{2,10},{3,7},{8,16},{9,1},{10,18},{11,3},{16,24},{17,9... | collective-permute-start | bytes 1179656 | tf_op jit(solution)/shard_map/ppermute | solution.py:326
  302.3 60.5 %collective-permute-start.53 = (bf16[3,64,1024]{2,1,0:T(8,128)(2,1)S(1)}, bf16[3,64,1024]{2,1,0:T(8,128)(2,1)S(1)}, u32[]{:S(2)}, u32[]{:S(2)}) collective-permute-start(bf16[3,64,1024]{2,1,0:T(8,128)(2,1)S(1)} %collective-permute-done.52.refs_1_), channel_id=1, source_target_pairs={{0,8},{1,5},{2,10},{3,7},{8,16},{9,1},{10,18},{11,3},{16,24},{17,9... | collective-permute-start | bytes 1179656 | tf_op jit(solution)/shard_map/ppermute | solution.py:326
  306.5 57.9 %collective-permute-start.37 = (bf16[3,64,1024]{2,1,0:T(8,128)(2,1)S(1)}, bf16[3,64,1024]{2,1,0:T(8,128)(2,1)S(1)}, u32[]{:S(2)}, u32[]{:S(2)}) collective-permute-start(bf16[3,64,1024]{2,1,0:T(8,128)(2,1)S(1)} %collective-permute-done.36.refs_1_), channel_id=1, source_target_pairs={{0,8},{1,5},{2,10},{3,7},{8,16},{9,1},{10,18},{11,3},{16,24},{17,9... | collective-permute-start | bytes 1179656 | tf_op jit(solution)/shard_map/ppermute | solution.py:326
  362.8 14.3 %collective-permute-start.20 = (bf16[512,512]{1,0:T(8,128)(2,1)S(1)}, bf16[512,512]{1,0:T(8,128)(2,1)S(1)}, u32[]{:S(2)}, u32[]{:S(2)}) collective-permute-start(bf16[512,512]{1,0:T(8,128)(2,1)S(1)} %copy-done.29), channel_id=1, source_target_pairs={{0,3},{1,2},{2,1},{3,0},{4,7},{5,6},{6,5},{7,4},{8,11},{9,10},{10,... | collective-permute-start | bytes 1572872 | tf_op jit(solution)/shard_map/ppermute | solution.py:29
  364.5 10.4 %collective-permute-start.38 = (bf16[3,64,1024]{2,1,0:T(8,128)(2,1)S(1)}, bf16[3,64,1024]{2,1,0:T(8,128)(2,1)S(1)}, u32[]{:S(2)}, u32[]{:S(2)}) collective-permute-start(bf16[3,64,1024]{2,1,0:T(8,128)(2,1)S(1)} %collective-permute-done.37.refs_2_), channel_id=1, source_target_pairs={{0,8},{1,5},{2,10},{3,7},{8,16},{9,1},{10,18},{11,3},{16,24},{17,9... | collective-permute-start | bytes 1179656 | tf_op jit(solution)/shard_map/ppermute | solution.py:326
  395.9 9.6 %collective-permute-start.58 = (bf16[3,64,1024]{2,1,0:T(8,128)(2,1)S(1)}, bf16[3,64,1024]{2,1,0:T(8,128)(2,1)S(1)}, u32[]{:S(2)}, u32[]{:S(2)}) collective-permute-start(bf16[3,64,1024]{2,1,0:T(8,128)(2,1)S(1)} %collective-permute-done.57.refs_6_), channel_id=1, source_target_pairs={{0,8},{1,5},{2,10},{3,7},{8,16},{9,1},{10,18},{11,3},{16,24},{17,9... | collective-permute-start | bytes 1179656 | tf_op jit(solution)/shard_map/ppermute | solution.py:326
  400.1 12.8 %collective-permute-start.42 = (bf16[3,64,1024]{2,1,0:T(8,128)(2,1)S(1)}, bf16[3,64,1024]{2,1,0:T(8,128)(2,1)S(1)}, u32[]{:S(2)}, u32[]{:S(2)}) collective-permute-start(bf16[3,64,1024]{2,1,0:T(8,128)(2,1)S(1)} %collective-permute-done.41.refs_6_), channel_id=1, source_target_pairs={{0,8},{1,5},{2,10},{3,7},{8,16},{9,1},{10,18},{11,3},{16,24},{17,9... | collective-permute-start | bytes 1179656 | tf_op jit(solution)/shard_map/ppermute | solution.py:326
  (68 other events, 1291.4 us)

commit v2 on v1

v2 whole, which is shorter than its diff:
```python
import functools

import jax
import jax.numpy as jnp
from jax import lax
from jax.experimental import pallas as pl
from jax.experimental.pallas import tpu as pltpu
from jax.sharding import PartitionSpec as P

BF = jnp.bfloat16
F32 = jnp.float32
SENT = 4
TP = 4
TILE = 256
SEG = 8
FIELDS = 10
EPS = 1e-05
HALVES = 2
RING = 8
CHEAP = pl.CostEstimate(flops=1, transcendentals=0, bytes_accessed=1)

CORE, XSIDE, DIAG = 1, 2, 3
KIND_OF = ((0, 1, 2), (1, 0, 2), (2, 0, 1), (2, 1, 0))


def after(value, earlier):
    return lax.optimization_barrier((value, earlier))[0]


def swap(value, by):
    return lax.ppermute(value, "tp", [(t, t ^ by) for t in range(TP)])


def norm_kernel(x_ref, gain_ref, bias_ref, n_ref, mean_ref, rstd_ref):
    rows, wide = x_ref.shape

    def norm_rows(i, carry):
        at = pl.ds(pl.multiple_of(i * 32, 32), 32)
        v = x_ref[at, :].astype(F32)
        mean = jnp.sum(v, axis=1, keepdims=True) * (1.0 / wide)
        cen = v - mean
        rstd = lax.rsqrt(jnp.sum(cen * cen, axis=1, keepdims=True) * (1.0 / wide) + EPS)
        n_ref[at, :] = (cen * rstd * gain_ref[...] + bias_ref[...]).astype(BF)
        mean_ref[at, :] = jnp.broadcast_to(mean, (32, 128))
        rstd_ref[at, :] = jnp.broadcast_to(rstd, (32, 128))
        return carry

    lax.fori_loop(0, rows // 32, norm_rows, 0)


def run_norm(x, gain, bias):
    tok, wide = x.shape
    rows = 256
    spec = pl.BlockSpec
    return pl.pallas_call(
        norm_kernel,
        name="norm",
        grid=(tok // rows,),
        in_specs=[spec((rows, wide), lambda i: (i, 0))] + [spec((1, wide), lambda i: (0, 0))] * 2,
        out_specs=[spec((rows, wide), lambda i: (i, 0))] + [spec((rows, 128), lambda i: (i, 0))] * 2,
        out_shape=[jax.ShapeDtypeStruct((tok, wide), BF)] + [jax.ShapeDtypeStruct((tok, 128), F32)] * 2,
        cost_estimate=CHEAP,
    )(x, gain, bias)


def project(n_ref, w_ref):
    return lax.dot_general(
        n_ref[...], w_ref[...], (((1,), (1,)), ((), ())), preferred_element_type=F32
    ).astype(BF)


def early_kernel(sc, n0_ref, n1_ref, w0_ref, w1_ref, out_ref):
    for b, n_ref in enumerate((n0_ref, n1_ref)):
        for kind, w_ref in enumerate((w0_ref, w1_ref)):
            out_ref[b, kind] = project(n_ref, w_ref)


def run_early(scal, n0, n1, weight, w_core):
    tok, wide = n0.shape
    own = wide // TP
    tile = own // HALVES
    spec = pl.BlockSpec
    whole = spec((tok, wide), lambda h, sc: (0, 0))
    return pl.pallas_call(
        early_kernel,
        name="early",
        grid_spec=pltpu.PrefetchScalarGridSpec(
            num_scalar_prefetch=1,
            grid=(HALVES,),
            in_specs=[
                whole,
                whole,
                spec((tile, wide), lambda h, sc: (sc[9] * HALVES + h, 0)),
                spec((tile, wide), lambda h, sc: (h, 0)),
            ],
            out_specs=spec((2, 2, tok, tile), lambda h, sc: (0, 0, 0, h)),
        ),
        out_shape=jax.ShapeDtypeStruct((2, 2, tok, own), BF),
        cost_estimate=pl.CostEstimate(flops=8 * tok * own * wide, transcendentals=0, bytes_accessed=8 * tok * wide),
    )(scal, n0, n1, weight, w_core)


def project_kernel(sc, n_ref, w0_ref, w1_ref, w2_ref, out_ref):
    for kind, w_ref in enumerate((w0_ref, w1_ref, w2_ref)):
        out_ref[kind] = project(n_ref, w_ref)


def run_project(scal, n, weight, w_core, w_x):
    tok, wide = n.shape
    own = wide // TP
    tile = own // HALVES
    spec = pl.BlockSpec
    other = spec((tile, wide), lambda h, sc: (h, 0))
    return pl.pallas_call(
        project_kernel,
        name="project",
        grid_spec=pltpu.PrefetchScalarGridSpec(
            num_scalar_prefetch=1,
            grid=(HALVES,),
            in_specs=[
                spec((tok, wide), lambda h, sc: (0, 0)),
                spec((tile, wide), lambda h, sc: (sc[9] * HALVES + h, 0)),
                other,
                other,
            ],
            out_specs=spec((3, tok, tile), lambda h, sc: (0, 0, h)),
        ),
        out_shape=jax.ShapeDtypeStruct((3, tok, own), BF),
        cost_estimate=CHEAP,
    )(scal, n, weight, w_core, w_x)


def scan_block(
    sc, base, s_ref, n_ref, og_ref, st_ref, gb_ref, out_ref, sg_ref, ex_ref, ends_ref, bsum_ref, scratch
):
    f_sc, d_sc, r_sc, dir_sc, prev_sc, a_sc, b_sc, row_sc = scratch
    tok = n_ref.shape[0]
    seg = tok // SEG
    pad = seg + 1
    kc, kf, kr = sc[base + 1], sc[base + 2], sc[base + 3]
    lanes = [(n, slice(128 * n, 128 * n + 128)) for n in range(TILE // 128)]

    def place(token):
        return pl.ds(token + token // seg, 1)

    def gates(i, carry):
        rows = pl.ds(pl.multiple_of(i * seg, seg), seg)
        at = pl.ds(i * pad, seg)
        for n, cols in lanes:
            cand = s_ref[kc, rows, cols].astype(F32)
            fg = jax.nn.sigmoid(s_ref[kf, rows, cols].astype(F32) + gb_ref[0:1, cols])
            rs = jax.nn.sigmoid(s_ref[kr, rows, cols].astype(F32) + gb_ref[1:2, cols])
            f_sc[n, at, :] = fg
            r_sc[n, rows, :] = rs
            d_sc[n, at, :] = (1.0 - fg) * cand
            dir_sc[n, at, :] = og_ref[rows, cols].astype(F32) * rs
        return carry

    lax.fori_loop(0, SEG, gates, 0)
    for s in range(SENT):
        at = place(sc[base + 4 + s])
        for n, cols in lanes:
            fg = f_sc[n, at, :]
            row_sc[s : s + 1, cols] = fg
            d_sc[n, at, :] = d_sc[n, at, :] + fg * st_ref[s : s + 1, cols]
            f_sc[n, at, :] = jnp.zeros_like(fg)

    def at_step(i):
        return pl.ds(i, SEG, stride=pad)

    ones = jnp.ones((SEG, 128), F32)
    zeros = jnp.zeros((SEG, 128), F32)

    def scan_step(i, carries):
        new = []
        j = seg - 1 - i
        for (n, cols), (c, a, g, b, nd) in zip(lanes, carries):
            fw = f_sc[n, at_step(i), :]
            c = fw * c + d_sc[n, at_step(i), :]
            a = fw * a
            d_sc[n, at_step(i), :] = c
            a_sc[n, at_step(i), :] = a
            g = dir_sc[n, at_step(j), :] + nd * g
            b = nd * b
            dir_sc[n, at_step(j), :] = g
            b_sc[n, at_step(j), :] = b
            new.append((c, a, g, b, f_sc[n, at_step(j), :]))
        return tuple(new)

    begin = []
    for n, cols in lanes:
        first_decay = f_sc[n, at_step(0), :]
        begin.append((zeros, ones, zeros, ones, jnp.concatenate([first_decay[1:], zeros[:1]], axis=0)))
    into = []
    for c, a, g, b, _ in lax.fori_loop(0, seg, scan_step, tuple(begin), unroll=8):
        carry_f = [zeros[:1]]
        for s in range(SEG - 1):
            carry_f.append(a[s : s + 1] * carry_f[-1] + c[s : s + 1])
        carry_b = [zeros[:1]]
        for s in range(SEG - 1, 0, -1):
            carry_b.append(b[s : s + 1] * carry_b[-1] + g[s : s + 1])
        into.append((jnp.concatenate(carry_f, axis=0), jnp.concatenate(carry_b[::-1], axis=0)))

    def fix_step(i, before):
        new = []
        for (n, cols), (into_f, into_b), last in zip(lanes, into, before):
            cell = d_sc[n, at_step(i), :] + a_sc[n, at_step(i), :] * into_f
            d_sc[n, at_step(i), :] = cell
            prev_sc[n, at_step(i), :] = last
            dir_sc[n, at_step(i), :] = dir_sc[n, at_step(i), :] + b_sc[n, at_step(i), :] * into_b
            new.append(cell)
        return tuple(new)

    lax.fori_loop(0, seg, fix_step, tuple(v[0] for v in into), unroll=8)
    for s in range(SENT):
        at = place(sc[base + 4 + s])
        for n, cols in lanes:
            fg = row_sc[s : s + 1, cols]
            f_sc[n, at, :] = fg
            prev_sc[n, at, :] = st_ref[s : s + 1, cols]
            ends_ref[s : s + 1, cols] = d_sc[n, place(sc[base + 5 + s] - 1), :]
            ends_ref[SENT + s : SENT + s + 1, cols] = fg * dir_sc[n, at, :]

    def grads(i, carry):
        rows = pl.ds(pl.multiple_of(i * seg, seg), seg)
        at = pl.ds(i * pad, seg)
        new = []
        for (n, cols), (fsum, rsum) in zip(lanes, carry):
            normed = n_ref[rows, cols].astype(F32)
            outer = og_ref[rows, cols].astype(F32)
            cand = s_ref[kc, rows, cols].astype(F32)
            fg, rs, cell, cg = f_sc[n, at, :], r_sc[n, rows, :], d_sc[n, at, :], dir_sc[n, at, :]
            keep = 1.0 - rs
            out_ref[rows, cols] = (rs * cell + keep * normed).astype(BF)
            pass_on = outer * keep
            ex_ref[rows, cols] = pass_on.astype(BF)
            rpg = pass_on * (cell - normed) * rs
            cng = cg * (1.0 - fg)
            fpg = cng * (prev_sc[n, at, :] - cand) * fg
            sg_ref[kc, rows, cols] = cng.astype(BF)
            sg_ref[kf, rows, cols] = fpg.astype(BF)
            sg_ref[kr, rows, cols] = rpg.astype(BF)
            fsum = fsum + jnp.sum(fpg.reshape(seg // 8, 8, 128), axis=0)
            rsum = rsum + jnp.sum(rpg.reshape(seg // 8, 8, 128), axis=0)
            new.append((fsum, rsum))
        return tuple(new)

    sums = lax.fori_loop(0, SEG, grads, ((zeros, zeros),) * len(lanes))
    for (n, cols), (fsum, rsum) in zip(lanes, sums):
        bsum_ref[0:1, cols] = jnp.sum(fsum, axis=0, keepdims=True)
        bsum_ref[1:2, cols] = jnp.sum(rsum, axis=0, keepdims=True)
        bsum_ref[2:8, cols] = jnp.zeros((6, 128), F32)


def near_kernel(
    sc, e_ref, w_ref, n0_ref, n1_ref, c0_ref, c1_ref, og0_ref, og1_ref, st0_ref, st1_ref, gb_ref,
    out_ref, sg_ref, ex_ref, ends_ref, bsum_ref, s_sc, *scratch,
):
    blocks = ((n0_ref, c0_ref, og0_ref, st0_ref), (n1_ref, c1_ref, og1_ref, st1_ref))
    for b, (n_ref, c_ref, og_ref, st_ref) in enumerate(blocks):
        s_sc[0] = e_ref[b, 0]
        s_sc[1] = e_ref[b, 1]
        s_sc[2] = project(n_ref, w_ref)
        scan_block(
            sc, FIELDS * b, s_sc, c_ref, og_ref, st_ref, gb_ref,
            out_ref.at[b], sg_ref.at[b], ex_ref.at[b], ends_ref.at[b], bsum_ref.at[b], scratch,
        )


def far_kernel(
    sc, s0_ref, s1_ref, c0_ref, c1_ref, og0_ref, og1_ref, st0_ref, st1_ref, gb_ref,
    out_ref, sg_ref, ex_ref, ends_ref, bsum_ref, *scratch,
):
    blocks = ((s0_ref, c0_ref, og0_ref, st0_ref), (s1_ref, c1_ref, og1_ref, st1_ref))
    for b, (s_ref, c_ref, og_ref, st_ref) in enumerate(blocks):
        scan_block(
            sc, FIELDS * b, s_ref, c_ref, og_ref, st_ref, gb_ref,
            out_ref.at[b], sg_ref.at[b], ex_ref.at[b], ends_ref.at[b], bsum_ref.at[b], scratch,
        )


def scan_parts(tok, own, steps):
    tile = own // HALVES
    spec = pl.BlockSpec
    out = steps * tile
    f32 = lambda *s: jax.ShapeDtypeStruct(s, F32)
    b16 = lambda *s: jax.ShapeDtypeStruct(s, BF)
    three = lambda k, sc: (0, 0, k)
    return dict(
        specs=[
            spec((2, tok, tile), three),
            spec((2, 3, tok, tile), lambda k, sc: (0, 0, 0, k)),
            spec((2, tok, tile), three),
            spec((2, 8, tile), three),
            spec((2, 8, tile), three),
        ],
        shapes=[b16(2, tok, out), b16(2, 3, tok, out), b16(2, tok, out), f32(2, 8, out), f32(2, 8, out)],
        scratch=[pltpu.VMEM((tile // 128, tok + SEG, 128), F32)] * 7 + [pltpu.VMEM((8, tile), F32)],
    )


def run_near(scal, early, w_x, ns, ogs, sts, gate_bias):
    tok, wide = ns[0].shape
    own = wide // TP
    tile = own // HALVES
    spec = pl.BlockSpec
    parts = scan_parts(tok, own, HALVES)
    whole = spec((tok, wide), lambda k, sc: (0, 0))
    col = lambda k, sc: (0, sc[0] * HALVES + k)
    part = lambda k, sc: (0, k)
    return pl.pallas_call(
        near_kernel,
        name="near",
        grid_spec=pltpu.PrefetchScalarGridSpec(
            num_scalar_prefetch=1,
            grid=(HALVES,),
            in_specs=[
                spec((2, 2, tok, tile), lambda k, sc: (0, 0, 0, k)),
                spec((tile, wide), lambda k, sc: (k, 0)),
                whole,
                whole,
                spec((tok, tile), col),
                spec((tok, tile), col),
                spec((tok, tile), part),
                spec((tok, tile), part),
                spec((SENT, tile), part),
                spec((SENT, tile), part),
                spec((2, tile), col),
            ],
            out_specs=parts["specs"],
            scratch_shapes=[pltpu.VMEM((3, tok, tile), BF)] + parts["scratch"],
        ),
        out_shape=parts["shapes"],
        cost_estimate=CHEAP,
    )(scal, early, w_x, *ns, *ns, *ogs, *sts, gate_bias)


def run_far(scal, streams, ns, ogs, sts, gate_bias, half):
    tok, wide = ns[0].shape
    own = wide // TP
    tile = own // HALVES
    spec = pl.BlockSpec
    parts = scan_parts(tok, own, 1)
    col = lambda k, sc: (0, sc[0] * HALVES + half)
    part = lambda k, sc: (0, half)
    return pl.pallas_call(
        far_kernel,
        name="far",
        grid_spec=pltpu.PrefetchScalarGridSpec(
            num_scalar_prefetch=1,
            grid=(1,),
            in_specs=[
                spec((3, tok, tile), lambda k, sc: (0, 0, half)),
                spec((3, tok, tile), lambda k, sc: (0, 0, half)),
                spec((tok, tile), col),
                spec((tok, tile), col),
                spec((tok, tile), part),
                spec((tok, tile), part),
                spec((SENT, tile), part),
                spec((SENT, tile), part),
                spec((2, tile), col),
            ],
            out_specs=parts["specs"],
            scratch_shapes=parts["scratch"],
        ),
        out_shape=parts["shapes"],
        cost_estimate=CHEAP,
    )(scal, *streams, *ns, *ogs, *sts, gate_bias)


def weight_kernel(sc, near_ref, far_ref, n0_ref, n1_ref, n2_ref, n3_ref, out_ref):
    total = None
    sgs = (near_ref.at[0, 0], near_ref.at[1, 0], far_ref.at[0, 0], far_ref.at[1, 0])
    for sg, n_ref in zip(sgs, (n0_ref, n1_ref, n2_ref, n3_ref)):
        part = lax.dot_general(sg[...], n_ref[...], (((0,), (0,)), ((), ())), preferred_element_type=F32)
        total = part if total is None else total + part
    rows = out_ref.shape[2]
    for shard in range(RING):
        out_ref[sc[shard], 0] = total[shard * rows : (shard + 1) * rows].astype(BF)


def run_weight(slots, near, far, ns, half):
    tok, wide = ns[0].shape
    tile = wide // TP // HALVES
    rows = tile // RING
    cols = wide // 2
    spec = pl.BlockSpec
    return pl.pallas_call(
        weight_kernel,
        name="weight_grad",
        grid_spec=pltpu.PrefetchScalarGridSpec(
            num_scalar_prefetch=1,
            grid=(wide // cols, 3),
            in_specs=[
                spec((2, 1, tok, tile), lambda j, k, sc: (0, k, 0, half)),
                spec((2, 1, tok, tile), lambda j, k, sc: (0, k, 0, 0)),
            ]
            + [spec((tok, cols), lambda j, k, sc: (0, j))] * 4,
            out_specs=spec((RING, 1, rows, cols), lambda j, k, sc: (0, k, 0, j)),
        ),
        out_shape=jax.ShapeDtypeStruct((RING, 3, rows, wide), BF),
        cost_estimate=CHEAP,
    )(slots, near, far, *ns)


def input_near_kernel(sc, w0_ref, w1_ref, w2_ref, sg_ref, ex_ref, out_ref):
    mine = (pl.program_id(0) == sc[0]).astype(F32)
    for b in range(2):
        total = ex_ref[b].astype(F32) * mine
        for kind, w_ref in enumerate((w0_ref, w1_ref, w2_ref)):
            total = total + jnp.dot(sg_ref[b, kind], w_ref[...], preferred_element_type=F32)
        out_ref[b] = total.astype(BF)


def input_far_kernel(sc, w0_ref, w1_ref, w2_ref, sg0_ref, sg1_ref, ex0_ref, ex1_ref, out_ref):
    w_refs = (w0_ref, w1_ref, w2_ref)
    mine = (pl.program_id(0) == sc[0]).astype(F32)
    tile = sg0_ref.shape[3]
    for b in range(2):
        total = None
        for h, sg_ref in enumerate((sg0_ref, sg1_ref)):
            for kind in range(3):
                w = w_refs[kind][h * tile : (h + 1) * tile, :]
                part = jnp.dot(sg_ref[b, kind], w, preferred_element_type=F32)
                total = part if total is None else total + part
        for h, ex_ref in enumerate((ex0_ref, ex1_ref)):
            cols = slice(h * tile, (h + 1) * tile)
            out_ref[b, :, cols] = (total[:, cols] + ex_ref[b].astype(F32) * mine).astype(BF)


def run_input(scal, kernel, name, sgs, exs, weight, w_core, w_x):
    tok = exs[0].shape[1]
    wide = weight.shape[1]
    own = wide // TP
    part = own // len(sgs)
    spec = pl.BlockSpec
    return pl.pallas_call(
        kernel,
        name=name,
        grid_spec=pltpu.PrefetchScalarGridSpec(
            num_scalar_prefetch=1,
            grid=(TP,),
            in_specs=[
                spec((own, own), lambda n, sc: (sc[9], n)),
                spec((own, own), lambda n, sc: (0, n)),
                spec((own, own), lambda n, sc: (0, n)),
            ]
            + [spec((2, 3, tok, part), lambda n, sc: (0, 0, 0, 0))] * len(sgs)
            + [spec((2, tok, part), lambda n, sc: (0, 0, 0))] * len(exs),
            out_specs=spec((2, tok, own), lambda n, sc: (0, 0, n)),
        ),
        out_shape=jax.ShapeDtypeStruct((2, tok, wide), BF),
        cost_estimate=CHEAP,
    )(scal, weight, w_core, w_x, *sgs, *exs)


def back_kernel(
    home_ref, back_ref, side0_ref, side1_ref, side2_ref, x_ref, mean_ref, rstd_ref, gain_ref, og_ref, out_ref, sum_ref
):
    rows, wide = x_ref.shape
    per = 16
    step = pl.program_id(0)

    def some_rows(i, carry):
        gains, shifts = carry
        at = pl.ds(pl.multiple_of(i * per, per), per)
        side = jnp.where(step < 2, side0_ref[at, :], jnp.where(step < 3, side1_ref[at, :], side2_ref[at, :]))
        grad = home_ref[0, at, :].astype(F32) + back_ref[at, :].astype(F32) + side.astype(F32)
        rstd = rstd_ref[at, 0:1]
        scaled_in = (x_ref[at, :].astype(F32) - mean_ref[at, 0:1]) * rstd
        product = grad * scaled_in
        scaled = grad * gain_ref[...]
        mean_s = jnp.sum(scaled, axis=1, keepdims=True) * (1.0 / wide)
        mean_p = jnp.sum(scaled * scaled_in, axis=1, keepdims=True) * (1.0 / wide)
        out_ref[at, :] = rstd * (scaled - mean_s - scaled_in * mean_p) + og_ref[at, :].astype(F32)
        gains = gains + product[:8] + product[8:]
        shifts = shifts + grad[:8] + grad[8:]
        return gains, shifts

    blank = jnp.zeros((8, wide), F32)
    gains, shifts = lax.fori_loop(0, rows // per, some_rows, (blank, blank))

    @pl.when(pl.program_id(0) == 0)
    def _():
        sum_ref[...] = jnp.zeros_like(sum_ref)

    sum_ref[0:8, :] += gains
    sum_ref[8:16, :] += shifts


def run_back(home, back, sides, x, mean, rstd, gain, og):
    tok, wide = x.shape
    rows = tok // 4
    spec = pl.BlockSpec
    row = lambda i: (i, 0)
    return pl.pallas_call(
        back_kernel,
        name="norm_back",
        grid=(tok // rows,),
        in_specs=[
            spec((1, rows, wide), lambda i: (0, i, 0)),
            spec((rows, wide), row),
            spec((rows, wide), lambda i: (jnp.minimum(i, 1), 0)),
            spec((rows, wide), lambda i: (0, 0)),
            spec((rows, wide), lambda i: (0, 0)),
            spec((rows, wide), row),
            spec((rows, 128), row),
            spec((rows, 128), row),
            spec((1, wide), lambda i: (0, 0)),
            spec((rows, wide), row),
        ],
        out_specs=[spec((rows, wide), row), spec((16, wide), lambda i: (0, 0))],
        out_shape=[jax.ShapeDtypeStruct((tok, wide), F32), jax.ShapeDtypeStruct((16, wide), F32)],
        cost_estimate=CHEAP,
    )(home, back, *sides, x, mean, rstd, gain, og)


def output_kernel(sc, x_ref, own_ref, core_ref, side_ref, out_ref):
    by = pl.program_id(0) ^ sc[0]
    for other in range(TP):

        @pl.when(by == other)
        def _(other=other):
            if other == 0:
                part = own_ref[0]
            elif other == CORE:
                part = core_ref[0]
            else:
                part = side_ref[other - 2]
            out_ref[...] = (x_ref[...].astype(F32) + part.astype(F32)).astype(BF)


def run_output(scal, x, own_part, core_parts, side_parts):
    tok, wide = x.shape
    own = wide // TP
    spec = pl.BlockSpec
    return pl.pallas_call(
        output_kernel,
        name="output",
        grid_spec=pltpu.PrefetchScalarGridSpec(
            num_scalar_prefetch=1,
            grid=(TP,),
            in_specs=[
                spec((tok, own), lambda n, sc: (0, n)),
                spec((1, tok, own), lambda n, sc: (0, 0, 0)),
                spec((2, tok, own), lambda n, sc: (0, 0, 0)),
                spec((2, tok, own), lambda n, sc: (0, 0, 0)),
            ],
            out_specs=spec((tok, own), lambda n, sc: (0, n)),
        ),
        out_shape=jax.ShapeDtypeStruct((tok, wide), BF),
        cost_estimate=CHEAP,
    )(scal, x, own_part, core_parts, side_parts)


def add(*parts):
    total = parts[0].astype(F32)
    for part in parts[1:]:
        total = total + part.astype(F32)
    return total.astype(BF)


def ring_device(p):
    return 2 * p if p < 4 else 2 * (7 - p) + 1


def ring_place(d):
    z, y = d // 2, d % 2
    return jnp.where(y == 0, z, 7 - z)


def around(value, step_of):
    pairs = []
    for p in range(RING):
        for t in range(TP):
            to = (p + step_of(t & 1)) % RING
            pairs.append((ring_device(p) * TP + t, ring_device(to) * TP + t))
    return lax.ppermute(value, ("dp", "tp"), pairs)


def opposite(core):
    return 1 - 2 * core


class Ring:
    def __init__(self, grad):
        self.grad = grad
        self.piece = grad[1]
        self.count = 0
        self.pieces = []
        self.moving = around(self.piece, opposite)

    def step(self, gate):
        self.count += 1
        got = gate(self.moving)
        if self.count < RING:
            self.piece = add(got, self.grad[(1 + self.count) % RING])
            if self.count == RING - 1:
                self.units = [swap(self.piece[1], CORE), swap(self.piece[2], XSIDE)]
                self.moving = self.piece
                return
        elif self.count == RING:
            self.piece = jnp.stack([got[0], *self.units])
            self.pieces.append(self.piece)
        else:
            self.piece = got
            self.pieces.append(got)
        if len(self.pieces) < RING:
            self.moving = around(self.piece, opposite)


def place_kernel(sc, *refs):
    pieces, out_ref = refs[:RING], refs[-1]
    for k in range(RING):
        out_ref[0, sc[k]] = pieces[k][0].astype(F32)


def place_pieces(where, pieces, half, before):
    _, rows, wide = pieces[0].shape
    held = [] if before is None else [before]
    return pl.pallas_call(
        place_kernel,
        name="place",
        grid_spec=pltpu.PrefetchScalarGridSpec(
            num_scalar_prefetch=1,
            grid=(3,),
            in_specs=[pl.BlockSpec((1, rows, wide), lambda k, sc: (k, 0, 0))] * RING
            + [pl.BlockSpec(memory_space=pl.ANY)] * len(held),
            out_specs=pl.BlockSpec((1, RING, rows, wide), lambda k, sc: (sc[RING + k], half, 0, 0)),
        ),
        out_shape=jax.ShapeDtypeStruct((3, HALVES * RING, rows, wide), F32),
        input_output_aliases={1 + RING: 0} if held else {},
        cost_estimate=CHEAP,
    )(where, *pieces, *held)


def sum_all(value, sizes, axis):
    size = sizes[axis]
    if size & (size - 1):
        return lax.psum(value, axis)
    bit = 1
    while bit < size:
        value = value + lax.ppermute(value, axis, [(i, i ^ bit) for i in range(size)])
        bit *= 2
    return value


def in_order(core, side, own, other, far, further):
    near = jnp.where(core == 0, jnp.concatenate([own, other], -1), jnp.concatenate([other, own], -1))
    away = jnp.where(core == 0, jnp.concatenate([far, further], -1), jnp.concatenate([further, far], -1))
    return jnp.where(side == 0, jnp.concatenate([near, away], -1), jnp.concatenate([away, near], -1))


def local(sizes, inputs, sentence_ids, start_states, ln_gain, ln_bias, weight, gate_bias, out_grad):
    tok, wide = inputs.shape
    own = wide // TP
    tile = own // HALVES
    t = lax.axis_index("tp")
    d = lax.axis_index("dp")
    core, side = t & 1, t >> 1
    stay_at = 2 * core
    x_at = 2 - stay_at
    dp = sizes["dp"]
    ringed = dp == RING

    if ringed:
        z, y = d // 2, d % 2
        place = ring_place(d)
        shards = (place - opposite(core) * jnp.arange(RING, dtype=jnp.int32)) % RING
        quarter = own // 4
        k = 2 * y + z % 2
        over_y = [(i, i ^ 1) for i in range(dp)]
        over_z = [(i, i ^ 2) for i in range(dp)]
        w_send = lax.dynamic_slice_in_dim(weight, x_at * own + k * quarter, quarter, axis=0)
        w_part = swap(w_send, XSIDE)
        by_y = lax.ppermute(w_part, "dp", over_y)
        by_z = lax.ppermute(w_part, "dp", over_z)
    else:
        w_send = lax.dynamic_slice_in_dim(weight, x_at * own, own, axis=0)
        w_part = swap(w_send, XSIDE)
    w_pass = weight[own : 2 * own]
    w_core = swap(w_pass, CORE)

    def columns(value, index, start=0, width=own):
        return lax.dynamic_slice_in_dim(value, index * own + start, width, axis=1)

    firsts = jnp.sum(sentence_ids[0][None, :] < jnp.arange(SENT, dtype=jnp.int32)[:, None], axis=1)
    small = jnp.concatenate(
        [start_states, jnp.zeros((SENT, wide), F32) + firsts.astype(F32)[:, None]], axis=0
    )
    near_small = [small, swap(small, CORE)]
    far_small = [swap(small, XSIDE), swap(small, DIAG)]

    norm_own, mean, rstd = run_norm(after(inputs, (w_send, w_pass, small)), ln_gain[None], ln_bias[None])
    norm_core = swap(norm_own, CORE)
    norm_side = swap(after(norm_own, w_part), XSIDE)
    smalls = [columns(v, t) for v in (*near_small, *far_small)]
    out_later = after(out_grad, norm_own)
    og_own = columns(out_later, t)
    og_core = swap(columns(out_later, t ^ CORE), CORE)
    og_send = [columns(out_later, t ^ by) for by in (XSIDE, DIAG)]

    table = jnp.asarray(KIND_OF, jnp.int32)[t]
    scals = [
        jnp.concatenate(
            [
                t[None].astype(jnp.int32),
                table,
                part[SENT:, 0].astype(jnp.int32),
                jnp.full((1,), tok, jnp.int32),
                stay_at[None].astype(jnp.int32),
            ]
        )
        for part in smalls
    ]
    starts = [part[:SENT] for part in smalls]
    near_scal = jnp.concatenate(scals[:2])
    far_scal = jnp.concatenate(scals[2:])
    scal = jnp.concatenate([t[None].astype(jnp.int32), jnp.zeros((8,), jnp.int32), stay_at[None].astype(jnp.int32)])

    early = run_early(scal, norm_own, norm_core, weight, after(w_core, (og_own, *og_send, *starts)))
    if ringed:
        by_both = lax.ppermute(after(w_part, early), "dp", [(i, i ^ 3) for i in range(dp)])
        w_x = jnp.zeros((4, quarter, wide), BF)
        for i, part in ((k, w_part), (k ^ 1, by_z), (k ^ 2, by_y), (k ^ 3, by_both)):
            w_x = lax.dynamic_update_slice_in_dim(w_x, part[None], i, axis=0)
        w_x = w_x.reshape(own, wide)
    else:
        w_x = w_part
    near = run_near(
        near_scal, early, w_x, (norm_own, norm_core), (og_own, og_core), starts[:2], gate_bias
    )
    og_far = [swap(after(og_send[i], early), by) for i, by in ((0, XSIDE), (1, DIAG))]
    near_in = run_input(scal, input_near_kernel, "input_near", near[1:2], near[2:3], weight, w_core, w_x)
    near_back = swap(near_in[1], CORE)
    norm_side = after(norm_side, near_in)
    norm_diag = swap(norm_side, CORE)
    ns = [norm_own, norm_core, norm_side, norm_diag]
    far_streams = [run_project(scal, norm_side, weight, w_core, w_x)]
    far_streams.append(run_project(scal, after(norm_diag, far_streams[0]), weight, w_core, w_x))
    if ringed:
        slots = (jnp.arange(RING, dtype=jnp.int32) - place) * -opposite(core) % RING
    else:
        slots = jnp.arange(RING, dtype=jnp.int32)

    def far_part(h, gate):
        return run_far(far_scal, gate(far_streams), ns[2:], og_far, starts[2:], gate_bias, h)

    def far_weight(h, gate):
        return run_weight(slots, near[1], gate(far[h][1]), ns, h)

    def joined(far, i, which):
        return jnp.concatenate([v[i][which] for v in far], axis=-1)

    def send_ends(sums, near_end, far_end):
        return jnp.concatenate([sums, jnp.concatenate([near_end, far_end], axis=1).reshape(4, wide)], axis=0)

    last = [None]

    def gate(value):
        return value if last[0] is None else lax.optimization_barrier((value, last[0]))[0]

    def mark(value):
        last[0] = value

    work = {}

    def far_in():
        sgs, exs = [[v[i] for v in far] for i in (1, 2)]
        work["far_in"] = run_input(scal, input_far_kernel, "input_far", sgs, gate(exs), weight, w_core, w_x)
        work["far_back"] = swap(work["far_in"][1], CORE)
        work["sides"] = []
        mark(work["far_in"])

    def to_x(start, count):
        def task():
            rows = slice(start * tok // 4, (start + count) * tok // 4)
            sent = gate(add(work["far_in"][0, rows], work["far_back"][rows]))
            work["sides"].append(swap(sent, XSIDE))
            mark(sent)

        return task

    def arrive(i):
        def task():
            work["sides"][i] = gate(work["sides"][i])
            mark(work["sides"][i])

        return task

    def outs_arrive():
        work["side_outs"] = gate(work["side_outs"])
        mark(work["side_outs"])

    def out_core():
        sent = jnp.stack([gate(near[0])[1], joined(far, 0, 1)])
        work["core_outs"] = swap(sent, CORE)
        mark(sent)

    def out_side():
        sent = jnp.stack([joined(far, 0, 0), gate(work["core_outs"])[1]])
        work["side_outs"] = swap(sent, XSIDE)
        mark(sent)

    def norm_back():
        work["input_grad"], work["norm_sums"] = run_back(
            near_in, near_back, gate(work["sides"]), inputs, mean, rstd, ln_gain[None], out_grad
        )
        mark(work["norm_sums"])

    def output():
        work["output"] = run_output(scal, inputs, near[0], work["core_outs"], gate(work["side_outs"]))
        mark(work["output"])

    def sums_core():
        bias_sum = near[4][0] + near[4][1] + joined(far, 4, 0) + joined(far, 4, 1)
        spread = lax.dynamic_update_slice_in_dim(jnp.zeros((2, wide), F32), bias_sum[:2], t * own, axis=1)
        norm_sums = gate(work["norm_sums"]).reshape(2, 8, wide).sum(axis=1)
        work["sums"] = jnp.concatenate([spread, norm_sums], axis=0)
        sent = send_ends(work["sums"], near[3][1], joined(far, 3, 1))
        work["got"] = swap(sent, CORE)
        mark(sent)

    def sums_side():
        got = gate(work["got"])
        work["core_ends"] = got[4:].reshape(8, 2 * own)
        work["sums"] = work["sums"] + got[:4]
        sent = send_ends(work["sums"], joined(far, 3, 0), work["core_ends"][:, own:])
        work["got"] = swap(sent, XSIDE)
        mark(sent)

    def sums_ends():
        got = gate(work["got"])
        side_ends = got[4:].reshape(8, 2 * own)
        core_ends = work["core_ends"]
        work["tails"] = in_order(core, side, near[3][0], core_ends[:, :own], side_ends[:, :own], side_ends[:, own:])
        work["sums"] = work["sums"] + got[:4]
        if ringed:
            send_sums(1)
        else:
            work["sums"] = sum_all(work["sums"], sizes, "dp")

    def send_sums(bit):
        work["moving"] = lax.ppermute(work["sums"], "dp", [(i, i ^ bit) for i in range(dp)])
        mark(work["sums"])

    def sums_dp(bit):
        def task():
            work["sums"] = work["sums"] + gate(work["moving"])
            if bit < dp:
                send_sums(bit)

        return task

    def units(piece):
        return jnp.stack([piece[0], swap(piece[1], CORE), swap(piece[2], XSIDE)])

    far = []
    if ringed:
        kinds = jnp.stack([stay_at, jnp.ones_like(core), x_at])
        where = jnp.concatenate([shards, kinds]).astype(jnp.int32)
        fill = {
            1: [out_core, far_in],
            2: [to_x(0, 2)],
            5: [arrive(0)],
            6: [to_x(2, 1)],
            7: [arrive(1)],
            8: [to_x(3, 1), out_side],
            10: [arrive(2), norm_back],
            11: [outs_arrive, sums_core],
            12: [sums_side],
            13: [output, sums_ends],
            14: [sums_dp(2)],
            15: [sums_dp(4)],
        }
        far.append(far_part(0, gate))
        grad = far_weight(0, gate)
        rings = [Ring(grad)]
        mark(rings[0].piece)
        far.append(far_part(1, gate))
        mark(far[1][1])
        rings[0].step(gate)
        mark(rings[0].piece)
        grad = far_weight(1, gate)
        mark(grad)
        rings[0].step(gate)
        mark(rings[0].piece)
        rings.append(Ring(gate(grad)))
        mark(rings[1].piece)
        weight_grad = None
        for n in range(1, 16):
            for task in fill.get(n, ()):
                task()
            for i, ring in enumerate(rings):
                if len(ring.pieces) < RING:
                    ring.step(gate)
                    mark(ring.piece)
                    if len(ring.pieces) == RING:
                        weight_grad = place_pieces(where, ring.pieces, i, weight_grad)
        sums_dp(8)()
        weight_grad = weight_grad.reshape(3 * own, wide)
    else:
        rows = []
        for h in range(HALVES):
            far.append(far_part(h, gate))
            grad = far_weight(h, gate)
            whole = lax.psum(grad.astype(F32), "dp").astype(BF)
            rows.append(units(jnp.swapaxes(whole, 0, 1)).reshape(3, tile, wide))
        rows = jnp.concatenate(rows, axis=1).astype(F32)
        weight_grad = jnp.where(core == 0, rows, rows[::-1]).reshape(3 * own, wide)
        for task in (
            far_in, to_x(0, 2), to_x(2, 1), to_x(3, 1), out_core, out_side, norm_back, sums_core, sums_side, output,
            sums_ends,
        ):
            task()
    sums, tails = work["sums"], work["tails"]
    return (
        work["output"], tails[:SENT], work["input_grad"], weight_grad, sums[:2], sums[2], sums[3], tails[SENT:],
    )


def solution(mesh):
    rows = P(("dp", "tp"), None)
    sizes = dict(mesh.shape)
    return jax.shard_map(
        functools.partial(local, sizes),
        mesh=mesh,
        in_specs=(rows, rows, rows, P(), P(), P("tp", None), P(), rows),
        out_specs=(rows, rows, rows, P("tp", None), P(), P(), P(), rows),
        check_vma=False,
    )
```

time: 422 us -> 358 us (0.85)
  waiting for transfers between devices: 148 us -> 108 us
  between operations: 16.7 us -> 1.39 us
  other arithmetic: 31.7 us -> 18.1 us
    ppermute x24, waiting for transfers between devices: 65.8 us -> 38.1 us  [swap(): return lax.ppermute(value, 'tp', [(t, t ^ by) for t in range(TP)])]
    ppermute x35 -> x28, waiting for transfers between devices: 75.3 us -> 57.1 us  [around(): return lax.ppermute(value, ('dp', 'tp'), pairs)]
    squeeze x2 -> x10, local copies, waits for them, and re-layouts: 2.04 us -> 10.6 us  [the longest x1 3.31 us: far_in(): work['far_back'] = swap(work['far_in'][1], CORE)]
    convert_element_type x15 -> x16, other arithmetic: 17.6 us -> 10.1 us  [add(): return total.astype(BF)]
    add x7 -> x5, other arithmetic: 6.22 us -> 0.08 us  [the longest x3 0.04 us: task(): work['sums'] = work['sums'] + gate(work['moving'])]
    ppermute x5 -> x6, waiting for transfers between devices: 7.04 us -> 12.8 us  [the longest x1 11.9 us: local(): by_y = lax.ppermute(w_part, 'dp', over_y)]
    ppermute x24, starting transfers between devices: 13.9 us -> 18.2 us  [swap(): return lax.ppermute(value, 'tp', [(t, t ^ by) for t in range(TP)])]
    slice x9 -> x11, local copies, waits for them, and re-layouts: 8.63 us -> 5.66 us  [the longest x1 3.17 us: local(): w_pass = weight[own:2 * own]]
  transfers between devices with their start and end apart: 64 -> 58, of which waited for: 30 -> 28; matrix products, arithmetic and copies ran while one was open for 12% -> 8% of each run, Pallas kernels for 25% -> 29%
where the time goes in v2:
time: 358 us; the launch traced here: 357 us
  Pallas kernels  139 us (39%)
  waiting for transfers between devices  108 us (30%)
  starting transfers between devices  61.5 us (17%)
  local copies, waits for them, and re-layouts  28.7 us (8%)
  other arithmetic  18.1 us (5%)
    ppermute x28, waiting for transfers between devices, around(): return lax.ppermute(value, ('dp', 'tp'), pairs)  57.1 us
    ppermute x24, waiting for transfers between devices, swap(): return lax.ppermute(value, 'tp', [(t, t ^ by) for t in range(TP)])  38.1 us
    ppermute x28, starting transfers between devices, around(): return lax.ppermute(value, ('dp', 'tp'), pairs)  36.4 us
    pallas_call x2, Pallas kernels, run_weight(): pl.pallas_call(weight_kernel, name='weight_grad', grid_spec=pltpu.Prefetc...  27 us
    pallas_call x2, Pallas kernels, run_input(): pl.pallas_call(kernel, name=name, grid_spec=pltpu.PrefetchScalarGridSpec(...  23.6 us
    ppermute x24, starting transfers between devices, swap(): return lax.ppermute(value, 'tp', [(t, t ^ by) for t in range(TP)])  18.2 us
    pallas_call x1, Pallas kernels, run_near(): pl.pallas_call(near_kernel, name='near', grid_spec=pltpu.PrefetchScalarGr...  16.7 us
    pallas_call x2, Pallas kernels, run_project(): pl.pallas_call(project_kernel, name='project', grid_spec=pltpu.PrefetchSc...  16.4 us
  transfers between devices with their start and end apart: 58, of which 28 were waited for; matrix products, arithmetic and copies ran while one was open for 8% of the time, Pallas kernels for 29%

profile of v2, /device:TPU:0, one launch (start us, length us, event | category | flops | bytes accessed | tf_op | source)
XLA Modules:
  0.0 357.0 jit_solution(16323212059572447587)
XLA Ops:
  0.7 3.2 slice.216
  5.7 6.1 %norm.1 = (bf16[512,2048]{1,0:T(8,128)(2,1)}, f32[512,128]{1,0:T(8,128)}, f32[512,128]{1,0:T(8,128)}) custom-call(bf16[512,2048]{1,0:T(8,128)(2,1)} %x_ref.4, f32[1,2048]{1,0:T(1,128)} %bitcast.157, f32[1,2048]{1,0:T(1,128)} %bitcast.159), custom_call_target="tpu_custom_call" | custom-call | flops 1 | bytes 1 | tf_op jit(solution)/shard_map/norm/pallas_call | solution.py:55
  22.6 6.9 %collective-permute-done.4 = f32[8,2048]{1,0:T(8,128)S(1)} collective-permute-done((f32[8,2048]{1,0:T(8,128)S(1)}, f32[8,2048]{1,0:T(8,128)S(1)}, u32[]{:S(2)}, u32[]{:S(2)}) %collective-permute-start.4) | collective-permute-done | bytes 65568 | tf_op jit(solution)/shard_map/ppermute | solution.py:31
  35.5 9.3 %early.1.e_ref = bf16[2,2,512,512]{3,2,1,0:T(8,128)(2,1)} custom-call(s32[10]{0:T(128)} %pad_add_fusion.sc, bf16[512,2048]{1,0:T(8,128)(2,1)} %get-tuple-element.99.n0_ref.c0_ref, bf16[512,2048]{1,0:T(8,128)(2,1)} %collective-permute-done.1.n1_ref.c1_ref, bf16[1536,2048]{1,0:T(8,128)(2,1)} %w0_ref.9, bf16[512,2048]{1,0:T(8,128)(2,1)} %collective-permute-done.2.w1_ref), custom_call_target="tpu_custom_call" | custom-call | flops 4294967296 | bytes 8388608 | tf_op jit(solution)/shard_map/early/pallas_call | solution.py:84
  46.0 11.9 %collective-permute-done.7 = bf16[128,2048]{1,0:T(8,128)(2,1)} collective-permute-done((bf16[128,2048]{1,0:T(8,128)(2,1)S(1)}, bf16[128,2048]{1,0:T(8,128)(2,1)}, u32[]{:S(2)}, u32[]{:S(2)}) %collective-permute-start.7) | collective-permute-done | bytes 524320 | tf_op jit(solution)/shard_map/ppermute | solution.py:676
  60.5 16.7 %near.1 = (bf16[2,512,512]{2,1,0:T(8,128)(2,1)}, bf16[2,3,512,512]{3,2,1,0:T(8,128)(2,1)}, bf16[2,512,512]{2,1,0:T(8,128)(2,1)}, f32[2,8,512]{2,1,0:T(8,128)}, f32[2,8,512]{2,1,0:T(8,128)}) custom-call(s32[20]{0:T(128)} %concatenate.61.sc, bf16[2,2,512,512]{3,2,1,0:T(8,128)(2,1)} %early.1.e_ref, bf16[512,2048]{1,0:T(8,128)(2,1)} %bitcast.147, ...), custom_call_target="tpu_custom_call" | custom-call | flops 1 | bytes 1 | tf_op jit(solution)/shard_map/near/pallas_call | solution.py:311
  77.3 11.8 %input_near.1.home_ref = bf16[2,512,2048]{2,1,0:T(8,128)(2,1)} custom-call(s32[10]{0:T(128)} %pad_add_fusion.sc, bf16[1536,2048]{1,0:T(8,128)(2,1)} %w0_ref.9, bf16[512,2048]{1,0:T(8,128)(2,1)} %collective-permute-done.2.w1_ref, bf16[512,2048]{1,0:T(8,128)(2,1)} %bitcast.148, bf16[2,3,512,512]{3,2,1,0:T(8,128)(2,1)} %get-tuple-element.98.sg_ref.near_ref, ...), custom_call_target="tpu_custom_call" | custom-call | flops 1 | bytes 1 | tf_op jit(solution)/shard_map/input_near/pallas_call | solution.py:437
  92.4 8.2 %project.2.s0_ref = bf16[3,512,512]{2,1,0:T(8,128)(2,1)} custom-call(s32[10]{0:T(128)} %pad_add_fusion.sc, bf16[512,2048]{1,0:T(8,128)(2,1)} %collective-permute-done.10.n_ref.c0_ref.n2_ref, bf16[1536,2048]{1,0:T(8,128)(2,1)} %w0_ref.9, bf16[512,2048]{1,0:T(8,128)(2,1)} %collective-permute-done.2.w1_ref, bf16[512,2048]{1,0:T(8,128)(2,1)} %bitcast.149), custom_call_target="tpu_custom_call" | custom-call | flops 1 | bytes 1 | tf_op jit(solution)/shard_map/project/pallas_call | solution.py:114
  102.0 8.2 %project.3.s1_ref = bf16[3,512,512]{2,1,0:T(8,128)(2,1)} custom-call(s32[10]{0:T(128)} %pad_add_fusion.sc, bf16[512,2048]{1,0:T(8,128)(2,1)} %copy-done.1, bf16[1536,2048]{1,0:T(8,128)(2,1)} %w0_ref.9, bf16[512,2048]{1,0:T(8,128)(2,1)} %collective-permute-done.2.w1_ref, bf16[512,2048]{1,0:T(8,128)(2,1)} %bitcast.150), custom_call_target="tpu_custom_call" | custom-call | flops 1 | bytes 1 | tf_op jit(solution)/shard_map/project/pallas_call | solution.py:114
  110.2 4.2 %collective-permute-done.13.og1_ref = bf16[512,512]{1,0:T(8,128)(2,1)S(1)} collective-permute-done((bf16[512,512]{1,0:T(8,128)(2,1)}, bf16[512,512]{1,0:T(8,128)(2,1)S(1)}, u32[]{:S(2)}, u32[]{:S(2)}) %collective-permute-start.13) | collective-permute-done | bytes 524320 | tf_op jit(solution)/shard_map/ppermute | solution.py:31
  115.1 6.7 %far.2 = (bf16[2,512,256]{2,1,0:T(8,128)(2,1)}, bf16[2,3,512,256]{3,2,1,0:T(8,128)(2,1)}, bf16[2,512,256]{2,1,0:T(8,128)(2,1)}, f32[2,8,256]{2,1,0:T(8,128)}, f32[2,8,256]{2,1,0:T(8,128)}) custom-call(s32[20]{0:T(128)} %concatenate.62.sc, bf16[3,512,512]{2,1,0:T(8,128)(2,1)} %project.2.s0_ref, bf16[3,512,512]{2,1,0:T(8,128)(2,1)} %project.3.s1_ref, ...), custom_call_target="tpu_custom_call" | custom-call | flops 1 | bytes 1 | tf_op jit(solution)/shard_map/far/pallas_call | solution.py:346
  121.8 13.5 %weight_grad.2 = bf16[8,3,32,2048]{3,2,1,0:T(8,128)(2,1)} custom-call(s32[8]{0:T(128)} %and_select_fusion.1.sc, bf16[2,3,512,512]{3,2,1,0:T(8,128)(2,1)} %get-tuple-element.98.sg_ref.near_ref, bf16[2,3,512,256]{3,2,1,0:T(8,128)(2,1)} %get-tuple-element.105.far_ref.sg0_ref, bf16[512,2048]{1,0:T(8,128)(2,1)} %get-tuple-element.99.n0_ref.c0_ref, ...), custom_call_target="tpu_custom_call" | custom-call | flops 1 | bytes 1 | tf_op jit(solution)/shard_map/weight_grad/pallas_call | solution.py:388
  137.2 6.6 %far.3 = (bf16[2,512,256]{2,1,0:T(8,128)(2,1)}, bf16[2,3,512,256]{3,2,1,0:T(8,128)(2,1)}, bf16[2,512,256]{2,1,0:T(8,128)(2,1)}, f32[2,8,256]{2,1,0:T(8,128)}, f32[2,8,256]{2,1,0:T(8,128)}) custom-call(s32[20]{0:T(128)} %concatenate.62.sc, bf16[3,512,512]{2,1,0:T(8,128)(2,1)} %project.2.s0_ref, bf16[3,512,512]{2,1,0:T(8,128)(2,1)} %project.3.s1_ref, ...), custom_call_target="tpu_custom_call" | custom-call | flops 1 | bytes 1 | tf_op jit(solution)/shard_map/far/pallas_call | solution.py:346
  149.4 13.5 %weight_grad.3 = bf16[8,3,32,2048]{3,2,1,0:T(8,128)(2,1)} custom-call(s32[8]{0:T(128)} %and_select_fusion.1.sc, bf16[2,3,512,512]{3,2,1,0:T(8,128)(2,1)} %get-tuple-element.98.sg_ref.near_ref, bf16[2,3,512,256]{3,2,1,0:T(8,128)(2,1)} %get-tuple-element.110.far_ref.sg1_ref, bf16[512,2048]{1,0:T(8,128)(2,1)} %get-tuple-element.99.n0_ref.c0_ref, ...), custom_call_target="tpu_custom_call" | custom-call | flops 1 | bytes 1 | tf_op jit(solution)/shard_map/weight_grad/pallas_call | solution.py:388
  167.8 11.7 %input_far.1 = bf16[2,512,2048]{2,1,0:T(8,128)(2,1)} custom-call(s32[10]{0:T(128)} %pad_add_fusion.sc, bf16[1536,2048]{1,0:T(8,128)(2,1)} %w0_ref.9, bf16[512,2048]{1,0:T(8,128)(2,1)} %collective-permute-done.2.w1_ref, bf16[512,2048]{1,0:T(8,128)(2,1)} %bitcast.151, bf16[2,3,512,256]{3,2,1,0:T(8,128)(2,1)} %get-tuple-element.105.far_ref.sg0_ref, ...), custom_call_target="tpu_custom_call" | custom-call | flops 1 | bytes 1 | tf_op jit(solution)/shard_map/input_far/pallas_call | solution.py:437
  179.5 3.3 slice_bitcast_fusion.1
  186.3 4.9 %collective-permute-done.19 = bf16[3,32,2048]{2,1,0:T(8,128)(2,1)} collective-permute-done((bf16[3,32,2048]{2,1,0:T(8,128)(2,1)}, bf16[3,32,2048]{2,1,0:T(8,128)(2,1)}, u32[]{:S(2)}, u32[]{:S(2)}) %collective-permute-start.19) | collective-permute-done | bytes 393248 | tf_op jit(solution)/shard_map/ppermute | solution.py:578
  205.5 3.2 collective-permute-done.23
  209.8 3.2 collective-permute-done.22
  214.0 3.2 collective-permute-done.25
  218.2 3.2 collective-permute-done.24
  225.7 4.1 %collective-permute-done.26 = bf16[3,32,2048]{2,1,0:T(8,128)(2,1)S(1)} collective-permute-done((bf16[3,32,2048]{2,1,0:T(8,128)(2,1)S(1)}, bf16[3,32,2048]{2,1,0:T(8,128)(2,1)S(1)}, u32[]{:S(2)}, u32[]{:S(2)}) %collective-permute-start.26) | collective-permute-done | bytes 393248 | tf_op jit(solution)/shard_map/ppermute | solution.py:578
  241.0 7.4 %collective-permute-done.34.side1_ref = bf16[128,2048]{1,0:T(8,128)(2,1)S(1)} collective-permute-done((bf16[128,2048]{1,0:T(8,128)(2,1)S(1)}, bf16[128,2048]{1,0:T(8,128)(2,1)S(1)}, u32[]{:S(2)}, u32[]{:S(2)}) %collective-permute-start.34) | collective-permute-done | bytes 524320 | tf_op jit(solution)/shard_map/ppermute | solution.py:31
  252.8 3.4 collective-permute-done.36.refs_2_
  270.8 18.5 %collective-permute-done.44.side2_ref = bf16[128,2048]{1,0:T(8,128)(2,1)S(1)} collective-permute-done((bf16[128,2048]{1,0:T(8,128)(2,1)}, bf16[128,2048]{1,0:T(8,128)(2,1)S(1)}, u32[]{:S(2)}, u32[]{:S(2)}) %collective-permute-start.44) | collective-permute-done | bytes 524320 | tf_op jit(solution)/shard_map/ppermute | solution.py:31
  290.0 10.3 %norm_back.1 = (f32[512,2048]{1,0:T(8,128)}, f32[16,2048]{1,0:T(8,128)}) custom-call(bf16[2,512,2048]{2,1,0:T(8,128)(2,1)} %input_near.1.home_ref, bf16[512,2048]{1,0:T(8,128)(2,1)} %collective-permute-done.43.back_ref, bf16[256,2048]{1,0:T(8,128)(2,1)} %copy-done.13, bf16[128,2048]{1,0:T(8,128)(2,1)} %copy-done.15, bf16[128,2048]{1,0:T(8,128)(2,1)} %copy-done.16, ...), custom_call_target="tpu_custom_call" | custom-call | flops 1 | bytes 1 | tf_op jit(solution)/shard_map/norm_back/pallas_call | solution.py:496
  305.0 3.4 collective-permute-done.46.refs_5_
  317.4 3.7 %collective-permute-done.47.refs_4_ = bf16[3,32,2048]{2,1,0:T(8,128)(2,1)S(1)} collective-permute-done((bf16[3,32,2048]{2,1,0:T(8,128)(2,1)S(1)}, bf16[3,32,2048]{2,1,0:T(8,128)(2,1)S(1)}, u32[]{:S(2)}, u32[]{:S(2)}) %collective-permute-start.47) | collective-permute-done | bytes 393248 | tf_op jit(solution)/shard_map/ppermute | solution.py:578
  323.8 5.5 %output.1 = bf16[512,2048]{1,0:T(8,128)(2,1)} custom-call(s32[10]{0:T(128)} %pad_add_fusion.sc, bf16[512,2048]{1,0:T(8,128)(2,1)} %x_ref.4, bf16[2,512,512]{2,1,0:T(8,128)(2,1)} %get-tuple-element.113.own_ref, bf16[2,512,512]{2,1,0:T(8,128)(2,1)} %copy-done.7, bf16[2,512,512]{2,1,0:T(8,128)(2,1)} %copy-done.14), custom_call_target="tpu_custom_call" | custom-call | flops 1 | bytes 1 | tf_op jit(solution)/shard_map/output/pallas_call | solution.py:537
  335.9 5.6 %collective-permute-done.53.refs_6_ = bf16[3,32,2048]{2,1,0:T(8,128)(2,1)S(1)} collective-permute-done((bf16[3,32,2048]{2,1,0:T(8,128)(2,1)}, bf16[3,32,2048]{2,1,0:T(8,128)(2,1)S(1)}, u32[]{:S(2)}, u32[]{:S(2)}) %collective-permute-start.53) | collective-permute-done | bytes 393248 | tf_op jit(solution)/shard_map/ppermute | solution.py:578
  344.5 5.6 %place.2.refs_8_ = f32[3,16,32,2048]{3,2,1,0:T(8,128)} custom-call(s32[11]{0:T(128)} %pad_add_fusion.1.sc, bf16[3,32,2048]{2,1,0:T(8,128)(2,1)} %copy-done.10, bf16[3,32,2048]{2,1,0:T(8,128)(2,1)} %copy-done.18, bf16[3,32,2048]{2,1,0:T(8,128)(2,1)} %copy-done.19, bf16[3,32,2048]{2,1,0:T(8,128)(2,1)} %collective-permute-done.40.refs_3_, ...), custom_call_target="tpu_custom_call" | custom-call | flops 1 | bytes 1 | tf_op jit(solution)/shard_map/place/pallas_call | solution.py:621
  351.4 5.6 %place.3 = f32[3,16,32,2048]{3,2,1,0:T(8,128)} custom-call(s32[11]{0:T(128)} %pad_add_fusion.1.sc, bf16[3,32,2048]{2,1,0:T(8,128)(2,1)} %copy-done.11, bf16[3,32,2048]{2,1,0:T(8,128)(2,1)} %collective-permute-done.39.refs_1_, bf16[3,32,2048]{2,1,0:T(8,128)(2,1)} %collective-permute-done.41.refs_2_, ...), custom_call_target="tpu_custom_call", output_to_operand_aliasing={{}: (9, {})} | custom-call | flops 1 | bytes 1 | tf_op jit(solution)/shard_map/place/pallas_call | solution.py:621
  (260 shorter events, 123.3 us)
Async XLA Ops:
  3.8 30.1 %collective-permute-start.2 = (bf16[512,2048]{1,0:T(8,128)(2,1)}, bf16[512,2048]{1,0:T(8,128)(2,1)}, u32[]{:S(2)}, u32[]{:S(2)}) collective-permute-start(bf16[512,2048]{1,0:T(8,128)(2,1)} %slice.216), channel_id=1, source_target_pairs={{0,1},{1,0},{2,3},{3,2},{4,5},{5,4},{6,7},{7,6},{8,9},{9,8},{10,11... | collective-permute-start | bytes 6291464 | tf_op jit(solution)/shard_map/ppermute | solution.py:31
  11.9 23.6 %collective-permute-start.1 = (bf16[512,2048]{1,0:T(8,128)(2,1)}, bf16[512,2048]{1,0:T(8,128)(2,1)}, u32[]{:S(2)}, u32[]{:S(2)}) collective-permute-start(bf16[512,2048]{1,0:T(8,128)(2,1)} %get-tuple-element.99.n0_ref.c0_ref), channel_id=1, source_target_pairs={{0,1},{1,0},{2,3},{3,2},{4,5},{5,4},{6,7},{7,6},{8,9},{9,8},{10,11... | collective-permute-start | bytes 6291464 | tf_op jit(solution)/shard_map/ppermute | solution.py:31
  15.0 15.1 %collective-permute-start.5 = (bf16[128,2048]{1,0:T(8,128)(2,1)S(1)}, bf16[128,2048]{1,0:T(8,128)(2,1)S(1)}, u32[]{:S(2)}, u32[]{:S(2)}) collective-permute-start(bf16[128,2048]{1,0:T(8,128)(2,1)S(1)} %constant_dynamic-slice_fusion.6), channel_id=1, source_target_pairs={{0,2},{1,3},{2,0},{3,1},{4,6},{5,7},{6,4},{7,5},{8,10},{9,11},{10,... | collective-permute-start | bytes 1572872 | tf_op jit(solution)/shard_map/ppermute | solution.py:31
  18.5 11.0 %collective-permute-start.4 = (f32[8,2048]{1,0:T(8,128)S(1)}, f32[8,2048]{1,0:T(8,128)S(1)}, u32[]{:S(2)}, u32[]{:S(2)}) collective-permute-start(f32[8,2048]{1,0:T(8,128)S(1)} %pad_maximum_fusion.4), channel_id=1, source_target_pairs={{0,3},{1,2},{2,1},{3,0},{4,7},{5,6},{6,5},{7,4},{8,11},{9,10},{10,... | collective-permute-start | bytes 196616 | tf_op jit(solution)/shard_map/ppermute | solution.py:31
  21.4 37.8 %collective-permute-start.9 = (bf16[512,512]{1,0:T(8,128)(2,1)}, bf16[512,512]{1,0:T(8,128)(2,1)}, u32[]{:S(2)}, u32[]{:S(2)}) collective-permute-start(bf16[512,512]{1,0:T(8,128)(2,1)} %get-tuple-element.178), channel_id=1, source_target_pairs={{0,1},{1,0},{2,3},{3,2},{4,5},{5,4},{6,7},{7,6},{8,9},{9,8},{10,11... | collective-permute-start | bytes 1572872 | tf_op jit(solution)/shard_map/ppermute | solution.py:31
  30.1 59.0 %collective-permute-start.10 = (bf16[512,2048]{1,0:T(8,128)(2,1)}, bf16[512,2048]{1,0:T(8,128)(2,1)}, u32[]{:S(2)}, u32[]{:S(2)}) collective-permute-start(bf16[512,2048]{1,0:T(8,128)(2,1)} %get-tuple-element.99.n0_ref.c0_ref), channel_id=1, source_target_pairs={{0,2},{1,3},{2,0},{3,1},{4,6},{5,7},{6,4},{7,5},{8,10},{9,11},{10,... | collective-permute-start | bytes 6291464 | tf_op jit(solution)/shard_map/ppermute | solution.py:31
  32.0 14.0 %collective-permute-start.6 = (bf16[128,2048]{1,0:T(8,128)(2,1)S(1)}, bf16[128,2048]{1,0:T(8,128)(2,1)S(1)}, u32[]{:S(2)}, u32[]{:S(2)}) collective-permute-start(bf16[128,2048]{1,0:T(8,128)(2,1)S(1)} %collective-permute-done.5), channel_id=1, source_target_pairs={{0,8},{4,12},{8,0},{12,4},{16,24},{20,28},{24,16},{28,20},{1,9},{5... | collective-permute-start | bytes 1572872 | tf_op jit(solution)/shard_map/ppermute | solution.py:677
  33.9 24.0 %collective-permute-start.7 = (bf16[128,2048]{1,0:T(8,128)(2,1)S(1)}, bf16[128,2048]{1,0:T(8,128)(2,1)}, u32[]{:S(2)}, u32[]{:S(2)}) collective-permute-start(bf16[128,2048]{1,0:T(8,128)(2,1)S(1)} %collective-permute-done.5), channel_id=1, source_target_pairs={{0,4},{4,0},{8,12},{12,8},{16,20},{20,16},{24,28},{28,24},{1,5},{5... | collective-permute-start | bytes 1572872 | tf_op jit(solution)/shard_map/ppermute | solution.py:676
  44.8 14.3 %collective-permute-start.8 = (bf16[128,2048]{1,0:T(8,128)(2,1)S(1)}, bf16[128,2048]{1,0:T(8,128)(2,1)S(1)}, u32[]{:S(2)}, u32[]{:S(2)}) collective-permute-start(bf16[128,2048]{1,0:T(8,128)(2,1)S(1)} %collective-permute-done.5), channel_id=1, source_target_pairs={{0,12},{4,8},{8,4},{12,0},{16,28},{20,24},{24,20},{28,16},{1,13},{... | collective-permute-start | bytes 1572872 | tf_op jit(solution)/shard_map/ppermute | solution.py:723
  89.1 11.6 %collective-permute-start.11 = (bf16[512,2048]{1,0:T(8,128)(2,1)}, bf16[512,2048]{1,0:T(8,128)(2,1)S(1)}, u32[]{:S(2)}, u32[]{:S(2)}) collective-permute-start(bf16[512,2048]{1,0:T(8,128)(2,1)} %collective-permute-done.10.n_ref.c0_ref.n2_ref), channel_id=1, source_target_pairs={{0,1},{1,0},{2,3},{3,2},{4,5},{5,4},{6,7},{7,6},{8,9},{9,8},{10,11... | collective-permute-start | bytes 6291464 | tf_op jit(solution)/shard_map/ppermute | solution.py:31
  89.1 21.1 %collective-permute-start.12 = (bf16[512,512]{1,0:T(8,128)(2,1)}, bf16[512,512]{1,0:T(8,128)(2,1)S(1)}, u32[]{:S(2)}, u32[]{:S(2)}) collective-permute-start(bf16[512,512]{1,0:T(8,128)(2,1)} %get-tuple-element.103), channel_id=1, source_target_pairs={{0,2},{1,3},{2,0},{3,1},{4,6},{5,7},{6,4},{7,5},{8,10},{9,11},{10,... | collective-permute-start | bytes 1572872 | tf_op jit(solution)/shard_map/ppermute | solution.py:31
  89.7 24.6 %collective-permute-start.13 = (bf16[512,512]{1,0:T(8,128)(2,1)}, bf16[512,512]{1,0:T(8,128)(2,1)S(1)}, u32[]{:S(2)}, u32[]{:S(2)}) collective-permute-start(bf16[512,512]{1,0:T(8,128)(2,1)} %get-tuple-element.104), channel_id=1, source_target_pairs={{0,3},{1,2},{2,1},{3,0},{4,7},{5,6},{6,5},{7,4},{8,11},{9,10},{10,... | collective-permute-start | bytes 1572872 | tf_op jit(solution)/shard_map/ppermute | solution.py:31
  145.9 17.0 %collective-permute-start.15 = (bf16[3,32,2048]{2,1,0:T(8,128)(2,1)S(1)}, bf16[3,32,2048]{2,1,0:T(8,128)(2,1)S(1)}, u32[]{:S(2)}, u32[]{:S(2)}) collective-permute-start(bf16[3,32,2048]{2,1,0:T(8,128)(2,1)S(1)} %fusion.16), channel_id=1, source_target_pairs={{0,8},{1,5},{2,10},{3,7},{8,16},{9,1},{10,18},{11,3},{16,24},{17,9... | collective-permute-start | bytes 1179656 | tf_op jit(solution)/shard_map/ppermute | solution.py:578
  182.8 13.6 %collective-permute-start.17 = (bf16[512,2048]{1,0:T(8,128)(2,1)}, bf16[512,2048]{1,0:T(8,128)(2,1)}, u32[]{:S(2)}, u32[]{:S(2)}) collective-permute-start(bf16[512,2048]{1,0:T(8,128)(2,1)} %slice_bitcast_fusion.1), channel_id=1, source_target_pairs={{0,1},{1,0},{2,3},{3,2},{4,5},{5,4},{6,7},{7,6},{8,9},{9,8},{10,11... | collective-permute-start | bytes 6291464 | tf_op jit(solution)/shard_map/ppermute | solution.py:31
  184.6 65.8 %collective-permute-start.16 = (bf16[2,512,512]{2,1,0:T(8,128)(2,1)}, bf16[2,512,512]{2,1,0:T(8,128)(2,1)S(1)}, u32[]{:S(2)}, u32[]{:S(2)}) collective-permute-start(bf16[2,512,512]{2,1,0:T(8,128)(2,1)} %pad_maximum_fusion), channel_id=1, source_target_pairs={{0,1},{1,0},{2,3},{3,2},{4,5},{5,4},{6,7},{7,6},{8,9},{9,8},{10,11... | collective-permute-start | bytes 3145736 | tf_op jit(solution)/shard_map/ppermute | solution.py:31
  185.4 9.9 %collective-permute-start.18 = (bf16[3,32,2048]{2,1,0:T(8,128)(2,1)}, bf16[3,32,2048]{2,1,0:T(8,128)(2,1)S(1)}, u32[]{:S(2)}, u32[]{:S(2)}) collective-permute-start(bf16[3,32,2048]{2,1,0:T(8,128)(2,1)} %slice_bitcast_fusion.13), channel_id=1, source_target_pairs={{0,8},{1,5},{2,10},{3,7},{8,16},{9,1},{10,18},{11,3},{16,24},{17,9... | collective-permute-start | bytes 1179656 | tf_op jit(solution)/shard_map/ppermute | solution.py:578
  195.4 9.1 %collective-permute-start.20 = (bf16[3,32,2048]{2,1,0:T(8,128)(2,1)S(1)}, bf16[3,32,2048]{2,1,0:T(8,128)(2,1)S(1)}, u32[]{:S(2)}, u32[]{:S(2)}) collective-permute-start(bf16[3,32,2048]{2,1,0:T(8,128)(2,1)S(1)} %fusion.13), channel_id=1, source_target_pairs={{0,8},{1,5},{2,10},{3,7},{8,16},{9,1},{10,18},{11,3},{16,24},{17,9... | collective-permute-start | bytes 1179656 | tf_op jit(solution)/shard_map/ppermute | solution.py:578
  198.3 25.1 %collective-permute-start.28 = (bf16[256,2048]{1,0:T(8,128)(2,1)S(1)}, bf16[256,2048]{1,0:T(8,128)(2,1)S(1)}, u32[]{:S(2)}, u32[]{:S(2)}) collective-permute-start(bf16[256,2048]{1,0:T(8,128)(2,1)S(1)} %fusion), channel_id=1, source_target_pairs={{0,2},{1,3},{2,0},{3,1},{4,6},{5,7},{6,4},{7,5},{8,10},{9,11},{10,... | collective-permute-start | bytes 3145736 | tf_op jit(solution)/shard_map/ppermute | solution.py:31
  234.2 14.2 %collective-permute-start.34 = (bf16[128,2048]{1,0:T(8,128)(2,1)S(1)}, bf16[128,2048]{1,0:T(8,128)(2,1)S(1)}, u32[]{:S(2)}, u32[]{:S(2)}) collective-permute-start(bf16[128,2048]{1,0:T(8,128)(2,1)S(1)} %get-tuple-element.132), channel_id=1, source_target_pairs={{0,2},{1,3},{2,0},{3,1},{4,6},{5,7},{6,4},{7,5},{8,10},{9,11},{10,... | collective-permute-start | bytes 1572872 | tf_op jit(solution)/shard_map/ppermute | solution.py:31
  235.9 12.5 %collective-permute-start.33 = (bf16[3,32,2048]{2,1,0:T(8,128)(2,1)S(1)}, bf16[3,32,2048]{2,1,0:T(8,128)(2,1)S(1)}, u32[]{:S(2)}, u32[]{:S(2)}) collective-permute-start(bf16[3,32,2048]{2,1,0:T(8,128)(2,1)S(1)} %pad_maximum_fusion.2.refs_0_), channel_id=1, source_target_pairs={{0,8},{1,5},{2,10},{3,7},{8,16},{9,1},{10,18},{11,3},{16,24},{17,9... | collective-permute-start | bytes 1179656 | tf_op jit(solution)/shard_map/ppermute | solution.py:578
  237.8 12.4 %collective-permute-start.32 = (bf16[3,32,2048]{2,1,0:T(8,128)(2,1)S(1)}, bf16[3,32,2048]{2,1,0:T(8,128)(2,1)S(1)}, u32[]{:S(2)}, u32[]{:S(2)}) collective-permute-start(bf16[3,32,2048]{2,1,0:T(8,128)(2,1)S(1)} %fusion.4), channel_id=1, source_target_pairs={{0,8},{1,5},{2,10},{3,7},{8,16},{9,1},{10,18},{11,3},{16,24},{17,9... | collective-permute-start | bytes 1179656 | tf_op jit(solution)/shard_map/ppermute | solution.py:578
  240.9 48.3 %collective-permute-start.43 = (bf16[512,2048]{1,0:T(8,128)(2,1)}, bf16[512,2048]{1,0:T(8,128)(2,1)}, u32[]{:S(2)}, u32[]{:S(2)}) collective-permute-start(bf16[512,2048]{1,0:T(8,128)(2,1)} %slice_bitcast_fusion), channel_id=1, source_target_pairs={{0,1},{1,0},{2,3},{3,2},{4,5},{5,4},{6,7},{7,6},{8,9},{9,8},{10,11... | collective-permute-start | bytes 6291464 | tf_op jit(solution)/shard_map/ppermute | solution.py:31
  252.2 51.0 %collective-permute-start.35 = (bf16[2,512,512]{2,1,0:T(8,128)(2,1)S(1)}, bf16[2,512,512]{2,1,0:T(8,128)(2,1)S(1)}, u32[]{:S(2)}, u32[]{:S(2)}) collective-permute-start(bf16[2,512,512]{2,1,0:T(8,128)(2,1)S(1)} %pad_maximum_fusion.1), channel_id=1, source_target_pairs={{0,2},{1,3},{2,0},{3,1},{4,6},{5,7},{6,4},{7,5},{8,10},{9,11},{10,... | collective-permute-start | bytes 3145736 | tf_op jit(solution)/shard_map/ppermute | solution.py:31
  258.1 10.2 %collective-permute-start.39 = (bf16[3,32,2048]{2,1,0:T(8,128)(2,1)S(1)}, bf16[3,32,2048]{2,1,0:T(8,128)(2,1)}, u32[]{:S(2)}, u32[]{:S(2)}) collective-permute-start(bf16[3,32,2048]{2,1,0:T(8,128)(2,1)S(1)} %pad_maximum_fusion.3.refs_0_), channel_id=1, source_target_pairs={{0,8},{1,5},{2,10},{3,7},{8,16},{9,1},{10,18},{11,3},{16,24},{17,9... | collective-permute-start | bytes 1179656 | tf_op jit(solution)/shard_map/ppermute | solution.py:578
  261.0 28.3 %collective-permute-start.44 = (bf16[128,2048]{1,0:T(8,128)(2,1)}, bf16[128,2048]{1,0:T(8,128)(2,1)S(1)}, u32[]{:S(2)}, u32[]{:S(2)}) collective-permute-start(bf16[128,2048]{1,0:T(8,128)(2,1)} %get-tuple-element.138), channel_id=1, source_target_pairs={{0,2},{1,3},{2,0},{3,1},{4,6},{5,7},{6,4},{7,5},{8,10},{9,11},{10,... | collective-permute-start | bytes 1572872 | tf_op jit(solution)/shard_map/ppermute | solution.py:31
  264.1 36.3 %collective-permute-start.42 = (bf16[3,32,2048]{2,1,0:T(8,128)(2,1)}, bf16[3,32,2048]{2,1,0:T(8,128)(2,1)}, u32[]{:S(2)}, u32[]{:S(2)}) collective-permute-start(bf16[3,32,2048]{2,1,0:T(8,128)(2,1)} %collective-permute-done.40.refs_3_), channel_id=1, source_target_pairs={{0,8},{1,5},{2,10},{3,7},{8,16},{9,1},{10,18},{11,3},{16,24},{17,9... | collective-permute-start | bytes 1179656 | tf_op jit(solution)/shard_map/ppermute | solution.py:578
  268.3 33.7 %collective-permute-start.41 = (bf16[3,32,2048]{2,1,0:T(8,128)(2,1)}, bf16[3,32,2048]{2,1,0:T(8,128)(2,1)}, u32[]{:S(2)}, u32[]{:S(2)}) collective-permute-start(bf16[3,32,2048]{2,1,0:T(8,128)(2,1)} %collective-permute-done.39.refs_1_), channel_id=1, source_target_pairs={{0,8},{1,5},{2,10},{3,7},{8,16},{9,1},{10,18},{11,3},{16,24},{17,9... | collective-permute-start | bytes 1179656 | tf_op jit(solution)/shard_map/ppermute | solution.py:578
  302.0 10.6 %collective-permute-start.45 = (bf16[3,32,2048]{2,1,0:T(8,128)(2,1)}, bf16[3,32,2048]{2,1,0:T(8,128)(2,1)S(1)}, u32[]{:S(2)}, u32[]{:S(2)}) collective-permute-start(bf16[3,32,2048]{2,1,0:T(8,128)(2,1)} %collective-permute-done.41.refs_2_), channel_id=1, source_target_pairs={{0,8},{1,5},{2,10},{3,7},{8,16},{9,1},{10,18},{11,3},{16,24},{17,9... | collective-permute-start | bytes 1179656 | tf_op jit(solution)/shard_map/ppermute | solution.py:578
  304.3 10.0 %collective-permute-start.49 = (f32[8,2048]{1,0:T(8,128)S(1)}, f32[8,2048]{1,0:T(8,128)S(1)}, u32[]{:S(2)}, u32[]{:S(2)}) collective-permute-start(f32[8,2048]{1,0:T(8,128)S(1)} %pad_maximum_fusion.5), channel_id=1, source_target_pairs={{0,1},{1,0},{2,3},{3,2},{4,5},{5,4},{6,7},{7,6},{8,9},{9,8},{10,11... | collective-permute-start | bytes 196616 | tf_op jit(solution)/shard_map/ppermute | solution.py:31
  315.1 14.2 %collective-permute-start.50 = (f32[8,2048]{1,0:T(8,128)S(1)}, f32[8,2048]{1,0:T(8,128)S(1)}, u32[]{:S(2)}, u32[]{:S(2)}) collective-permute-start(f32[8,2048]{1,0:T(8,128)S(1)} %pad_maximum_fusion.6), channel_id=1, source_target_pairs={{0,2},{1,3},{2,0},{3,1},{4,6},{5,7},{6,4},{7,5},{8,10},{9,11},{10,... | collective-permute-start | bytes 196616 | tf_op jit(solution)/shard_map/ppermute | solution.py:31
  321.1 12.3 %collective-permute-start.51 = (bf16[3,32,2048]{2,1,0:T(8,128)(2,1)S(1)}, bf16[3,32,2048]{2,1,0:T(8,128)(2,1)}, u32[]{:S(2)}, u32[]{:S(2)}) collective-permute-start(bf16[3,32,2048]{2,1,0:T(8,128)(2,1)S(1)} %collective-permute-done.47.refs_4_), channel_id=1, source_target_pairs={{0,8},{1,5},{2,10},{3,7},{8,16},{9,1},{10,18},{11,3},{16,24},{17,9... | collective-permute-start | bytes 1179656 | tf_op jit(solution)/shard_map/ppermute | solution.py:578
  322.7 10.8 %collective-permute-start.52 = (bf16[3,32,2048]{2,1,0:T(8,128)(2,1)S(1)}, bf16[3,32,2048]{2,1,0:T(8,128)(2,1)S(1)}, u32[]{:S(2)}, u32[]{:S(2)}) collective-permute-start(bf16[3,32,2048]{2,1,0:T(8,128)(2,1)S(1)} %collective-permute-done.48.refs_6_), channel_id=1, source_target_pairs={{0,8},{1,5},{2,10},{3,7},{8,16},{9,1},{10,18},{11,3},{16,24},{17,9... | collective-permute-start | bytes 1179656 | tf_op jit(solution)/shard_map/ppermute | solution.py:578
  (62 other events, 577.9 us)

commit v3 on v2

--- a/solution.py
+++ b/solution.py
@@ -403,20 +403,20 @@
     )(slots, near, far, *ns)
 
 
-def input_near_kernel(sc, w0_ref, w1_ref, w2_ref, sg_ref, ex_ref, out_ref):
+def input_near_kernel(sc, w0_ref, w1_ref, w2_ref, sg_ref, ex_ref, *out_refs):
     mine = (pl.program_id(0) == sc[0]).astype(F32)
-    for b in range(2):
+    for b, out_ref in enumerate(out_refs):
         total = ex_ref[b].astype(F32) * mine
         for kind, w_ref in enumerate((w0_ref, w1_ref, w2_ref)):
             total = total + jnp.dot(sg_ref[b, kind], w_ref[...], preferred_element_type=F32)
-        out_ref[b] = total.astype(BF)
-
-
-def input_far_kernel(sc, w0_ref, w1_ref, w2_ref, sg0_ref, sg1_ref, ex0_ref, ex1_ref, out_ref):
+        out_ref[...] = total.astype(BF)
+
+
+def input_far_kernel(sc, w0_ref, w1_ref, w2_ref, sg0_ref, sg1_ref, ex0_ref, ex1_ref, *out_refs):
     w_refs = (w0_ref, w1_ref, w2_ref)
     mine = (pl.program_id(0) == sc[0]).astype(F32)
     tile = sg0_ref.shape[3]
-    for b in range(2):
+    for b, out_ref in enumerate(out_refs):
         total = None
         for h, sg_ref in enumerate((sg0_ref, sg1_ref)):
             for kind in range(3):
@@ -425,7 +425,7 @@
                 total = part if total is None else total + part
         for h, ex_ref in enumerate((ex0_ref, ex1_ref)):
             cols = slice(h * tile, (h + 1) * tile)
-            out_ref[b, :, cols] = (total[:, cols] + ex_ref[b].astype(F32) * mine).astype(BF)
+            out_ref[:, cols] = (total[:, cols] + ex_ref[b].astype(F32) * mine).astype(BF)
 
 
 def run_input(scal, kernel, name, sgs, exs, weight, w_core, w_x):
@@ -447,25 +447,24 @@
             ]
             + [spec((2, 3, tok, part), lambda n, sc: (0, 0, 0, 0))] * len(sgs)
             + [spec((2, tok, part), lambda n, sc: (0, 0, 0))] * len(exs),
-            out_specs=spec((2, tok, own), lambda n, sc: (0, 0, n)),
+            out_specs=[spec((tok, own), lambda n, sc: (0, n))] * 2,
         ),
-        out_shape=jax.ShapeDtypeStruct((2, tok, wide), BF),
+        out_shape=[jax.ShapeDtypeStruct((tok, wide), BF)] * 2,
         cost_estimate=CHEAP,
     )(scal, weight, w_core, w_x, *sgs, *exs)
 
 
 def back_kernel(
-    home_ref, back_ref, side0_ref, side1_ref, side2_ref, x_ref, mean_ref, rstd_ref, gain_ref, og_ref, out_ref, sum_ref
+    home_ref, back_ref, side_ref, x_ref, mean_ref, rstd_ref, gain_ref, og_ref, *refs
 ):
     rows, wide = x_ref.shape
     per = 16
-    step = pl.program_id(0)
+    out_ref, sum_ref = refs[-2:]
 
     def some_rows(i, carry):
         gains, shifts = carry
         at = pl.ds(pl.multiple_of(i * per, per), per)
-        side = jnp.where(step < 2, side0_ref[at, :], jnp.where(step < 3, side1_ref[at, :], side2_ref[at, :]))
-        grad = home_ref[0, at, :].astype(F32) + back_ref[at, :].astype(F32) + side.astype(F32)
+        grad = home_ref[at, :].astype(F32) + back_ref[at, :].astype(F32) + side_ref[at, :].astype(F32)
         rstd = rstd_ref[at, 0:1]
         scaled_in = (x_ref[at, :].astype(F32) - mean_ref[at, 0:1]) * rstd
         product = grad * scaled_in
@@ -488,31 +487,32 @@
     sum_ref[8:16, :] += shifts
 
 
-def run_back(home, back, sides, x, mean, rstd, gain, og):
+def run_back(home, back, side, x, mean, rstd, gain, og, half, before):
     tok, wide = x.shape
     rows = tok // 4
+    held = [] if before is None else [before]
     spec = pl.BlockSpec
-    row = lambda i: (i, 0)
+    row = lambda i: (i + 2 * half, 0)
     return pl.pallas_call(
         back_kernel,
         name="norm_back",
-        grid=(tok // rows,),
+        grid=(2,),
         in_specs=[
-            spec((1, rows, wide), lambda i: (0, i, 0)),
             spec((rows, wide), row),
-            spec((rows, wide), lambda i: (jnp.minimum(i, 1), 0)),
-            spec((rows, wide), lambda i: (0, 0)),
-            spec((rows, wide), lambda i: (0, 0)),
+            spec((rows, wide), row),
+            spec((rows, wide), lambda i: (i, 0)),
             spec((rows, wide), row),
             spec((rows, 128), row),
             spec((rows, 128), row),
             spec((1, wide), lambda i: (0, 0)),
             spec((rows, wide), row),
-        ],
+        ]
+        + [spec(memory_space=pl.ANY)] * len(held),
         out_specs=[spec((rows, wide), row), spec((16, wide), lambda i: (0, 0))],
         out_shape=[jax.ShapeDtypeStruct((tok, wide), F32), jax.ShapeDtypeStruct((16, wide), F32)],
+        input_output_aliases={8: 0} if held else {},
         cost_estimate=CHEAP,
-    )(home, back, *sides, x, mean, rstd, gain, og)
+    )(home, back, side, x, mean, rstd, gain, og, *held)
 
 
 def output_kernel(sc, x_ref, own_ref, core_ref, side_ref, out_ref):
@@ -678,47 +678,43 @@
     else:
         w_send = lax.dynamic_slice_in_dim(weight, x_at * own, own, axis=0)
         w_part = swap(w_send, XSIDE)
-    w_pass = weight[own : 2 * own]
-    w_core = swap(w_pass, CORE)
+    norm_own, mean, rstd = run_norm(after(inputs, w_send), ln_gain[None], ln_bias[None])
+    norm_core = swap(norm_own, CORE)
+    norm_side = swap(norm_own, XSIDE)
+    w_core = swap(after(weight, norm_own)[own : 2 * own], CORE)
 
     def columns(value, index, start=0, width=own):
         return lax.dynamic_slice_in_dim(value, index * own + start, width, axis=1)
 
-    firsts = jnp.sum(sentence_ids[0][None, :] < jnp.arange(SENT, dtype=jnp.int32)[:, None], axis=1)
+    firsts = jnp.sum(after(sentence_ids, norm_own)[0][None, :] < jnp.arange(SENT, dtype=jnp.int32)[:, None], axis=1)
     small = jnp.concatenate(
         [start_states, jnp.zeros((SENT, wide), F32) + firsts.astype(F32)[:, None]], axis=0
     )
     near_small = [small, swap(small, CORE)]
-    far_small = [swap(small, XSIDE), swap(small, DIAG)]
-
-    norm_own, mean, rstd = run_norm(after(inputs, (w_send, w_pass, small)), ln_gain[None], ln_bias[None])
-    norm_core = swap(norm_own, CORE)
-    norm_side = swap(after(norm_own, w_part), XSIDE)
-    smalls = [columns(v, t) for v in (*near_small, *far_small)]
-    out_later = after(out_grad, norm_own)
-    og_own = columns(out_later, t)
-    og_core = swap(columns(out_later, t ^ CORE), CORE)
-    og_send = [columns(out_later, t ^ by) for by in (XSIDE, DIAG)]
 
     table = jnp.asarray(KIND_OF, jnp.int32)[t]
-    scals = [
-        jnp.concatenate(
-            [
+
+    def tables(pair):
+        parts = [columns(v, t) for v in pair]
+        numbers = []
+        for part in parts:
+            numbers += [
                 t[None].astype(jnp.int32),
                 table,
                 part[SENT:, 0].astype(jnp.int32),
                 jnp.full((1,), tok, jnp.int32),
                 stay_at[None].astype(jnp.int32),
             ]
-        )
-        for part in smalls
-    ]
-    starts = [part[:SENT] for part in smalls]
-    near_scal = jnp.concatenate(scals[:2])
-    far_scal = jnp.concatenate(scals[2:])
+        return jnp.concatenate(numbers), [part[:SENT] for part in parts]
+
+    near_scal, near_starts = tables(near_small)
     scal = jnp.concatenate([t[None].astype(jnp.int32), jnp.zeros((8,), jnp.int32), stay_at[None].astype(jnp.int32)])
 
-    early = run_early(scal, norm_own, norm_core, weight, after(w_core, (og_own, *og_send, *starts)))
+    out_later = after(out_grad, norm_own)
+    og_own = columns(out_later, t)
+    og_core = swap(columns(out_later, t ^ CORE), CORE)
+    og_send = [columns(out_later, t ^ by) for by in (XSIDE, DIAG)]
+    early = run_early(scal, norm_own, norm_core, weight, after(w_core, (og_own, *og_send, *near_starts)))
     if ringed:
         by_both = lax.ppermute(after(w_part, early), "dp", [(i, i ^ 3) for i in range(dp)])
         w_x = jnp.zeros((4, quarter, wide), BF)
@@ -728,12 +724,11 @@
     else:
         w_x = w_part
     near = run_near(
-        near_scal, early, w_x, (norm_own, norm_core), (og_own, og_core), starts[:2], gate_bias
+        near_scal, early, w_x, (norm_own, norm_core), (og_own, og_core), near_starts, gate_bias
     )
-    og_far = [swap(after(og_send[i], early), by) for i, by in ((0, XSIDE), (1, DIAG))]
-    near_in = run_input(scal, input_near_kernel, "input_near", near[1:2], near[2:3], weight, w_core, w_x)
-    near_back = swap(near_in[1], CORE)
-    norm_side = after(norm_side, near_in)
+    far_scal, far_starts = tables([swap(after(small, near[0]), by) for by in (XSIDE, DIAG)])
+    og_far = [swap(after(sent, early), by) for sent, by in zip(og_send, (XSIDE, DIAG))]
+    norm_side = after(norm_side, (near[0], far_scal))
     norm_diag = swap(norm_side, CORE)
     ns = [norm_own, norm_core, norm_side, norm_diag]
     far_streams = [run_project(scal, norm_side, weight, w_core, w_x)]
@@ -744,7 +739,7 @@
         slots = jnp.arange(RING, dtype=jnp.int32)
 
     def far_part(h, gate):
-        return run_far(far_scal, gate(far_streams), ns[2:], og_far, starts[2:], gate_bias, h)
+        return run_far(far_scal, gate(far_streams), ns[2:], og_far, far_starts, gate_bias, h)
 
     def far_weight(h, gate):
         return run_weight(slots, near[1], gate(far[h][1]), ns, h)
@@ -769,22 +764,22 @@
         sgs, exs = [[v[i] for v in far] for i in (1, 2)]
         work["far_in"] = run_input(scal, input_far_kernel, "input_far", sgs, gate(exs), weight, w_core, w_x)
         work["far_back"] = swap(work["far_in"][1], CORE)
-        work["sides"] = []
+        work["side"] = []
         mark(work["far_in"])
 
-    def to_x(start, count):
+    def to_x(half):
         def task():
-            rows = slice(start * tok // 4, (start + count) * tok // 4)
-            sent = gate(add(work["far_in"][0, rows], work["far_back"][rows]))
-            work["sides"].append(swap(sent, XSIDE))
+            rows = slice(half * tok // 2, (half + 1) * tok // 2)
+            sent = gate(add(gate(work["far_in"][0])[rows], work["far_back"][rows]))
+            work["side"].append(swap(sent, XSIDE))
             mark(sent)
 
         return task
 
-    def arrive(i):
+    def arrive(half):
         def task():
-            work["sides"][i] = gate(work["sides"][i])
-            mark(work["sides"][i])
+            work["side"][half] = gate(work["side"][half])
+            mark(work["side"][half])
 
         return task
 
@@ -802,11 +797,24 @@
         work["side_outs"] = swap(sent, XSIDE)
         mark(sent)
 
-    def norm_back():
-        work["input_grad"], work["norm_sums"] = run_back(
-            near_in, near_back, gate(work["sides"]), inputs, mean, rstd, ln_gain[None], out_grad
+    def near_input():
+        work["near_in"] = run_input(
+            scal, input_near_kernel, "input_near", near[1:2], [gate(near[2])], weight, w_core, w_x
         )
-        mark(work["norm_sums"])
+        work["near_back"] = swap(work["near_in"][1], CORE)
+        mark(work["near_in"])
+
+    def norm_back(half):
+        def task():
+            side = gate(work["side"][half])
+            work["input_grad"], sums = run_back(
+                work["near_in"][0], work["near_back"], side, inputs, mean, rstd, ln_gain[None], out_grad,
+                half, work.get("input_grad"),
+            )
+            work["norm_sums"] = work["norm_sums"] + sums if half else sums
+            mark(sums)
+
+        return task
 
     def output():
         work["output"] = run_output(scal, inputs, near[0], work["core_outs"], gate(work["side_outs"]))
@@ -859,45 +867,55 @@
     if ringed:
         kinds = jnp.stack([stay_at, jnp.ones_like(core), x_at])
         where = jnp.concatenate([shards, kinds]).astype(jnp.int32)
-        fill = {
-            1: [out_core, far_in],
-            2: [to_x(0, 2)],
-            5: [arrive(0)],
-            6: [to_x(2, 1)],
-            7: [arrive(1)],
-            8: [to_x(3, 1), out_side],
-            10: [arrive(2), norm_back],
-            11: [outs_arrive, sums_core],
-            12: [sums_side],
-            13: [output, sums_ends],
-            14: [sums_dp(2)],
-            15: [sums_dp(4)],
-        }
-        far.append(far_part(0, gate))
-        grad = far_weight(0, gate)
-        rings = [Ring(grad)]
-        mark(rings[0].piece)
-        far.append(far_part(1, gate))
-        mark(far[1][1])
-        rings[0].step(gate)
-        mark(rings[0].piece)
-        grad = far_weight(1, gate)
-        mark(grad)
-        rings[0].step(gate)
-        mark(rings[0].piece)
-        rings.append(Ring(gate(grad)))
-        mark(rings[1].piece)
-        weight_grad = None
-        for n in range(1, 16):
-            for task in fill.get(n, ()):
-                task()
-            for i, ring in enumerate(rings):
-                if len(ring.pieces) < RING:
-                    ring.step(gate)
-                    mark(ring.piece)
-                    if len(ring.pieces) == RING:
-                        weight_grad = place_pieces(where, ring.pieces, i, weight_grad)
-        sums_dp(8)()
+        rings = []
+        placed = [None]
+
+        def start(h):
+            def task():
+                rings.append(Ring(gate(work["grad"])))
+                mark(rings[h].piece)
+
+            return task
+
+        def scan(h):
+            def task():
+                far.append(far_part(h, gate))
+                mark(far[h][1])
+
+            return task
+
+        def weigh(h):
+            def task():
+                work["grad"] = far_weight(h, gate)
+                mark(work["grad"])
+
+            return task
+
+        def hop(h):
+            def task():
+                ring = rings[h]
+                ring.step(gate)
+                mark(ring.piece)
+
+            return task
+
+        def put(h):
+            def task():
+                placed[0] = place_pieces(where, gate(rings[h].pieces), h, placed[0])
+                mark(placed[0])
+
+            return task
+
+        r0, r1 = hop(0), hop(1)
+        for task in (
+            scan(0), weigh(0), start(0), scan(1), r0, far_in, r0, weigh(1), r0, start(1), to_x(0),
+            out_core, r0, r1, r0, r1, r0, r1, arrive(0), r0, to_x(1), r1, near_input, r0, r1, r0, norm_back(0), r1,
+            arrive(1), r0, r1, norm_back(1), r0, r1, sums_core, r0, r1, sums_side, out_side, r0, r1, sums_ends, r0, r1,
+            sums_dp(2), r0, r1, outs_arrive, sums_dp(4), r1, put(0), r1, output, sums_dp(8), r1, put(1),
+        ):
+            task()
+        assert all(len(ring.pieces) == RING for ring in rings)
+        weight_grad = placed[0]
         weight_grad = weight_grad.reshape(3 * own, wide)
     else:
         rows = []
@@ -909,7 +927,7 @@
         rows = jnp.concatenate(rows, axis=1).astype(F32)
         weight_grad = jnp.where(core == 0, rows, rows[::-1]).reshape(3 * own, wide)
         for task in (
-            far_in, to_x(0, 2), to_x(2, 1), to_x(3, 1), out_core, out_side, norm_back, sums_core, sums_side, output,
+            near_input, far_in, to_x(0), to_x(1), out_core, out_side, norm_back(0), norm_back(1), sums_core, sums_side, output,
             sums_ends,
         ):
             task()

time: 358 us -> 341 us (0.953)
  waiting for transfers between devices: 108 us -> 84.3 us
    ppermute x28, waiting for transfers between devices: 57.1 us -> 38.9 us  [around(): return lax.ppermute(value, ('dp', 'tp'), pairs)]
    ppermute x24 -> x23, waiting for transfers between devices: 38.1 us -> 23.5 us  [swap(): return lax.ppermute(value, 'tp', [(t, t ^ by) for t in range(TP)])]
    ppermute x3, waiting for transfers between devices: 0.01 us -> 10.6 us  [send_sums(): lax.ppermute(work['sums'], 'dp', [(i, i ^ bit) for i in range(dp)])]
    ppermute x28, starting transfers between devices: 36.4 us -> 42.4 us  [around(): return lax.ppermute(value, ('dp', 'tp'), pairs)]
    ppermute x24 -> x23, starting transfers between devices: 18.2 us -> 13 us  [swap(): return lax.ppermute(value, 'tp', [(t, t ^ by) for t in range(TP)])]
    squeeze x2 -> x0, local copies, waits for them, and re-layouts: 4.76 us -> none  [the longest x1 3.31 us: far_in(): work['far_back'] = swap(work['far_in'][1], CORE)]
    pallas_call x1 -> x2, Pallas kernels: 10.3 us -> 12.5 us  [run_back(): pl.pallas_call(back_kernel, name='norm_back', grid=(2,), in_specs=[spec((...]
  transfers between devices with their start and end apart: 58 -> 57, of which waited for: 28 -> 26; matrix products, arithmetic and copies ran while one was open for 8% -> 10% of each run, Pallas kernels for 29% -> 29%
where the time goes in v3:
time: 341 us; the launch traced here: 339 us
  Pallas kernels  141 us (41%)
  waiting for transfers between devices  84.3 us (25%)
  starting transfers between devices  63.8 us (19%)
  local copies, waits for them, and re-layouts  26.9 us (8%)
  other arithmetic  21.5 us (6%)
    ppermute x28, starting transfers between devices, around(): return lax.ppermute(value, ('dp', 'tp'), pairs)  42.4 us
    ppermute x28, waiting for transfers between devices, around(): return lax.ppermute(value, ('dp', 'tp'), pairs)  38.9 us
    pallas_call x2, Pallas kernels, run_weight(): pl.pallas_call(weight_kernel, name='weight_grad', grid_spec=pltpu.Prefetc...  27 us
    ppermute x23, waiting for transfers between devices, swap(): return lax.ppermute(value, 'tp', [(t, t ^ by) for t in range(TP)])  23.5 us
    pallas_call x2, Pallas kernels, run_input(): pl.pallas_call(kernel, name=name, grid_spec=pltpu.PrefetchScalarGridSpec(...  23.4 us
    pallas_call x1, Pallas kernels, run_near(): pl.pallas_call(near_kernel, name='near', grid_spec=pltpu.PrefetchScalarGr...  16.7 us
    pallas_call x2, Pallas kernels, run_project(): pl.pallas_call(project_kernel, name='project', grid_spec=pltpu.PrefetchSc...  16.3 us
    pallas_call x2, Pallas kernels, run_far(): pl.pallas_call(far_kernel, name='far', grid_spec=pltpu.PrefetchScalarGrid...  13.3 us
  transfers between devices with their start and end apart: 57, of which 26 were waited for; matrix products, arithmetic and copies ran while one was open for 10% of the time, Pallas kernels for 29%

profile of v3, /device:TPU:0, one launch (start us, length us, event | category | flops | bytes accessed | tf_op | source)
XLA Modules:
  0.0 339.0 jit_solution(4377234745615921664)
XLA Ops:
  1.8 6.2 %norm.1 = (bf16[512,2048]{1,0:T(8,128)(2,1)}, f32[512,128]{1,0:T(8,128)}, f32[512,128]{1,0:T(8,128)}) custom-call(bf16[512,2048]{1,0:T(8,128)(2,1)} %x_ref.6, f32[1,2048]{1,0:T(1,128)} %bitcast.138, f32[1,2048]{1,0:T(1,128)} %bitcast.141), custom_call_target="tpu_custom_call" | custom-call | flops 1 | bytes 1 | tf_op jit(solution)/shard_map/norm/pallas_call | solution.py:55
  7.9 3.3 slice.204
  11.8 3.0 collective-permute-start.3
  20.6 6.9 %collective-permute-done.3 = bf16[128,2048]{1,0:T(8,128)(2,1)S(1)} collective-permute-done((bf16[128,2048]{1,0:T(8,128)(2,1)S(1)}, bf16[128,2048]{1,0:T(8,128)(2,1)S(1)}, u32[]{:S(2)}, u32[]{:S(2)}) %collective-permute-start.3) | collective-permute-done | bytes 524320 | tf_op jit(solution)/shard_map/ppermute | solution.py:31
  31.5 9.3 %early.1.e_ref = bf16[2,2,512,512]{3,2,1,0:T(8,128)(2,1)} custom-call(s32[10]{0:T(128)} %pad_add_fusion.sc, bf16[512,2048]{1,0:T(8,128)(2,1)} %get-tuple-element.118.n0_ref.c0_ref, bf16[512,2048]{1,0:T(8,128)(2,1)} %collective-permute-done.1.n1_ref.c1_ref, bf16[1536,2048]{1,0:T(8,128)(2,1)} %w0_ref.9, bf16[512,2048]{1,0:T(8,128)(2,1)} %collective-permute-done.2.w1_ref), custom_call_target="tpu_custom_call" | custom-call | flops 4294967296 | bytes 8388608 | tf_op jit(solution)/shard_map/early/pallas_call | solution.py:84
  40.9 11.1 %collective-permute-done.5 = bf16[128,2048]{1,0:T(8,128)(2,1)} collective-permute-done((bf16[128,2048]{1,0:T(8,128)(2,1)S(1)}, bf16[128,2048]{1,0:T(8,128)(2,1)}, u32[]{:S(2)}, u32[]{:S(2)}) %collective-permute-start.5) | collective-permute-done | bytes 524320 | tf_op jit(solution)/shard_map/ppermute | solution.py:676
  54.6 16.7 %near.1 = (bf16[2,512,512]{2,1,0:T(8,128)(2,1)}, bf16[2,3,512,512]{3,2,1,0:T(8,128)(2,1)}, bf16[2,512,512]{2,1,0:T(8,128)(2,1)}, f32[2,8,512]{2,1,0:T(8,128)}, f32[2,8,512]{2,1,0:T(8,128)}) custom-call(s32[20]{0:T(128)} %concatenate.61.sc, bf16[2,2,512,512]{3,2,1,0:T(8,128)(2,1)} %early.1.e_ref, bf16[512,2048]{1,0:T(8,128)(2,1)} %bitcast.128, ...), custom_call_target="tpu_custom_call" | custom-call | flops 1 | bytes 1 | tf_op jit(solution)/shard_map/near/pallas_call | solution.py:311
  80.4 8.1 %project.2.s0_ref = bf16[3,512,512]{2,1,0:T(8,128)(2,1)} custom-call(s32[10]{0:T(128)} %pad_add_fusion.sc, bf16[512,2048]{1,0:T(8,128)(2,1)} %collective-permute-done.10.n_ref.c0_ref.n2_ref, bf16[1536,2048]{1,0:T(8,128)(2,1)} %w0_ref.9, bf16[512,2048]{1,0:T(8,128)(2,1)} %collective-permute-done.2.w1_ref, bf16[512,2048]{1,0:T(8,128)(2,1)} %bitcast.129), custom_call_target="tpu_custom_call" | custom-call | flops 1 | bytes 1 | tf_op jit(solution)/shard_map/project/pallas_call | solution.py:114
  91.1 8.1 %project.3.s1_ref = bf16[3,512,512]{2,1,0:T(8,128)(2,1)} custom-call(s32[10]{0:T(128)} %pad_add_fusion.sc, bf16[512,2048]{1,0:T(8,128)(2,1)} %copy-done.1, bf16[1536,2048]{1,0:T(8,128)(2,1)} %w0_ref.9, bf16[512,2048]{1,0:T(8,128)(2,1)} %collective-permute-done.2.w1_ref, bf16[512,2048]{1,0:T(8,128)(2,1)} %bitcast.130), custom_call_target="tpu_custom_call" | custom-call | flops 1 | bytes 1 | tf_op jit(solution)/shard_map/project/pallas_call | solution.py:114
  99.2 4.0 %collective-permute-done.13.og1_ref = bf16[512,512]{1,0:T(8,128)(2,1)S(1)} collective-permute-done((bf16[512,512]{1,0:T(8,128)(2,1)}, bf16[512,512]{1,0:T(8,128)(2,1)S(1)}, u32[]{:S(2)}, u32[]{:S(2)}) %collective-permute-start.13) | collective-permute-done | bytes 524320 | tf_op jit(solution)/shard_map/ppermute | solution.py:31
  104.1 6.7 %far.2 = (bf16[2,512,256]{2,1,0:T(8,128)(2,1)}, bf16[2,3,512,256]{3,2,1,0:T(8,128)(2,1)}, bf16[2,512,256]{2,1,0:T(8,128)(2,1)}, f32[2,8,256]{2,1,0:T(8,128)}, f32[2,8,256]{2,1,0:T(8,128)}) custom-call(s32[20]{0:T(128)} %concatenate.62.sc, bf16[3,512,512]{2,1,0:T(8,128)(2,1)} %project.2.s0_ref, bf16[3,512,512]{2,1,0:T(8,128)(2,1)} %project.3.s1_ref, ...), custom_call_target="tpu_custom_call" | custom-call | flops 1 | bytes 1 | tf_op jit(solution)/shard_map/far/pallas_call | solution.py:346
  110.7 13.5 %weight_grad.2 = bf16[8,3,32,2048]{3,2,1,0:T(8,128)(2,1)} custom-call(s32[8]{0:T(128)} %and_select_fusion.1.sc, bf16[2,3,512,512]{3,2,1,0:T(8,128)(2,1)} %get-tuple-element.131.near_ref.sg_ref, bf16[2,3,512,256]{3,2,1,0:T(8,128)(2,1)} %get-tuple-element.132.far_ref.sg0_ref, bf16[512,2048]{1,0:T(8,128)(2,1)} %get-tuple-element.118.n0_ref.c0_ref, ...), custom_call_target="tpu_custom_call" | custom-call | flops 1 | bytes 1 | tf_op jit(solution)/shard_map/weight_grad/pallas_call | solution.py:388
  125.9 6.6 %far.3 = (bf16[2,512,256]{2,1,0:T(8,128)(2,1)}, bf16[2,3,512,256]{3,2,1,0:T(8,128)(2,1)}, bf16[2,512,256]{2,1,0:T(8,128)(2,1)}, f32[2,8,256]{2,1,0:T(8,128)}, f32[2,8,256]{2,1,0:T(8,128)}) custom-call(s32[20]{0:T(128)} %concatenate.62.sc, bf16[3,512,512]{2,1,0:T(8,128)(2,1)} %project.2.s0_ref, bf16[3,512,512]{2,1,0:T(8,128)(2,1)} %project.3.s1_ref, ...), custom_call_target="tpu_custom_call" | custom-call | flops 1 | bytes 1 | tf_op jit(solution)/shard_map/far/pallas_call | solution.py:346
  136.4 11.7 %input_far.1 = (bf16[512,2048]{1,0:T(8,128)(2,1)}, bf16[512,2048]{1,0:T(8,128)(2,1)}) custom-call(s32[10]{0:T(128)} %pad_add_fusion.sc, bf16[1536,2048]{1,0:T(8,128)(2,1)} %w0_ref.9, bf16[512,2048]{1,0:T(8,128)(2,1)} %collective-permute-done.2.w1_ref, bf16[512,2048]{1,0:T(8,128)(2,1)} %bitcast.131, ...), custom_call_target="tpu_custom_call" | custom-call | flops 1 | bytes 1 | tf_op jit(solution)/shard_map/input_far/pallas_call | solution.py:437
  152.3 13.6 %weight_grad.3 = bf16[8,3,32,2048]{3,2,1,0:T(8,128)(2,1)} custom-call(s32[8]{0:T(128)} %and_select_fusion.1.sc, bf16[2,3,512,512]{3,2,1,0:T(8,128)(2,1)} %get-tuple-element.131.near_ref.sg_ref, bf16[2,3,512,256]{3,2,1,0:T(8,128)(2,1)} %get-tuple-element.144.sg1_ref.far_ref, bf16[512,2048]{1,0:T(8,128)(2,1)} %get-tuple-element.118.n0_ref.c0_ref, ...), custom_call_target="tpu_custom_call" | custom-call | flops 1 | bytes 1 | tf_op jit(solution)/shard_map/weight_grad/pallas_call | solution.py:388
  175.2 4.9 %collective-permute-done.20 = bf16[3,32,2048]{2,1,0:T(8,128)(2,1)S(1)} collective-permute-done((bf16[3,32,2048]{2,1,0:T(8,128)(2,1)S(1)}, bf16[3,32,2048]{2,1,0:T(8,128)(2,1)S(1)}, u32[]{:S(2)}, u32[]{:S(2)}) %collective-permute-start.20) | collective-permute-done | bytes 393248 | tf_op jit(solution)/shard_map/ppermute | solution.py:578
  183.8 4.2 %collective-permute-done.22 = bf16[3,32,2048]{2,1,0:T(8,128)(2,1)S(1)} collective-permute-done((bf16[3,32,2048]{2,1,0:T(8,128)(2,1)S(1)}, bf16[3,32,2048]{2,1,0:T(8,128)(2,1)S(1)}, u32[]{:S(2)}, u32[]{:S(2)}) %collective-permute-start.22) | collective-permute-done | bytes 393248 | tf_op jit(solution)/shard_map/ppermute | solution.py:578
  210.0 11.6 %input_near.1 = (bf16[512,2048]{1,0:T(8,128)(2,1)}, bf16[512,2048]{1,0:T(8,128)(2,1)}) custom-call(s32[10]{0:T(128)} %pad_add_fusion.sc, bf16[1536,2048]{1,0:T(8,128)(2,1)} %w0_ref.9, bf16[512,2048]{1,0:T(8,128)(2,1)} %collective-permute-done.2.w1_ref, bf16[512,2048]{1,0:T(8,128)(2,1)} %bitcast.132, ...), custom_call_target="tpu_custom_call" | custom-call | flops 1 | bytes 1 | tf_op jit(solution)/shard_map/input_near/pallas_call | solution.py:437
  226.3 3.3 collective-permute-done.30
  235.2 3.1 collective-permute-done.31.refs_1_
  239.8 6.2 %norm_back.2 = (f32[512,2048]{1,0:T(8,128)}, f32[16,2048]{1,0:T(8,128)}) custom-call(bf16[512,2048]{1,0:T(8,128)(2,1)} %get-tuple-element.168.home_ref, bf16[512,2048]{1,0:T(8,128)(2,1)} %collective-permute-done.28.back_ref, bf16[256,2048]{1,0:T(8,128)(2,1)} %copy-done.16, bf16[512,2048]{1,0:T(8,128)(2,1)} %x_ref.6, f32[512,128]{1,0:T(8,128)} %get-tuple-element.174.mean_ref, ...), custom_call_target="tpu_custom_call" | custom-call | flops 1 | bytes 1 | tf_op jit(solution)/shard_map/norm_back/pallas_call | solution.py:496
  253.8 3.0 collective-permute-done.33.side_ref
  261.3 6.3 %norm_back.3 = (f32[512,2048]{1,0:T(8,128)}, f32[16,2048]{1,0:T(8,128)}) custom-call(bf16[512,2048]{1,0:T(8,128)(2,1)} %get-tuple-element.168.home_ref, bf16[512,2048]{1,0:T(8,128)(2,1)} %collective-permute-done.28.back_ref, bf16[256,2048]{1,0:T(8,128)(2,1)} %collective-permute-done.33.side_ref, ...), custom_call_target="tpu_custom_call", output_to_operand_aliasing={{0}: (8, {})} | custom-call | flops 1 | bytes 1 | tf_op jit(solution)/shard_map/norm_back/pallas_call | solution.py:496
  271.8 4.9 %collective-permute-done.42.refs_4_ = bf16[3,32,2048]{2,1,0:T(8,128)(2,1)} collective-permute-done((bf16[3,32,2048]{2,1,0:T(8,128)(2,1)}, bf16[3,32,2048]{2,1,0:T(8,128)(2,1)}, u32[]{:S(2)}, u32[]{:S(2)}) %collective-permute-start.42) | collective-permute-done | bytes 393248 | tf_op jit(solution)/shard_map/ppermute | solution.py:578
  277.9 3.0 collective-permute-done.41.refs_1_
  290.6 2.8 collective-permute-done.47.refs_6_
  294.7 3.1 collective-permute-done.46.refs_3_
  300.4 6.4 %collective-permute-done.51 = f32[4,2048]{1,0:T(4,128)S(1)} collective-permute-done((f32[4,2048]{1,0:T(4,128)S(1)}, f32[4,2048]{1,0:T(4,128)S(1)}, u32[]{:S(2)}, u32[]{:S(2)}) %collective-permute-start.51) | collective-permute-done | bytes 32800 | tf_op jit(solution)/shard_map/ppermute | solution.py:852
  309.0 4.3 %collective-permute-done.53 = f32[4,2048]{1,0:T(4,128)S(1)} collective-permute-done((f32[4,2048]{1,0:T(4,128)S(1)}, f32[4,2048]{1,0:T(4,128)S(1)}, u32[]{:S(2)}, u32[]{:S(2)}) %collective-permute-start.53) | collective-permute-done | bytes 32800 | tf_op jit(solution)/shard_map/ppermute | solution.py:852
  318.6 5.6 %place.2.refs_8_ = f32[3,16,32,2048]{3,2,1,0:T(8,128)} custom-call(s32[11]{0:T(128)} %pad_add_fusion.1.sc, bf16[3,32,2048]{2,1,0:T(8,128)(2,1)} %copy-done.12, bf16[3,32,2048]{2,1,0:T(8,128)(2,1)} %collective-permute-done.31.refs_1_, bf16[3,32,2048]{2,1,0:T(8,128)(2,1)} %collective-permute-done.36.refs_2_, ...), custom_call_target="tpu_custom_call" | custom-call | flops 1 | bytes 1 | tf_op jit(solution)/shard_map/place/pallas_call | solution.py:621
  326.0 5.5 %output.1 = bf16[512,2048]{1,0:T(8,128)(2,1)} custom-call(s32[10]{0:T(128)} %pad_add_fusion.sc, bf16[512,2048]{1,0:T(8,128)(2,1)} %x_ref.6, bf16[2,512,512]{2,1,0:T(8,128)(2,1)} %get-tuple-element.149.own_ref, bf16[2,512,512]{2,1,0:T(8,128)(2,1)} %copy-done.6, bf16[2,512,512]{2,1,0:T(8,128)(2,1)} %collective-permute-done.43.side_ref), custom_call_target="tpu_custom_call" | custom-call | flops 1 | bytes 1 | tf_op jit(solution)/shard_map/output/pallas_call | solution.py:537
  333.5 5.6 %place.3 = f32[3,16,32,2048]{3,2,1,0:T(8,128)} custom-call(s32[11]{0:T(128)} %pad_add_fusion.1.sc, bf16[3,32,2048]{2,1,0:T(8,128)(2,1)} %copy-done.13, bf16[3,32,2048]{2,1,0:T(8,128)(2,1)} %collective-permute-done.41.refs_1_, bf16[3,32,2048]{2,1,0:T(8,128)(2,1)} %collective-permute-done.44.refs_2_, ...), custom_call_target="tpu_custom_call", output_to_operand_aliasing={{}: (9, {})} | custom-call | flops 1 | bytes 1 | tf_op jit(solution)/shard_map/place/pallas_call | solution.py:621
  (247 shorter events, 125.3 us)
Async XLA Ops:
  11.2 18.7 %collective-permute-start.2 = (bf16[512,2048]{1,0:T(8,128)(2,1)}, bf16[512,2048]{1,0:T(8,128)(2,1)}, u32[]{:S(2)}, u32[]{:S(2)}) collective-permute-start(bf16[512,2048]{1,0:T(8,128)(2,1)} %slice.204), channel_id=1, source_target_pairs={{0,1},{1,0},{2,3},{3,2},{4,5},{5,4},{6,7},{7,6},{8,9},{9,8},{10,11... | collective-permute-start | bytes 6291464 | tf_op jit(solution)/shard_map/ppermute | solution.py:31
  11.7 19.8 %collective-permute-start.1 = (bf16[512,2048]{1,0:T(8,128)(2,1)}, bf16[512,2048]{1,0:T(8,128)(2,1)}, u32[]{:S(2)}, u32[]{:S(2)}) collective-permute-start(bf16[512,2048]{1,0:T(8,128)(2,1)} %get-tuple-element.118.n0_ref.c0_ref), channel_id=1, source_target_pairs={{0,1},{1,0},{2,3},{3,2},{4,5},{5,4},{6,7},{7,6},{8,9},{9,8},{10,11... | collective-permute-start | bytes 6291464 | tf_op jit(solution)/shard_map/ppermute | solution.py:31
  11.8 15.7 %collective-permute-start.3 = (bf16[128,2048]{1,0:T(8,128)(2,1)S(1)}, bf16[128,2048]{1,0:T(8,128)(2,1)S(1)}, u32[]{:S(2)}, u32[]{:S(2)}) collective-permute-start(bf16[128,2048]{1,0:T(8,128)(2,1)S(1)} %constant_dynamic-slice_fusion.8), channel_id=1, source_target_pairs={{0,2},{1,3},{2,0},{3,1},{4,6},{5,7},{6,4},{7,5},{8,10},{9,11},{10,... | collective-permute-start | bytes 1572872 | tf_op jit(solution)/shard_map/ppermute | solution.py:31
  14.7 63.3 %collective-permute-start.10 = (bf16[512,2048]{1,0:T(8,128)(2,1)}, bf16[512,2048]{1,0:T(8,128)(2,1)}, u32[]{:S(2)}, u32[]{:S(2)}) collective-permute-start(bf16[512,2048]{1,0:T(8,128)(2,1)} %get-tuple-element.118.n0_ref.c0_ref), channel_id=1, source_target_pairs={{0,2},{1,3},{2,0},{3,1},{4,6},{5,7},{6,4},{7,5},{8,10},{9,11},{10,... | collective-permute-start | bytes 6291464 | tf_op jit(solution)/shard_map/ppermute | solution.py:31
  18.9 34.4 %collective-permute-start.7 = (bf16[512,512]{1,0:T(8,128)(2,1)}, bf16[512,512]{1,0:T(8,128)(2,1)}, u32[]{:S(2)}, u32[]{:S(2)}) collective-permute-start(bf16[512,512]{1,0:T(8,128)(2,1)} %get-tuple-element.226), channel_id=1, source_target_pairs={{0,1},{1,0},{2,3},{3,2},{4,5},{5,4},{6,7},{7,6},{8,9},{9,8},{10,11... | collective-permute-start | bytes 1572872 | tf_op jit(solution)/shard_map/ppermute | solution.py:31
  27.5 13.3 %collective-permute-start.4 = (bf16[128,2048]{1,0:T(8,128)(2,1)S(1)}, bf16[128,2048]{1,0:T(8,128)(2,1)S(1)}, u32[]{:S(2)}, u32[]{:S(2)}) collective-permute-start(bf16[128,2048]{1,0:T(8,128)(2,1)S(1)} %collective-permute-done.3), channel_id=1, source_target_pairs={{0,8},{4,12},{8,0},{12,4},{16,24},{20,28},{24,16},{28,20},{1,9},{5... | collective-permute-start | bytes 1572872 | tf_op jit(solution)/shard_map/ppermute | solution.py:677
  29.9 22.1 %collective-permute-start.5 = (bf16[128,2048]{1,0:T(8,128)(2,1)S(1)}, bf16[128,2048]{1,0:T(8,128)(2,1)}, u32[]{:S(2)}, u32[]{:S(2)}) collective-permute-start(bf16[128,2048]{1,0:T(8,128)(2,1)S(1)} %collective-permute-done.3), channel_id=1, source_target_pairs={{0,4},{4,0},{8,12},{12,8},{16,20},{20,16},{24,28},{28,24},{1,5},{5... | collective-permute-start | bytes 1572872 | tf_op jit(solution)/shard_map/ppermute | solution.py:676
  40.8 12.3 %collective-permute-start.6 = (bf16[128,2048]{1,0:T(8,128)(2,1)S(1)}, bf16[128,2048]{1,0:T(8,128)(2,1)S(1)}, u32[]{:S(2)}, u32[]{:S(2)}) collective-permute-start(bf16[128,2048]{1,0:T(8,128)(2,1)S(1)} %collective-permute-done.3), channel_id=1, source_target_pairs={{0,12},{4,8},{8,4},{12,0},{16,28},{20,24},{24,20},{28,16},{1,13},{... | collective-permute-start | bytes 1572872 | tf_op jit(solution)/shard_map/ppermute | solution.py:719
  78.0 11.8 %collective-permute-start.11 = (bf16[512,2048]{1,0:T(8,128)(2,1)}, bf16[512,2048]{1,0:T(8,128)(2,1)S(1)}, u32[]{:S(2)}, u32[]{:S(2)}) collective-permute-start(bf16[512,2048]{1,0:T(8,128)(2,1)} %collective-permute-done.10.n_ref.c0_ref.n2_ref), channel_id=1, source_target_pairs={{0,1},{1,0},{2,3},{3,2},{4,5},{5,4},{6,7},{7,6},{8,9},{9,8},{10,11... | collective-permute-start | bytes 6291464 | tf_op jit(solution)/shard_map/ppermute | solution.py:31
  78.1 21.2 %collective-permute-start.12 = (bf16[512,512]{1,0:T(8,128)(2,1)}, bf16[512,512]{1,0:T(8,128)(2,1)S(1)}, u32[]{:S(2)}, u32[]{:S(2)}) collective-permute-start(bf16[512,512]{1,0:T(8,128)(2,1)} %get-tuple-element.128), channel_id=1, source_target_pairs={{0,2},{1,3},{2,0},{3,1},{4,6},{5,7},{6,4},{7,5},{8,10},{9,11},{10,... | collective-permute-start | bytes 1572872 | tf_op jit(solution)/shard_map/ppermute | solution.py:31
  78.9 24.4 %collective-permute-start.13 = (bf16[512,512]{1,0:T(8,128)(2,1)}, bf16[512,512]{1,0:T(8,128)(2,1)S(1)}, u32[]{:S(2)}, u32[]{:S(2)}) collective-permute-start(bf16[512,512]{1,0:T(8,128)(2,1)} %get-tuple-element.129), channel_id=1, source_target_pairs={{0,3},{1,2},{2,1},{3,0},{4,7},{5,6},{6,5},{7,4},{8,11},{9,10},{10,... | collective-permute-start | bytes 1572872 | tf_op jit(solution)/shard_map/ppermute | solution.py:31
  134.7 13.5 %collective-permute-start.15 = (bf16[3,32,2048]{2,1,0:T(8,128)(2,1)S(1)}, bf16[3,32,2048]{2,1,0:T(8,128)(2,1)S(1)}, u32[]{:S(2)}, u32[]{:S(2)}) collective-permute-start(bf16[3,32,2048]{2,1,0:T(8,128)(2,1)S(1)} %fusion.13), channel_id=1, source_target_pairs={{0,8},{1,5},{2,10},{3,7},{8,16},{9,1},{10,18},{11,3},{16,24},{17,9... | collective-permute-start | bytes 1179656 | tf_op jit(solution)/shard_map/ppermute | solution.py:578
  148.1 23.4 %collective-permute-start.17 = (bf16[512,2048]{1,0:T(8,128)(2,1)}, bf16[512,2048]{1,0:T(8,128)(2,1)}, u32[]{:S(2)}, u32[]{:S(2)}) collective-permute-start(bf16[512,2048]{1,0:T(8,128)(2,1)} %get-tuple-element.142), channel_id=1, source_target_pairs={{0,1},{1,0},{2,3},{3,2},{4,5},{5,4},{6,7},{7,6},{8,9},{9,8},{10,11... | collective-permute-start | bytes 6291464 | tf_op jit(solution)/shard_map/ppermute | solution.py:31
  149.2 16.6 %collective-permute-start.16 = (bf16[3,32,2048]{2,1,0:T(8,128)(2,1)S(1)}, bf16[3,32,2048]{2,1,0:T(8,128)(2,1)S(1)}, u32[]{:S(2)}, u32[]{:S(2)}) collective-permute-start(bf16[3,32,2048]{2,1,0:T(8,128)(2,1)S(1)} %fusion.12), channel_id=1, source_target_pairs={{0,8},{1,5},{2,10},{3,7},{8,16},{9,1},{10,18},{11,3},{16,24},{17,9... | collective-permute-start | bytes 1179656 | tf_op jit(solution)/shard_map/ppermute | solution.py:578
  168.1 14.0 %collective-permute-start.19 = (bf16[3,32,2048]{2,1,0:T(8,128)(2,1)S(1)}, bf16[3,32,2048]{2,1,0:T(8,128)(2,1)S(1)}, u32[]{:S(2)}, u32[]{:S(2)}) collective-permute-start(bf16[3,32,2048]{2,1,0:T(8,128)(2,1)S(1)} %slice_bitcast_fusion.8), channel_id=1, source_target_pairs={{0,8},{1,5},{2,10},{3,7},{8,16},{9,1},{10,18},{11,3},{16,24},{17,9... | collective-permute-start | bytes 1179656 | tf_op jit(solution)/shard_map/ppermute | solution.py:578
  169.9 10.2 %collective-permute-start.20 = (bf16[3,32,2048]{2,1,0:T(8,128)(2,1)S(1)}, bf16[3,32,2048]{2,1,0:T(8,128)(2,1)S(1)}, u32[]{:S(2)}, u32[]{:S(2)}) collective-permute-start(bf16[3,32,2048]{2,1,0:T(8,128)(2,1)S(1)} %fusion.11), channel_id=1, source_target_pairs={{0,8},{1,5},{2,10},{3,7},{8,16},{9,1},{10,18},{11,3},{16,24},{17,9... | collective-permute-start | bytes 1179656 | tf_op jit(solution)/shard_map/ppermute | solution.py:578
  173.3 29.4 %collective-permute-start.27 = (bf16[256,2048]{1,0:T(8,128)(2,1)S(1)}, bf16[256,2048]{1,0:T(8,128)(2,1)S(1)}, u32[]{:S(2)}, u32[]{:S(2)}) collective-permute-start(bf16[256,2048]{1,0:T(8,128)(2,1)S(1)} %add_convert_fusion.1), channel_id=1, source_target_pairs={{0,2},{1,3},{2,0},{3,1},{4,6},{5,7},{6,4},{7,5},{8,10},{9,11},{10,... | collective-permute-start | bytes 3145736 | tf_op jit(solution)/shard_map/ppermute | solution.py:31
  221.6 18.2 %collective-permute-start.28 = (bf16[512,2048]{1,0:T(8,128)(2,1)}, bf16[512,2048]{1,0:T(8,128)(2,1)}, u32[]{:S(2)}, u32[]{:S(2)}) collective-permute-start(bf16[512,2048]{1,0:T(8,128)(2,1)} %get-tuple-element.169), channel_id=1, source_target_pairs={{0,1},{1,0},{2,3},{3,2},{4,5},{5,4},{6,7},{7,6},{8,9},{9,8},{10,11... | collective-permute-start | bytes 6291464 | tf_op jit(solution)/shard_map/ppermute | solution.py:31
  221.7 10.2 %collective-permute-start.32 = (bf16[3,32,2048]{2,1,0:T(8,128)(2,1)}, bf16[3,32,2048]{2,1,0:T(8,128)(2,1)S(1)}, u32[]{:S(2)}, u32[]{:S(2)}) collective-permute-start(bf16[3,32,2048]{2,1,0:T(8,128)(2,1)} %fusion.3), channel_id=1, source_target_pairs={{0,8},{1,5},{2,10},{3,7},{8,16},{9,1},{10,18},{11,3},{16,24},{17,9... | collective-permute-start | bytes 1179656 | tf_op jit(solution)/shard_map/ppermute | solution.py:578
  232.1 14.0 %collective-permute-start.34 = (bf16[3,32,2048]{2,1,0:T(8,128)(2,1)S(1)}, bf16[3,32,2048]{2,1,0:T(8,128)(2,1)}, u32[]{:S(2)}, u32[]{:S(2)}) collective-permute-start(bf16[3,32,2048]{2,1,0:T(8,128)(2,1)S(1)} %fusion.2), channel_id=1, source_target_pairs={{0,8},{1,5},{2,10},{3,7},{8,16},{9,1},{10,18},{11,3},{16,24},{17,9... | collective-permute-start | bytes 1179656 | tf_op jit(solution)/shard_map/ppermute | solution.py:578
  233.9 23.0 %collective-permute-start.33 = (bf16[256,2048]{1,0:T(8,128)(2,1)}, bf16[256,2048]{1,0:T(8,128)(2,1)}, u32[]{:S(2)}, u32[]{:S(2)}) collective-permute-start(bf16[256,2048]{1,0:T(8,128)(2,1)} %add_convert_fusion), channel_id=1, source_target_pairs={{0,2},{1,3},{2,0},{3,1},{4,6},{5,7},{6,4},{7,5},{8,10},{9,11},{10,... | collective-permute-start | bytes 3145736 | tf_op jit(solution)/shard_map/ppermute | solution.py:31
  238.3 18.6 %collective-permute-start.36 = (bf16[3,32,2048]{2,1,0:T(8,128)(2,1)}, bf16[3,32,2048]{2,1,0:T(8,128)(2,1)}, u32[]{:S(2)}, u32[]{:S(2)}) collective-permute-start(bf16[3,32,2048]{2,1,0:T(8,128)(2,1)} %collective-permute-done.31.refs_1_), channel_id=1, source_target_pairs={{0,8},{1,5},{2,10},{3,7},{8,16},{9,1},{10,18},{11,3},{16,24},{17,9... | collective-permute-start | bytes 1179656 | tf_op jit(solution)/shard_map/ppermute | solution.py:578
  247.2 11.1 %collective-permute-start.35 = (bf16[3,32,2048]{2,1,0:T(8,128)(2,1)S(1)}, bf16[3,32,2048]{2,1,0:T(8,128)(2,1)}, u32[]{:S(2)}, u32[]{:S(2)}) collective-permute-start(bf16[3,32,2048]{2,1,0:T(8,128)(2,1)S(1)} %fusion.1), channel_id=1, source_target_pairs={{0,8},{1,5},{2,10},{3,7},{8,16},{9,1},{10,18},{11,3},{16,24},{17,9... | collective-permute-start | bytes 1179656 | tf_op jit(solution)/shard_map/ppermute | solution.py:578
  256.8 11.7 %collective-permute-start.37 = (bf16[3,32,2048]{2,1,0:T(8,128)(2,1)}, bf16[3,32,2048]{2,1,0:T(8,128)(2,1)}, u32[]{:S(2)}, u32[]{:S(2)}) collective-permute-start(bf16[3,32,2048]{2,1,0:T(8,128)(2,1)} %collective-permute-done.36.refs_2_), channel_id=1, source_target_pairs={{0,8},{1,5},{2,10},{3,7},{8,16},{9,1},{10,18},{11,3},{16,24},{17,9... | collective-permute-start | bytes 1179656 | tf_op jit(solution)/shard_map/ppermute | solution.py:578
  259.4 10.4 %collective-permute-start.38 = (bf16[32,2048]{1,0:T(8,128)(2,1)S(1)}, bf16[32,2048]{1,0:T(8,128)(2,1)S(1)}, u32[]{:S(2)}, u32[]{:S(2)}) collective-permute-start(bf16[32,2048]{1,0:T(8,128)(2,1)S(1)} %get-tuple-element.234), channel_id=1, source_target_pairs={{0,1},{1,0},{2,3},{3,2},{4,5},{5,4},{6,7},{7,6},{8,9},{9,8},{10,11... | collective-permute-start | bytes 393224 | tf_op jit(solution)/shard_map/ppermute | solution.py:31
  259.5 10.4 %collective-permute-start.39 = (bf16[32,2048]{1,0:T(8,128)(2,1)S(1)}, bf16[32,2048]{1,0:T(8,128)(2,1)S(1)}, u32[]{:S(2)}, u32[]{:S(2)}) collective-permute-start(bf16[32,2048]{1,0:T(8,128)(2,1)S(1)} %get-tuple-element.235), channel_id=1, source_target_pairs={{0,2},{1,3},{2,0},{3,1},{4,6},{5,7},{6,4},{7,5},{8,10},{9,11},{10,... | collective-permute-start | bytes 393224 | tf_op jit(solution)/shard_map/ppermute | solution.py:31
  261.1 23.3 %collective-permute-start.18 = (bf16[2,512,512]{2,1,0:T(8,128)(2,1)}, bf16[2,512,512]{2,1,0:T(8,128)(2,1)S(1)}, u32[]{:S(2)}, u32[]{:S(2)}) collective-permute-start(bf16[2,512,512]{2,1,0:T(8,128)(2,1)} %pad_maximum_fusion), channel_id=1, source_target_pairs={{0,1},{1,0},{2,3},{3,2},{4,5},{5,4},{6,7},{7,6},{8,9},{9,8},{10,11... | collective-permute-start | bytes 3145736 | tf_op jit(solution)/shard_map/ppermute | solution.py:31
  269.9 11.0 %collective-permute-start.41 = (bf16[3,32,2048]{2,1,0:T(8,128)(2,1)S(1)}, bf16[3,32,2048]{2,1,0:T(8,128)(2,1)}, u32[]{:S(2)}, u32[]{:S(2)}) collective-permute-start(bf16[3,32,2048]{2,1,0:T(8,128)(2,1)S(1)} %pad_maximum_fusion.3.refs_0_), channel_id=1, source_target_pairs={{0,8},{1,5},{2,10},{3,7},{8,16},{9,1},{10,18},{11,3},{16,24},{17,9... | collective-permute-start | bytes 1179656 | tf_op jit(solution)/shard_map/ppermute | solution.py:578
  271.6 10.5 %collective-permute-start.40 = (f32[8,2048]{1,0:T(8,128)S(1)}, f32[8,2048]{1,0:T(8,128)S(1)}, u32[]{:S(2)}, u32[]{:S(2)}) collective-permute-start(f32[8,2048]{1,0:T(8,128)S(1)} %pad_maximum_fusion.5), channel_id=1, source_target_pairs={{0,1},{1,0},{2,3},{3,2},{4,5},{5,4},{6,7},{7,6},{8,9},{9,8},{10,11... | collective-permute-start | bytes 196616 | tf_op jit(solution)/shard_map/ppermute | solution.py:31
  284.5 24.5 %collective-permute-start.43 = (bf16[2,512,512]{2,1,0:T(8,128)(2,1)S(1)}, bf16[2,512,512]{2,1,0:T(8,128)(2,1)}, u32[]{:S(2)}, u32[]{:S(2)}) collective-permute-start(bf16[2,512,512]{2,1,0:T(8,128)(2,1)S(1)} %pad_maximum_fusion.1), channel_id=1, source_target_pairs={{0,2},{1,3},{2,0},{3,1},{4,6},{5,7},{6,4},{7,5},{8,10},{9,11},{10,... | collective-permute-start | bytes 3145736 | tf_op jit(solution)/shard_map/ppermute | solution.py:31
  293.4 13.4 %collective-permute-start.50 = (bf16[3,32,2048]{2,1,0:T(8,128)(2,1)S(1)}, bf16[3,32,2048]{2,1,0:T(8,128)(2,1)S(1)}, u32[]{:S(2)}, u32[]{:S(2)}) collective-permute-start(bf16[3,32,2048]{2,1,0:T(8,128)(2,1)S(1)} %collective-permute-done.47.refs_6_), channel_id=1, source_target_pairs={{0,8},{1,5},{2,10},{3,7},{8,16},{9,1},{10,18},{11,3},{16,24},{17,9... | collective-permute-start | bytes 1179656 | tf_op jit(solution)/shard_map/ppermute | solution.py:578
  313.3 18.2 %collective-permute-start.56 = (f32[4,2048]{1,0:T(4,128)S(1)}, f32[4,2048]{1,0:T(4,128)S(1)}, u32[]{:S(2)}, u32[]{:S(2)}) collective-permute-start(f32[4,2048]{1,0:T(4,128)S(1)} %add.183), channel_id=1, source_target_pairs={{0,16},{4,20},{8,24},{12,28},{16,0},{20,4},{24,8},{28,12},{1,17},{... | collective-permute-start | bytes 98312 | tf_op jit(solution)/shard_map/ppermute | solution.py:852
  (56 other events, 537.3 us)

commit v4 on v3

--- a/solution.py
+++ b/solution.py
@@ -369,11 +369,9 @@
 
 
 def weight_kernel(sc, near_ref, far_ref, n0_ref, n1_ref, n2_ref, n3_ref, out_ref):
-    total = None
-    sgs = (near_ref.at[0, 0], near_ref.at[1, 0], far_ref.at[0, 0], far_ref.at[1, 0])
-    for sg, n_ref in zip(sgs, (n0_ref, n1_ref, n2_ref, n3_ref)):
-        part = lax.dot_general(sg[...], n_ref[...], (((0,), (0,)), ((), ())), preferred_element_type=F32)
-        total = part if total is None else total + part
+    sg = jnp.concatenate([near_ref[0, 0], near_ref[1, 0], far_ref[0, 0], far_ref[1, 0]], axis=0)
+    n = jnp.concatenate([n0_ref[...], n1_ref[...], n2_ref[...], n3_ref[...]], axis=0)
+    total = lax.dot_general(sg, n, (((0,), (0,)), ((), ())), preferred_element_type=F32)
     rows = out_ref.shape[2]
     for shard in range(RING):
         out_ref[sc[shard], 0] = total[shard * rows : (shard + 1) * rows].astype(BF)
@@ -405,24 +403,20 @@
 
 def input_near_kernel(sc, w0_ref, w1_ref, w2_ref, sg_ref, ex_ref, *out_refs):
     mine = (pl.program_id(0) == sc[0]).astype(F32)
+    w = jnp.concatenate([w0_ref[...], w1_ref[...], w2_ref[...]], axis=0)
     for b, out_ref in enumerate(out_refs):
-        total = ex_ref[b].astype(F32) * mine
-        for kind, w_ref in enumerate((w0_ref, w1_ref, w2_ref)):
-            total = total + jnp.dot(sg_ref[b, kind], w_ref[...], preferred_element_type=F32)
-        out_ref[...] = total.astype(BF)
+        sg = jnp.concatenate([sg_ref[b, kind] for kind in range(3)], axis=1)
+        total = jnp.dot(sg, w, preferred_element_type=F32)
+        out_ref[...] = (total + ex_ref[b].astype(F32) * mine).astype(BF)
 
 
 def input_far_kernel(sc, w0_ref, w1_ref, w2_ref, sg0_ref, sg1_ref, ex0_ref, ex1_ref, *out_refs):
-    w_refs = (w0_ref, w1_ref, w2_ref)
+    w = jnp.concatenate([w0_ref[...], w1_ref[...], w2_ref[...]], axis=0)
     mine = (pl.program_id(0) == sc[0]).astype(F32)
     tile = sg0_ref.shape[3]
     for b, out_ref in enumerate(out_refs):
-        total = None
-        for h, sg_ref in enumerate((sg0_ref, sg1_ref)):
-            for kind in range(3):
-                w = w_refs[kind][h * tile : (h + 1) * tile, :]
-                part = jnp.dot(sg_ref[b, kind], w, preferred_element_type=F32)
-                total = part if total is None else total + part
+        sg = jnp.concatenate([ref[b, kind] for kind in range(3) for ref in (sg0_ref, sg1_ref)], axis=1)
+        total = jnp.dot(sg, w, preferred_element_type=F32)
         for h, ex_ref in enumerate((ex0_ref, ex1_ref)):
             cols = slice(h * tile, (h + 1) * tile)
             out_ref[:, cols] = (total[:, cols] + ex_ref[b].astype(F32) * mine).astype(BF)
@@ -679,9 +673,10 @@
         w_send = lax.dynamic_slice_in_dim(weight, x_at * own, own, axis=0)
         w_part = swap(w_send, XSIDE)
     norm_own, mean, rstd = run_norm(after(inputs, w_send), ln_gain[None], ln_bias[None])
+    norm_own = after(norm_own, w_part)
     norm_core = swap(norm_own, CORE)
     norm_side = swap(norm_own, XSIDE)
-    w_core = swap(after(weight, norm_own)[own : 2 * own], CORE)
+    w_core = swap(after(weight, w_send)[own : 2 * own], CORE)
 
     def columns(value, index, start=0, width=own):
         return lax.dynamic_slice_in_dim(value, index * own + start, width, axis=1)
@@ -726,7 +721,8 @@
     near = run_near(
         near_scal, early, w_x, (norm_own, norm_core), (og_own, og_core), near_starts, gate_bias
     )
-    far_scal, far_starts = tables([swap(after(small, near[0]), by) for by in (XSIDE, DIAG)])
+    far_small = [swap(after(small, early), by) for by in (XSIDE, DIAG)]
+    far_scal, far_starts = tables(after(far_small, near[0]))
     og_far = [swap(after(sent, early), by) for sent, by in zip(og_send, (XSIDE, DIAG))]
     norm_side = after(norm_side, (near[0], far_scal))
     norm_diag = swap(norm_side, CORE)

time: 341 us -> 335 us (0.982)
  waiting for transfers between devices: 84.3 us -> 80.6 us
    ppermute x23, waiting for transfers between devices: 23.5 us -> 18.6 us  [swap(): return lax.ppermute(value, 'tp', [(t, t ^ by) for t in range(TP)])]
  transfers between devices with their start and end apart: 57 -> 57, of which waited for: 26 -> 21; matrix products, arithmetic and copies ran while one was open for 10% -> 11% of each run, Pallas kernels for 29% -> 31%
where the time goes in v4:
time: 335 us; the launch traced here: 333 us
  Pallas kernels  142 us (42%)
  waiting for transfers between devices  80.6 us (24%)
  starting transfers between devices  62.8 us (19%)
  local copies, waits for them, and re-layouts  25.9 us (8%)
  other arithmetic  21.2 us (6%)
    ppermute x28, starting transfers between devices, around(): return lax.ppermute(value, ('dp', 'tp'), pairs)  39.7 us
    ppermute x28, waiting for transfers between devices, around(): return lax.ppermute(value, ('dp', 'tp'), pairs)  38.1 us
    pallas_call x2, Pallas kernels, run_weight(): pl.pallas_call(weight_kernel, name='weight_grad', grid_spec=pltpu.Prefetc...  27.2 us
    pallas_call x2, Pallas kernels, run_input(): pl.pallas_call(kernel, name=name, grid_spec=pltpu.PrefetchScalarGridSpec(...  23.4 us
    ppermute x23, waiting for transfers between devices, swap(): return lax.ppermute(value, 'tp', [(t, t ^ by) for t in range(TP)])  18.6 us
    pallas_call x1, Pallas kernels, run_near(): pl.pallas_call(near_kernel, name='near', grid_spec=pltpu.PrefetchScalarGr...  16.7 us
    pallas_call x2, Pallas kernels, run_project(): pl.pallas_call(project_kernel, name='project', grid_spec=pltpu.PrefetchSc...  16.3 us
    ppermute x23, starting transfers between devices, swap(): return lax.ppermute(value, 'tp', [(t, t ^ by) for t in range(TP)])  15.1 us
  transfers between devices with their start and end apart: 57, of which 21 were waited for; matrix products, arithmetic and copies ran while one was open for 11% of the time, Pallas kernels for 31%

profile of v4, /device:TPU:0, one launch (start us, length us, event | category | flops | bytes accessed | tf_op | source)
XLA Modules:
  0.0 333.4 jit_solution(682929807222600102)
XLA Ops:
  1.8 3.0 collective-permute-start
  4.8 3.2 slice.204
  8.0 6.3 %norm.1 = (bf16[512,2048]{1,0:T(8,128)(2,1)}, f32[512,128]{1,0:T(8,128)}, f32[512,128]{1,0:T(8,128)}) custom-call(bf16[512,2048]{1,0:T(8,128)(2,1)} %x_ref.6, f32[1,2048]{1,0:T(1,128)} %bitcast.138, f32[1,2048]{1,0:T(1,128)} %bitcast.141), custom_call_target="tpu_custom_call" | custom-call | flops 1 | bytes 1 | tf_op jit(solution)/shard_map/norm/pallas_call | solution.py:55
  27.3 9.3 %early.1.e_ref = bf16[2,2,512,512]{3,2,1,0:T(8,128)(2,1)} custom-call(s32[10]{0:T(128)} %pad_add_fusion.sc, bf16[512,2048]{1,0:T(8,128)(2,1)} %get-tuple-element.122.n0_ref.c0_ref, bf16[512,2048]{1,0:T(8,128)(2,1)} %collective-permute-done.2.n1_ref.c1_ref, bf16[1536,2048]{1,0:T(8,128)(2,1)} %w0_ref.9, bf16[512,2048]{1,0:T(8,128)(2,1)} %collective-permute-done.3.w1_ref), custom_call_target="tpu_custom_call" | custom-call | flops 4294967296 | bytes 8388608 | tf_op jit(solution)/shard_map/early/pallas_call | solution.py:84
  37.1 13.3 %collective-permute-done.5 = bf16[128,2048]{1,0:T(8,128)(2,1)} collective-permute-done((bf16[128,2048]{1,0:T(8,128)(2,1)S(1)}, bf16[128,2048]{1,0:T(8,128)(2,1)}, u32[]{:S(2)}, u32[]{:S(2)}) %collective-permute-start.5) | collective-permute-done | bytes 524320 | tf_op jit(solution)/shard_map/ppermute | solution.py:670
  53.6 16.7 %near.1 = (bf16[2,512,512]{2,1,0:T(8,128)(2,1)}, bf16[2,3,512,512]{3,2,1,0:T(8,128)(2,1)}, bf16[2,512,512]{2,1,0:T(8,128)(2,1)}, f32[2,8,512]{2,1,0:T(8,128)}, f32[2,8,512]{2,1,0:T(8,128)}) custom-call(s32[20]{0:T(128)} %concatenate.61.sc, bf16[2,2,512,512]{3,2,1,0:T(8,128)(2,1)} %early.1.e_ref, bf16[512,2048]{1,0:T(8,128)(2,1)} %bitcast.128, ...), custom_call_target="tpu_custom_call" | custom-call | flops 1 | bytes 1 | tf_op jit(solution)/shard_map/near/pallas_call | solution.py:311
  74.3 8.1 %project.2.s0_ref = bf16[3,512,512]{2,1,0:T(8,128)(2,1)} custom-call(s32[10]{0:T(128)} %pad_add_fusion.sc, bf16[512,2048]{1,0:T(8,128)(2,1)} %collective-permute-done.10.n_ref.c0_ref.n2_ref, bf16[1536,2048]{1,0:T(8,128)(2,1)} %w0_ref.9, bf16[512,2048]{1,0:T(8,128)(2,1)} %collective-permute-done.3.w1_ref, bf16[512,2048]{1,0:T(8,128)(2,1)} %bitcast.129), custom_call_target="tpu_custom_call" | custom-call | flops 1 | bytes 1 | tf_op jit(solution)/shard_map/project/pallas_call | solution.py:114
  84.3 8.2 %project.3.s1_ref = bf16[3,512,512]{2,1,0:T(8,128)(2,1)} custom-call(s32[10]{0:T(128)} %pad_add_fusion.sc, bf16[512,2048]{1,0:T(8,128)(2,1)} %copy-done.1, bf16[1536,2048]{1,0:T(8,128)(2,1)} %w0_ref.9, bf16[512,2048]{1,0:T(8,128)(2,1)} %collective-permute-done.3.w1_ref, bf16[512,2048]{1,0:T(8,128)(2,1)} %bitcast.130), custom_call_target="tpu_custom_call" | custom-call | flops 1 | bytes 1 | tf_op jit(solution)/shard_map/project/pallas_call | solution.py:114
  92.5 4.2 %collective-permute-done.13.og1_ref = bf16[512,512]{1,0:T(8,128)(2,1)S(1)} collective-permute-done((bf16[512,512]{1,0:T(8,128)(2,1)}, bf16[512,512]{1,0:T(8,128)(2,1)S(1)}, u32[]{:S(2)}, u32[]{:S(2)}) %collective-permute-start.13) | collective-permute-done | bytes 524320 | tf_op jit(solution)/shard_map/ppermute | solution.py:31
  97.5 6.7 %far.2 = (bf16[2,512,256]{2,1,0:T(8,128)(2,1)}, bf16[2,3,512,256]{3,2,1,0:T(8,128)(2,1)}, bf16[2,512,256]{2,1,0:T(8,128)(2,1)}, f32[2,8,256]{2,1,0:T(8,128)}, f32[2,8,256]{2,1,0:T(8,128)}) custom-call(s32[20]{0:T(128)} %concatenate.62.sc, bf16[3,512,512]{2,1,0:T(8,128)(2,1)} %project.2.s0_ref, bf16[3,512,512]{2,1,0:T(8,128)(2,1)} %project.3.s1_ref, ...), custom_call_target="tpu_custom_call" | custom-call | flops 1 | bytes 1 | tf_op jit(solution)/shard_map/far/pallas_call | solution.py:346
  104.2 13.5 %weight_grad.2 = bf16[8,3,32,2048]{3,2,1,0:T(8,128)(2,1)} custom-call(s32[8]{0:T(128)} %and_select_fusion.1.sc, bf16[2,3,512,512]{3,2,1,0:T(8,128)(2,1)} %get-tuple-element.137.near_ref.sg_ref, bf16[2,3,512,256]{3,2,1,0:T(8,128)(2,1)} %get-tuple-element.138.far_ref.sg0_ref, bf16[512,2048]{1,0:T(8,128)(2,1)} %get-tuple-element.122.n0_ref.c0_ref, ...), custom_call_target="tpu_custom_call" | custom-call | flops 1 | bytes 1 | tf_op jit(solution)/shard_map/weight_grad/pallas_call | solution.py:386
  119.3 6.6 %far.3 = (bf16[2,512,256]{2,1,0:T(8,128)(2,1)}, bf16[2,3,512,256]{3,2,1,0:T(8,128)(2,1)}, bf16[2,512,256]{2,1,0:T(8,128)(2,1)}, f32[2,8,256]{2,1,0:T(8,128)}, f32[2,8,256]{2,1,0:T(8,128)}) custom-call(s32[20]{0:T(128)} %concatenate.62.sc, bf16[3,512,512]{2,1,0:T(8,128)(2,1)} %project.2.s0_ref, bf16[3,512,512]{2,1,0:T(8,128)(2,1)} %project.3.s1_ref, ...), custom_call_target="tpu_custom_call" | custom-call | flops 1 | bytes 1 | tf_op jit(solution)/shard_map/far/pallas_call | solution.py:346
  129.9 11.7 %input_far.1 = (bf16[512,2048]{1,0:T(8,128)(2,1)}, bf16[512,2048]{1,0:T(8,128)(2,1)}) custom-call(s32[10]{0:T(128)} %pad_add_fusion.sc, bf16[1536,2048]{1,0:T(8,128)(2,1)} %w0_ref.9, bf16[512,2048]{1,0:T(8,128)(2,1)} %collective-permute-done.3.w1_ref, bf16[512,2048]{1,0:T(8,128)(2,1)} %bitcast.131, ...), custom_call_target="tpu_custom_call" | custom-call | flops 1 | bytes 1 | tf_op jit(solution)/shard_map/input_far/pallas_call | solution.py:431
  146.9 13.6 %weight_grad.3 = bf16[8,3,32,2048]{3,2,1,0:T(8,128)(2,1)} custom-call(s32[8]{0:T(128)} %and_select_fusion.1.sc, bf16[2,3,512,512]{3,2,1,0:T(8,128)(2,1)} %get-tuple-element.137.near_ref.sg_ref, bf16[2,3,512,256]{3,2,1,0:T(8,128)(2,1)} %get-tuple-element.150.sg1_ref.far_ref, bf16[512,2048]{1,0:T(8,128)(2,1)} %get-tuple-element.122.n0_ref.c0_ref, ...), custom_call_target="tpu_custom_call" | custom-call | flops 1 | bytes 1 | tf_op jit(solution)/shard_map/weight_grad/pallas_call | solution.py:386
  169.8 5.0 %collective-permute-done.20 = bf16[3,32,2048]{2,1,0:T(8,128)(2,1)S(1)} collective-permute-done((bf16[3,32,2048]{2,1,0:T(8,128)(2,1)S(1)}, bf16[3,32,2048]{2,1,0:T(8,128)(2,1)S(1)}, u32[]{:S(2)}, u32[]{:S(2)}) %collective-permute-start.20) | collective-permute-done | bytes 393248 | tf_op jit(solution)/shard_map/ppermute | solution.py:572
  178.1 4.6 %collective-permute-done.22 = bf16[3,32,2048]{2,1,0:T(8,128)(2,1)S(1)} collective-permute-done((bf16[3,32,2048]{2,1,0:T(8,128)(2,1)S(1)}, bf16[3,32,2048]{2,1,0:T(8,128)(2,1)S(1)}, u32[]{:S(2)}, u32[]{:S(2)}) %collective-permute-start.22) | collective-permute-done | bytes 393248 | tf_op jit(solution)/shard_map/ppermute | solution.py:572
  188.5 2.6 collective-permute-done.24
  192.7 2.6 collective-permute-done.23
  204.7 11.6 %input_near.1 = (bf16[512,2048]{1,0:T(8,128)(2,1)}, bf16[512,2048]{1,0:T(8,128)(2,1)}) custom-call(s32[10]{0:T(128)} %pad_add_fusion.sc, bf16[1536,2048]{1,0:T(8,128)(2,1)} %w0_ref.9, bf16[512,2048]{1,0:T(8,128)(2,1)} %collective-permute-done.3.w1_ref, bf16[512,2048]{1,0:T(8,128)(2,1)} %bitcast.132, ...), custom_call_target="tpu_custom_call" | custom-call | flops 1 | bytes 1 | tf_op jit(solution)/shard_map/input_near/pallas_call | solution.py:431
  221.0 3.5 %collective-permute-done.30 = bf16[32,2048]{1,0:T(8,128)(2,1)S(1)} collective-permute-done((bf16[32,2048]{1,0:T(8,128)(2,1)S(1)}, bf16[32,2048]{1,0:T(8,128)(2,1)S(1)}, u32[]{:S(2)}, u32[]{:S(2)}) %collective-permute-start.30) | collective-permute-done | bytes 131104 | tf_op jit(solution)/shard_map/ppermute | solution.py:31
  234.0 6.2 %norm_back.2 = (f32[512,2048]{1,0:T(8,128)}, f32[16,2048]{1,0:T(8,128)}) custom-call(bf16[512,2048]{1,0:T(8,128)(2,1)} %get-tuple-element.174.home_ref, bf16[512,2048]{1,0:T(8,128)(2,1)} %collective-permute-done.28.back_ref, bf16[256,2048]{1,0:T(8,128)(2,1)} %copy-done.16, bf16[512,2048]{1,0:T(8,128)(2,1)} %x_ref.6, f32[512,128]{1,0:T(8,128)} %get-tuple-element.180.mean_ref, ...), custom_call_target="tpu_custom_call" | custom-call | flops 1 | bytes 1 | tf_op jit(solution)/shard_map/norm_back/pallas_call | solution.py:490
  243.9 8.4 %collective-permute-done.33.side_ref = bf16[256,2048]{1,0:T(8,128)(2,1)} collective-permute-done((bf16[256,2048]{1,0:T(8,128)(2,1)}, bf16[256,2048]{1,0:T(8,128)(2,1)}, u32[]{:S(2)}, u32[]{:S(2)}) %collective-permute-start.33) | collective-permute-done | bytes 1048608 | tf_op jit(solution)/shard_map/ppermute | solution.py:31
  255.6 6.3 %norm_back.3 = (f32[512,2048]{1,0:T(8,128)}, f32[16,2048]{1,0:T(8,128)}) custom-call(bf16[512,2048]{1,0:T(8,128)(2,1)} %get-tuple-element.174.home_ref, bf16[512,2048]{1,0:T(8,128)(2,1)} %collective-permute-done.28.back_ref, bf16[256,2048]{1,0:T(8,128)(2,1)} %collective-permute-done.33.side_ref, ...), custom_call_target="tpu_custom_call", output_to_operand_aliasing={{0}: (8, {})} | custom-call | flops 1 | bytes 1 | tf_op jit(solution)/shard_map/norm_back/pallas_call | solution.py:490
  266.1 4.8 %collective-permute-done.42.refs_4_ = bf16[3,32,2048]{2,1,0:T(8,128)(2,1)} collective-permute-done((bf16[3,32,2048]{2,1,0:T(8,128)(2,1)}, bf16[3,32,2048]{2,1,0:T(8,128)(2,1)}, u32[]{:S(2)}, u32[]{:S(2)}) %collective-permute-start.42) | collective-permute-done | bytes 393248 | tf_op jit(solution)/shard_map/ppermute | solution.py:572
  272.2 2.9 collective-permute-done.41.refs_1_
  284.9 2.8 collective-permute-done.47.refs_6_
  289.0 3.0 collective-permute-done.46.refs_3_
  294.7 6.3 %collective-permute-done.51 = f32[4,2048]{1,0:T(4,128)S(1)} collective-permute-done((f32[4,2048]{1,0:T(4,128)S(1)}, f32[4,2048]{1,0:T(4,128)S(1)}, u32[]{:S(2)}, u32[]{:S(2)}) %collective-permute-start.51) | collective-permute-done | bytes 32800 | tf_op jit(solution)/shard_map/ppermute | solution.py:848
  303.3 4.3 %collective-permute-done.53 = f32[4,2048]{1,0:T(4,128)S(1)} collective-permute-done((f32[4,2048]{1,0:T(4,128)S(1)}, f32[4,2048]{1,0:T(4,128)S(1)}, u32[]{:S(2)}, u32[]{:S(2)}) %collective-permute-start.53) | collective-permute-done | bytes 32800 | tf_op jit(solution)/shard_map/ppermute | solution.py:848
  312.9 5.6 %place.2.refs_8_ = f32[3,16,32,2048]{3,2,1,0:T(8,128)} custom-call(s32[11]{0:T(128)} %pad_add_fusion.1.sc, bf16[3,32,2048]{2,1,0:T(8,128)(2,1)} %copy-done.12, bf16[3,32,2048]{2,1,0:T(8,128)(2,1)} %collective-permute-done.31.refs_1_, bf16[3,32,2048]{2,1,0:T(8,128)(2,1)} %collective-permute-done.36.refs_2_, ...), custom_call_target="tpu_custom_call" | custom-call | flops 1 | bytes 1 | tf_op jit(solution)/shard_map/place/pallas_call | solution.py:615
  320.3 5.5 %output.1 = bf16[512,2048]{1,0:T(8,128)(2,1)} custom-call(s32[10]{0:T(128)} %pad_add_fusion.sc, bf16[512,2048]{1,0:T(8,128)(2,1)} %x_ref.6, bf16[2,512,512]{2,1,0:T(8,128)(2,1)} %get-tuple-element.155.own_ref, bf16[2,512,512]{2,1,0:T(8,128)(2,1)} %copy-done.6, bf16[2,512,512]{2,1,0:T(8,128)(2,1)} %collective-permute-done.43.side_ref), custom_call_target="tpu_custom_call" | custom-call | flops 1 | bytes 1 | tf_op jit(solution)/shard_map/output/pallas_call | solution.py:531
  327.8 5.6 %place.3 = f32[3,16,32,2048]{3,2,1,0:T(8,128)} custom-call(s32[11]{0:T(128)} %pad_add_fusion.1.sc, bf16[3,32,2048]{2,1,0:T(8,128)(2,1)} %copy-done.13, bf16[3,32,2048]{2,1,0:T(8,128)(2,1)} %collective-permute-done.41.refs_1_, bf16[3,32,2048]{2,1,0:T(8,128)(2,1)} %collective-permute-done.44.refs_2_, ...), custom_call_target="tpu_custom_call", output_to_operand_aliasing={{}: (9, {})} | custom-call | flops 1 | bytes 1 | tf_op jit(solution)/shard_map/place/pallas_call | solution.py:615
  (248 shorter events, 115.7 us)
Async XLA Ops:
  1.8 15.0 %collective-permute-start = (bf16[128,2048]{1,0:T(8,128)(2,1)S(1)}, bf16[128,2048]{1,0:T(8,128)(2,1)S(1)}, u32[]{:S(2)}, u32[]{:S(2)}) collective-permute-start(bf16[128,2048]{1,0:T(8,128)(2,1)S(1)} %constant_dynamic-slice_fusion.8), channel_id=1, source_target_pairs={{0,2},{1,3},{2,0},{3,1},{4,6},{5,7},{6,4},{7,5},{8,10},{9,11},{10,... | collective-permute-start | bytes 1572872 | tf_op jit(solution)/shard_map/ppermute | solution.py:31
  8.0 17.8 %collective-permute-start.3 = (bf16[512,2048]{1,0:T(8,128)(2,1)}, bf16[512,2048]{1,0:T(8,128)(2,1)}, u32[]{:S(2)}, u32[]{:S(2)}) collective-permute-start(bf16[512,2048]{1,0:T(8,128)(2,1)} %slice.204), channel_id=1, source_target_pairs={{0,1},{1,0},{2,3},{3,2},{4,5},{5,4},{6,7},{7,6},{8,9},{9,8},{10,11... | collective-permute-start | bytes 6291464 | tf_op jit(solution)/shard_map/ppermute | solution.py:31
  16.7 10.6 %collective-permute-start.2 = (bf16[512,2048]{1,0:T(8,128)(2,1)}, bf16[512,2048]{1,0:T(8,128)(2,1)}, u32[]{:S(2)}, u32[]{:S(2)}) collective-permute-start(bf16[512,2048]{1,0:T(8,128)(2,1)} %get-tuple-element.122.n0_ref.c0_ref), channel_id=1, source_target_pairs={{0,1},{1,0},{2,3},{3,2},{4,5},{5,4},{6,7},{7,6},{8,9},{9,8},{10,11... | collective-permute-start | bytes 6291464 | tf_op jit(solution)/shard_map/ppermute | solution.py:31
  18.0 53.2 %collective-permute-start.10 = (bf16[512,2048]{1,0:T(8,128)(2,1)}, bf16[512,2048]{1,0:T(8,128)(2,1)}, u32[]{:S(2)}, u32[]{:S(2)}) collective-permute-start(bf16[512,2048]{1,0:T(8,128)(2,1)} %get-tuple-element.122.n0_ref.c0_ref), channel_id=1, source_target_pairs={{0,2},{1,3},{2,0},{3,1},{4,6},{5,7},{6,4},{7,5},{8,10},{9,11},{10,... | collective-permute-start | bytes 6291464 | tf_op jit(solution)/shard_map/ppermute | solution.py:31
  20.3 16.8 %collective-permute-start.4 = (bf16[128,2048]{1,0:T(8,128)(2,1)S(1)}, bf16[128,2048]{1,0:T(8,128)(2,1)S(1)}, u32[]{:S(2)}, u32[]{:S(2)}) collective-permute-start(bf16[128,2048]{1,0:T(8,128)(2,1)S(1)} %collective-permute-done), channel_id=1, source_target_pairs={{0,8},{4,12},{8,0},{12,4},{16,24},{20,28},{24,16},{28,20},{1,9},{5... | collective-permute-start | bytes 1572872 | tf_op jit(solution)/shard_map/ppermute | solution.py:671
  24.3 27.9 %collective-permute-start.7 = (bf16[512,512]{1,0:T(8,128)(2,1)}, bf16[512,512]{1,0:T(8,128)(2,1)}, u32[]{:S(2)}, u32[]{:S(2)}) collective-permute-start(bf16[512,512]{1,0:T(8,128)(2,1)} %get-tuple-element.232), channel_id=1, source_target_pairs={{0,1},{1,0},{2,3},{3,2},{4,5},{5,4},{6,7},{7,6},{8,9},{9,8},{10,11... | collective-permute-start | bytes 1572872 | tf_op jit(solution)/shard_map/ppermute | solution.py:31
  25.8 24.6 %collective-permute-start.5 = (bf16[128,2048]{1,0:T(8,128)(2,1)S(1)}, bf16[128,2048]{1,0:T(8,128)(2,1)}, u32[]{:S(2)}, u32[]{:S(2)}) collective-permute-start(bf16[128,2048]{1,0:T(8,128)(2,1)S(1)} %collective-permute-done), channel_id=1, source_target_pairs={{0,4},{4,0},{8,12},{12,8},{16,20},{20,16},{24,28},{28,24},{1,5},{5... | collective-permute-start | bytes 1572872 | tf_op jit(solution)/shard_map/ppermute | solution.py:670
  36.6 15.5 %collective-permute-start.6 = (bf16[128,2048]{1,0:T(8,128)(2,1)S(1)}, bf16[128,2048]{1,0:T(8,128)(2,1)S(1)}, u32[]{:S(2)}, u32[]{:S(2)}) collective-permute-start(bf16[128,2048]{1,0:T(8,128)(2,1)S(1)} %collective-permute-done), channel_id=1, source_target_pairs={{0,12},{4,8},{8,4},{12,0},{16,28},{20,24},{24,20},{28,16},{1,13},{... | collective-permute-start | bytes 1572872 | tf_op jit(solution)/shard_map/ppermute | solution.py:714
  51.5 18.9 %collective-permute-start.9 = (f32[8,2048]{1,0:T(8,128)S(1)}, f32[8,2048]{1,0:T(8,128)S(1)}, u32[]{:S(2)}, u32[]{:S(2)}) collective-permute-start(f32[8,2048]{1,0:T(8,128)S(1)} %pad_maximum_fusion.4), channel_id=1, source_target_pairs={{0,3},{1,2},{2,1},{3,0},{4,7},{5,6},{6,5},{7,4},{8,11},{9,10},{10,... | collective-permute-start | bytes 196616 | tf_op jit(solution)/shard_map/ppermute | solution.py:31
  51.6 18.8 %collective-permute-start.8 = (f32[8,2048]{1,0:T(8,128)S(1)}, f32[8,2048]{1,0:T(8,128)S(1)}, u32[]{:S(2)}, u32[]{:S(2)}) collective-permute-start(f32[8,2048]{1,0:T(8,128)S(1)} %pad_maximum_fusion.4), channel_id=1, source_target_pairs={{0,2},{1,3},{2,0},{3,1},{4,6},{5,7},{6,4},{7,5},{8,10},{9,11},{10,... | collective-permute-start | bytes 196616 | tf_op jit(solution)/shard_map/ppermute | solution.py:31
  71.2 11.9 %collective-permute-start.11 = (bf16[512,2048]{1,0:T(8,128)(2,1)}, bf16[512,2048]{1,0:T(8,128)(2,1)S(1)}, u32[]{:S(2)}, u32[]{:S(2)}) collective-permute-start(bf16[512,2048]{1,0:T(8,128)(2,1)} %collective-permute-done.10.n_ref.c0_ref.n2_ref), channel_id=1, source_target_pairs={{0,1},{1,0},{2,3},{3,2},{4,5},{5,4},{6,7},{7,6},{8,9},{9,8},{10,11... | collective-permute-start | bytes 6291464 | tf_op jit(solution)/shard_map/ppermute | solution.py:31
  72.4 20.1 %collective-permute-start.12 = (bf16[512,512]{1,0:T(8,128)(2,1)}, bf16[512,512]{1,0:T(8,128)(2,1)S(1)}, u32[]{:S(2)}, u32[]{:S(2)}) collective-permute-start(bf16[512,512]{1,0:T(8,128)(2,1)} %get-tuple-element.134), channel_id=1, source_target_pairs={{0,2},{1,3},{2,0},{3,1},{4,6},{5,7},{6,4},{7,5},{8,10},{9,11},{10,... | collective-permute-start | bytes 1572872 | tf_op jit(solution)/shard_map/ppermute | solution.py:31
  72.9 23.8 %collective-permute-start.13 = (bf16[512,512]{1,0:T(8,128)(2,1)}, bf16[512,512]{1,0:T(8,128)(2,1)S(1)}, u32[]{:S(2)}, u32[]{:S(2)}) collective-permute-start(bf16[512,512]{1,0:T(8,128)(2,1)} %get-tuple-element.135), channel_id=1, source_target_pairs={{0,3},{1,2},{2,1},{3,0},{4,7},{5,6},{6,5},{7,4},{8,11},{9,10},{10,... | collective-permute-start | bytes 1572872 | tf_op jit(solution)/shard_map/ppermute | solution.py:31
  128.3 13.7 %collective-permute-start.15 = (bf16[3,32,2048]{2,1,0:T(8,128)(2,1)S(1)}, bf16[3,32,2048]{2,1,0:T(8,128)(2,1)S(1)}, u32[]{:S(2)}, u32[]{:S(2)}) collective-permute-start(bf16[3,32,2048]{2,1,0:T(8,128)(2,1)S(1)} %fusion.13), channel_id=1, source_target_pairs={{0,8},{1,5},{2,10},{3,7},{8,16},{9,1},{10,18},{11,3},{16,24},{17,9... | collective-permute-start | bytes 1179656 | tf_op jit(solution)/shard_map/ppermute | solution.py:572
  141.7 24.1 %collective-permute-start.17 = (bf16[512,2048]{1,0:T(8,128)(2,1)}, bf16[512,2048]{1,0:T(8,128)(2,1)}, u32[]{:S(2)}, u32[]{:S(2)}) collective-permute-start(bf16[512,2048]{1,0:T(8,128)(2,1)} %get-tuple-element.148), channel_id=1, source_target_pairs={{0,1},{1,0},{2,3},{3,2},{4,5},{5,4},{6,7},{7,6},{8,9},{9,8},{10,11... | collective-permute-start | bytes 6291464 | tf_op jit(solution)/shard_map/ppermute | solution.py:31
  143.0 17.5 %collective-permute-start.16 = (bf16[3,32,2048]{2,1,0:T(8,128)(2,1)S(1)}, bf16[3,32,2048]{2,1,0:T(8,128)(2,1)S(1)}, u32[]{:S(2)}, u32[]{:S(2)}) collective-permute-start(bf16[3,32,2048]{2,1,0:T(8,128)(2,1)S(1)} %fusion.12), channel_id=1, source_target_pairs={{0,8},{1,5},{2,10},{3,7},{8,16},{9,1},{10,18},{11,3},{16,24},{17,9... | collective-permute-start | bytes 1179656 | tf_op jit(solution)/shard_map/ppermute | solution.py:572
  162.8 13.6 %collective-permute-start.19 = (bf16[3,32,2048]{2,1,0:T(8,128)(2,1)S(1)}, bf16[3,32,2048]{2,1,0:T(8,128)(2,1)S(1)}, u32[]{:S(2)}, u32[]{:S(2)}) collective-permute-start(bf16[3,32,2048]{2,1,0:T(8,128)(2,1)S(1)} %slice_bitcast_fusion.8), channel_id=1, source_target_pairs={{0,8},{1,5},{2,10},{3,7},{8,16},{9,1},{10,18},{11,3},{16,24},{17,9... | collective-permute-start | bytes 1179656 | tf_op jit(solution)/shard_map/ppermute | solution.py:572
  164.2 10.6 %collective-permute-start.20 = (bf16[3,32,2048]{2,1,0:T(8,128)(2,1)S(1)}, bf16[3,32,2048]{2,1,0:T(8,128)(2,1)S(1)}, u32[]{:S(2)}, u32[]{:S(2)}) collective-permute-start(bf16[3,32,2048]{2,1,0:T(8,128)(2,1)S(1)} %fusion.11), channel_id=1, source_target_pairs={{0,8},{1,5},{2,10},{3,7},{8,16},{9,1},{10,18},{11,3},{16,24},{17,9... | collective-permute-start | bytes 1179656 | tf_op jit(solution)/shard_map/ppermute | solution.py:572
  167.6 29.4 %collective-permute-start.27 = (bf16[256,2048]{1,0:T(8,128)(2,1)S(1)}, bf16[256,2048]{1,0:T(8,128)(2,1)S(1)}, u32[]{:S(2)}, u32[]{:S(2)}) collective-permute-start(bf16[256,2048]{1,0:T(8,128)(2,1)S(1)} %add_convert_fusion.1), channel_id=1, source_target_pairs={{0,2},{1,3},{2,0},{3,1},{4,6},{5,7},{6,4},{7,5},{8,10},{9,11},{10,... | collective-permute-start | bytes 3145736 | tf_op jit(solution)/shard_map/ppermute | solution.py:31
  176.5 10.5 %collective-permute-start.21 = (bf16[3,32,2048]{2,1,0:T(8,128)(2,1)S(1)}, bf16[3,32,2048]{2,1,0:T(8,128)(2,1)S(1)}, u32[]{:S(2)}, u32[]{:S(2)}) collective-permute-start(bf16[3,32,2048]{2,1,0:T(8,128)(2,1)S(1)} %fusion.9), channel_id=1, source_target_pairs={{0,8},{1,5},{2,10},{3,7},{8,16},{9,1},{10,18},{11,3},{16,24},{17,9... | collective-permute-start | bytes 1179656 | tf_op jit(solution)/shard_map/ppermute | solution.py:572
  216.3 17.7 %collective-permute-start.28 = (bf16[512,2048]{1,0:T(8,128)(2,1)}, bf16[512,2048]{1,0:T(8,128)(2,1)}, u32[]{:S(2)}, u32[]{:S(2)}) collective-permute-start(bf16[512,2048]{1,0:T(8,128)(2,1)} %get-tuple-element.175), channel_id=1, source_target_pairs={{0,1},{1,0},{2,3},{3,2},{4,5},{5,4},{6,7},{7,6},{8,9},{9,8},{10,11... | collective-permute-start | bytes 6291464 | tf_op jit(solution)/shard_map/ppermute | solution.py:31
  227.0 13.2 %collective-permute-start.34 = (bf16[3,32,2048]{2,1,0:T(8,128)(2,1)}, bf16[3,32,2048]{2,1,0:T(8,128)(2,1)}, u32[]{:S(2)}, u32[]{:S(2)}) collective-permute-start(bf16[3,32,2048]{2,1,0:T(8,128)(2,1)} %fusion.2), channel_id=1, source_target_pairs={{0,8},{1,5},{2,10},{3,7},{8,16},{9,1},{10,18},{11,3},{16,24},{17,9... | collective-permute-start | bytes 1179656 | tf_op jit(solution)/shard_map/ppermute | solution.py:572
  228.8 23.6 %collective-permute-start.33 = (bf16[256,2048]{1,0:T(8,128)(2,1)}, bf16[256,2048]{1,0:T(8,128)(2,1)}, u32[]{:S(2)}, u32[]{:S(2)}) collective-permute-start(bf16[256,2048]{1,0:T(8,128)(2,1)} %add_convert_fusion), channel_id=1, source_target_pairs={{0,2},{1,3},{2,0},{3,1},{4,6},{5,7},{6,4},{7,5},{8,10},{9,11},{10,... | collective-permute-start | bytes 3145736 | tf_op jit(solution)/shard_map/ppermute | solution.py:31
  232.4 20.0 %collective-permute-start.36 = (bf16[3,32,2048]{2,1,0:T(8,128)(2,1)}, bf16[3,32,2048]{2,1,0:T(8,128)(2,1)}, u32[]{:S(2)}, u32[]{:S(2)}) collective-permute-start(bf16[3,32,2048]{2,1,0:T(8,128)(2,1)} %collective-permute-done.31.refs_1_), channel_id=1, source_target_pairs={{0,8},{1,5},{2,10},{3,7},{8,16},{9,1},{10,18},{11,3},{16,24},{17,9... | collective-permute-start | bytes 1179656 | tf_op jit(solution)/shard_map/ppermute | solution.py:572
  241.3 12.3 %collective-permute-start.35 = (bf16[3,32,2048]{2,1,0:T(8,128)(2,1)S(1)}, bf16[3,32,2048]{2,1,0:T(8,128)(2,1)S(1)}, u32[]{:S(2)}, u32[]{:S(2)}) collective-permute-start(bf16[3,32,2048]{2,1,0:T(8,128)(2,1)S(1)} %fusion.1), channel_id=1, source_target_pairs={{0,8},{1,5},{2,10},{3,7},{8,16},{9,1},{10,18},{11,3},{16,24},{17,9... | collective-permute-start | bytes 1179656 | tf_op jit(solution)/shard_map/ppermute | solution.py:572
  252.4 10.4 %collective-permute-start.37 = (bf16[3,32,2048]{2,1,0:T(8,128)(2,1)}, bf16[3,32,2048]{2,1,0:T(8,128)(2,1)}, u32[]{:S(2)}, u32[]{:S(2)}) collective-permute-start(bf16[3,32,2048]{2,1,0:T(8,128)(2,1)} %collective-permute-done.36.refs_2_), channel_id=1, source_target_pairs={{0,8},{1,5},{2,10},{3,7},{8,16},{9,1},{10,18},{11,3},{16,24},{17,9... | collective-permute-start | bytes 1179656 | tf_op jit(solution)/shard_map/ppermute | solution.py:572
  255.4 23.0 %collective-permute-start.18 = (bf16[2,512,512]{2,1,0:T(8,128)(2,1)}, bf16[2,512,512]{2,1,0:T(8,128)(2,1)S(1)}, u32[]{:S(2)}, u32[]{:S(2)}) collective-permute-start(bf16[2,512,512]{2,1,0:T(8,128)(2,1)} %pad_maximum_fusion), channel_id=1, source_target_pairs={{0,1},{1,0},{2,3},{3,2},{4,5},{5,4},{6,7},{7,6},{8,9},{9,8},{10,11... | collective-permute-start | bytes 3145736 | tf_op jit(solution)/shard_map/ppermute | solution.py:31
  264.2 10.9 %collective-permute-start.41 = (bf16[3,32,2048]{2,1,0:T(8,128)(2,1)S(1)}, bf16[3,32,2048]{2,1,0:T(8,128)(2,1)}, u32[]{:S(2)}, u32[]{:S(2)}) collective-permute-start(bf16[3,32,2048]{2,1,0:T(8,128)(2,1)S(1)} %pad_maximum_fusion.3.refs_0_), channel_id=1, source_target_pairs={{0,8},{1,5},{2,10},{3,7},{8,16},{9,1},{10,18},{11,3},{16,24},{17,9... | collective-permute-start | bytes 1179656 | tf_op jit(solution)/shard_map/ppermute | solution.py:572
  266.0 10.5 %collective-permute-start.40 = (f32[8,2048]{1,0:T(8,128)S(1)}, f32[8,2048]{1,0:T(8,128)S(1)}, u32[]{:S(2)}, u32[]{:S(2)}) collective-permute-start(f32[8,2048]{1,0:T(8,128)S(1)} %pad_maximum_fusion.5), channel_id=1, source_target_pairs={{0,1},{1,0},{2,3},{3,2},{4,5},{5,4},{6,7},{7,6},{8,9},{9,8},{10,11... | collective-permute-start | bytes 196616 | tf_op jit(solution)/shard_map/ppermute | solution.py:31
  278.6 24.8 %collective-permute-start.43 = (bf16[2,512,512]{2,1,0:T(8,128)(2,1)S(1)}, bf16[2,512,512]{2,1,0:T(8,128)(2,1)}, u32[]{:S(2)}, u32[]{:S(2)}) collective-permute-start(bf16[2,512,512]{2,1,0:T(8,128)(2,1)S(1)} %pad_maximum_fusion.1), channel_id=1, source_target_pairs={{0,2},{1,3},{2,0},{3,1},{4,6},{5,7},{6,4},{7,5},{8,10},{9,11},{10,... | collective-permute-start | bytes 3145736 | tf_op jit(solution)/shard_map/ppermute | solution.py:31
  287.7 13.4 %collective-permute-start.50 = (bf16[3,32,2048]{2,1,0:T(8,128)(2,1)S(1)}, bf16[3,32,2048]{2,1,0:T(8,128)(2,1)S(1)}, u32[]{:S(2)}, u32[]{:S(2)}) collective-permute-start(bf16[3,32,2048]{2,1,0:T(8,128)(2,1)S(1)} %collective-permute-done.47.refs_6_), channel_id=1, source_target_pairs={{0,8},{1,5},{2,10},{3,7},{8,16},{9,1},{10,18},{11,3},{16,24},{17,9... | collective-permute-start | bytes 1179656 | tf_op jit(solution)/shard_map/ppermute | solution.py:572
  307.6 18.2 %collective-permute-start.56 = (f32[4,2048]{1,0:T(4,128)S(1)}, f32[4,2048]{1,0:T(4,128)S(1)}, u32[]{:S(2)}, u32[]{:S(2)}) collective-permute-start(f32[4,2048]{1,0:T(4,128)S(1)} %add.183), channel_id=1, source_target_pairs={{0,16},{4,20},{8,24},{12,28},{16,0},{20,4},{24,8},{28,12},{1,17},{... | collective-permute-start | bytes 98312 | tf_op jit(solution)/shard_map/ppermute | solution.py:848
  (56 other events, 567.0 us)

commit v5 on v4

--- a/solution.py
+++ b/solution.py
@@ -907,7 +907,7 @@
             scan(0), weigh(0), start(0), scan(1), r0, far_in, r0, weigh(1), r0, start(1), to_x(0),
             out_core, r0, r1, r0, r1, r0, r1, arrive(0), r0, to_x(1), r1, near_input, r0, r1, r0, norm_back(0), r1,
             arrive(1), r0, r1, norm_back(1), r0, r1, sums_core, r0, r1, sums_side, out_side, r0, r1, sums_ends, r0, r1,
-            sums_dp(2), r0, r1, outs_arrive, sums_dp(4), r1, put(0), r1, output, sums_dp(8), r1, put(1),
+            sums_dp(2), r0, r1, r1, sums_dp(4), put(0), r1, sums_dp(8), outs_arrive, output, r1, put(1),
         ):
             task()
         assert all(len(ring.pieces) == RING for ring in rings)

time: 335 us -> 334 us (level)
    ppermute x28, waiting for transfers between devices: 38.1 us -> 45.8 us  [around(): return lax.ppermute(value, ('dp', 'tp'), pairs)]
    ppermute x3, waiting for transfers between devices: 10.6 us -> 5.09 us  [send_sums(): lax.ppermute(work['sums'], 'dp', [(i, i ^ bit) for i in range(dp)])]
  transfers between devices with their start and end apart: 57 -> 57, of which waited for: 21 -> 24; matrix products, arithmetic and copies ran while one was open for 11% -> 11% of each run, Pallas kernels for 31% -> 31%
where the time goes in v5:
time: 334 us; the launch traced here: 333 us
  Pallas kernels  141 us (42%)
  waiting for transfers between devices  82.8 us (25%)
  starting transfers between devices  60.1 us (18%)
  local copies, waits for them, and re-layouts  25.9 us (8%)
  other arithmetic  21.1 us (6%)
    ppermute x28, waiting for transfers between devices, around(): return lax.ppermute(value, ('dp', 'tp'), pairs)  45.8 us
    ppermute x28, starting transfers between devices, around(): return lax.ppermute(value, ('dp', 'tp'), pairs)  36.7 us
    pallas_call x2, Pallas kernels, run_weight(): pl.pallas_call(weight_kernel, name='weight_grad', grid_spec=pltpu.Prefetc...  27.1 us
    pallas_call x2, Pallas kernels, run_input(): pl.pallas_call(kernel, name=name, grid_spec=pltpu.PrefetchScalarGridSpec(...  23.4 us
    ppermute x23, waiting for transfers between devices, swap(): return lax.ppermute(value, 'tp', [(t, t ^ by) for t in range(TP)])  18.6 us
    pallas_call x1, Pallas kernels, run_near(): pl.pallas_call(near_kernel, name='near', grid_spec=pltpu.PrefetchScalarGr...  16.7 us
    pallas_call x2, Pallas kernels, run_project(): pl.pallas_call(project_kernel, name='project', grid_spec=pltpu.PrefetchSc...  16.3 us
    ppermute x23, starting transfers between devices, swap(): return lax.ppermute(value, 'tp', [(t, t ^ by) for t in range(TP)])  15.1 us
  transfers between devices with their start and end apart: 57, of which 24 were waited for; matrix products, arithmetic and copies ran while one was open for 11% of the time, Pallas kernels for 31%

profile of v5, /device:TPU:0, one launch (start us, length us, event | category | flops | bytes accessed | tf_op | source)
XLA Modules:
  0.0 332.6 jit_solution(9815096835334562606)
XLA Ops:
  1.8 3.0 collective-permute-start
  4.8 3.2 slice.204
  8.0 6.3 %norm.1 = (bf16[512,2048]{1,0:T(8,128)(2,1)}, f32[512,128]{1,0:T(8,128)}, f32[512,128]{1,0:T(8,128)}) custom-call(bf16[512,2048]{1,0:T(8,128)(2,1)} %x_ref.6, f32[1,2048]{1,0:T(1,128)} %bitcast.138, f32[1,2048]{1,0:T(1,128)} %bitcast.141), custom_call_target="tpu_custom_call" | custom-call | flops 1 | bytes 1 | tf_op jit(solution)/shard_map/norm/pallas_call | solution.py:55
  27.4 9.3 %early.1.e_ref = bf16[2,2,512,512]{3,2,1,0:T(8,128)(2,1)} custom-call(s32[10]{0:T(128)} %pad_add_fusion.sc, bf16[512,2048]{1,0:T(8,128)(2,1)} %get-tuple-element.121.n0_ref.c0_ref, bf16[512,2048]{1,0:T(8,128)(2,1)} %collective-permute-done.2.n1_ref.c1_ref, bf16[1536,2048]{1,0:T(8,128)(2,1)} %w0_ref.9, bf16[512,2048]{1,0:T(8,128)(2,1)} %collective-permute-done.3.w1_ref), custom_call_target="tpu_custom_call" | custom-call | flops 4294967296 | bytes 8388608 | tf_op jit(solution)/shard_map/early/pallas_call | solution.py:84
  37.1 13.3 %collective-permute-done.5 = bf16[128,2048]{1,0:T(8,128)(2,1)} collective-permute-done((bf16[128,2048]{1,0:T(8,128)(2,1)S(1)}, bf16[128,2048]{1,0:T(8,128)(2,1)}, u32[]{:S(2)}, u32[]{:S(2)}) %collective-permute-start.5) | collective-permute-done | bytes 524320 | tf_op jit(solution)/shard_map/ppermute | solution.py:670
  53.7 16.7 %near.1 = (bf16[2,512,512]{2,1,0:T(8,128)(2,1)}, bf16[2,3,512,512]{3,2,1,0:T(8,128)(2,1)}, bf16[2,512,512]{2,1,0:T(8,128)(2,1)}, f32[2,8,512]{2,1,0:T(8,128)}, f32[2,8,512]{2,1,0:T(8,128)}) custom-call(s32[20]{0:T(128)} %concatenate.61.sc, bf16[2,2,512,512]{3,2,1,0:T(8,128)(2,1)} %early.1.e_ref, bf16[512,2048]{1,0:T(8,128)(2,1)} %bitcast.128, ...), custom_call_target="tpu_custom_call" | custom-call | flops 1 | bytes 1 | tf_op jit(solution)/shard_map/near/pallas_call | solution.py:311
  74.4 8.1 %project.2.s0_ref = bf16[3,512,512]{2,1,0:T(8,128)(2,1)} custom-call(s32[10]{0:T(128)} %pad_add_fusion.sc, bf16[512,2048]{1,0:T(8,128)(2,1)} %collective-permute-done.10.n_ref.c0_ref.n2_ref, bf16[1536,2048]{1,0:T(8,128)(2,1)} %w0_ref.9, bf16[512,2048]{1,0:T(8,128)(2,1)} %collective-permute-done.3.w1_ref, bf16[512,2048]{1,0:T(8,128)(2,1)} %bitcast.129), custom_call_target="tpu_custom_call" | custom-call | flops 1 | bytes 1 | tf_op jit(solution)/shard_map/project/pallas_call | solution.py:114
  84.4 8.2 %project.3.s1_ref = bf16[3,512,512]{2,1,0:T(8,128)(2,1)} custom-call(s32[10]{0:T(128)} %pad_add_fusion.sc, bf16[512,2048]{1,0:T(8,128)(2,1)} %copy-done.1, bf16[1536,2048]{1,0:T(8,128)(2,1)} %w0_ref.9, bf16[512,2048]{1,0:T(8,128)(2,1)} %collective-permute-done.3.w1_ref, bf16[512,2048]{1,0:T(8,128)(2,1)} %bitcast.130), custom_call_target="tpu_custom_call" | custom-call | flops 1 | bytes 1 | tf_op jit(solution)/shard_map/project/pallas_call | solution.py:114
  92.6 4.2 %collective-permute-done.13.og1_ref = bf16[512,512]{1,0:T(8,128)(2,1)S(1)} collective-permute-done((bf16[512,512]{1,0:T(8,128)(2,1)}, bf16[512,512]{1,0:T(8,128)(2,1)S(1)}, u32[]{:S(2)}, u32[]{:S(2)}) %collective-permute-start.13) | collective-permute-done | bytes 524320 | tf_op jit(solution)/shard_map/ppermute | solution.py:31
  97.6 6.7 %far.2 = (bf16[2,512,256]{2,1,0:T(8,128)(2,1)}, bf16[2,3,512,256]{3,2,1,0:T(8,128)(2,1)}, bf16[2,512,256]{2,1,0:T(8,128)(2,1)}, f32[2,8,256]{2,1,0:T(8,128)}, f32[2,8,256]{2,1,0:T(8,128)}) custom-call(s32[20]{0:T(128)} %concatenate.62.sc, bf16[3,512,512]{2,1,0:T(8,128)(2,1)} %project.2.s0_ref, bf16[3,512,512]{2,1,0:T(8,128)(2,1)} %project.3.s1_ref, ...), custom_call_target="tpu_custom_call" | custom-call | flops 1 | bytes 1 | tf_op jit(solution)/shard_map/far/pallas_call | solution.py:346
  104.3 13.5 %weight_grad.2 = bf16[8,3,32,2048]{3,2,1,0:T(8,128)(2,1)} custom-call(s32[8]{0:T(128)} %and_select_fusion.1.sc, bf16[2,3,512,512]{3,2,1,0:T(8,128)(2,1)} %get-tuple-element.136.near_ref.sg_ref, bf16[2,3,512,256]{3,2,1,0:T(8,128)(2,1)} %get-tuple-element.137.far_ref.sg0_ref, bf16[512,2048]{1,0:T(8,128)(2,1)} %get-tuple-element.121.n0_ref.c0_ref, ...), custom_call_target="tpu_custom_call" | custom-call | flops 1 | bytes 1 | tf_op jit(solution)/shard_map/weight_grad/pallas_call | solution.py:386
  119.3 6.6 %far.3 = (bf16[2,512,256]{2,1,0:T(8,128)(2,1)}, bf16[2,3,512,256]{3,2,1,0:T(8,128)(2,1)}, bf16[2,512,256]{2,1,0:T(8,128)(2,1)}, f32[2,8,256]{2,1,0:T(8,128)}, f32[2,8,256]{2,1,0:T(8,128)}) custom-call(s32[20]{0:T(128)} %concatenate.62.sc, bf16[3,512,512]{2,1,0:T(8,128)(2,1)} %project.2.s0_ref, bf16[3,512,512]{2,1,0:T(8,128)(2,1)} %project.3.s1_ref, ...), custom_call_target="tpu_custom_call" | custom-call | flops 1 | bytes 1 | tf_op jit(solution)/shard_map/far/pallas_call | solution.py:346
  130.0 11.7 %input_far.1 = (bf16[512,2048]{1,0:T(8,128)(2,1)}, bf16[512,2048]{1,0:T(8,128)(2,1)}) custom-call(s32[10]{0:T(128)} %pad_add_fusion.sc, bf16[1536,2048]{1,0:T(8,128)(2,1)} %w0_ref.9, bf16[512,2048]{1,0:T(8,128)(2,1)} %collective-permute-done.3.w1_ref, bf16[512,2048]{1,0:T(8,128)(2,1)} %bitcast.131, ...), custom_call_target="tpu_custom_call" | custom-call | flops 1 | bytes 1 | tf_op jit(solution)/shard_map/input_far/pallas_call | solution.py:431
  146.9 13.6 %weight_grad.3 = bf16[8,3,32,2048]{3,2,1,0:T(8,128)(2,1)} custom-call(s32[8]{0:T(128)} %and_select_fusion.1.sc, bf16[2,3,512,512]{3,2,1,0:T(8,128)(2,1)} %get-tuple-element.136.near_ref.sg_ref, bf16[2,3,512,256]{3,2,1,0:T(8,128)(2,1)} %get-tuple-element.149.sg1_ref.far_ref, bf16[512,2048]{1,0:T(8,128)(2,1)} %get-tuple-element.121.n0_ref.c0_ref, ...), custom_call_target="tpu_custom_call" | custom-call | flops 1 | bytes 1 | tf_op jit(solution)/shard_map/weight_grad/pallas_call | solution.py:386
  169.8 5.0 %collective-permute-done.20 = bf16[3,32,2048]{2,1,0:T(8,128)(2,1)S(1)} collective-permute-done((bf16[3,32,2048]{2,1,0:T(8,128)(2,1)S(1)}, bf16[3,32,2048]{2,1,0:T(8,128)(2,1)S(1)}, u32[]{:S(2)}, u32[]{:S(2)}) %collective-permute-start.20) | collective-permute-done | bytes 393248 | tf_op jit(solution)/shard_map/ppermute | solution.py:572
  178.2 4.6 %collective-permute-done.22 = bf16[3,32,2048]{2,1,0:T(8,128)(2,1)S(1)} collective-permute-done((bf16[3,32,2048]{2,1,0:T(8,128)(2,1)S(1)}, bf16[3,32,2048]{2,1,0:T(8,128)(2,1)S(1)}, u32[]{:S(2)}, u32[]{:S(2)}) %collective-permute-start.22) | collective-permute-done | bytes 393248 | tf_op jit(solution)/shard_map/ppermute | solution.py:572
  188.6 2.6 collective-permute-done.24
  204.7 11.6 %input_near.1 = (bf16[512,2048]{1,0:T(8,128)(2,1)}, bf16[512,2048]{1,0:T(8,128)(2,1)}) custom-call(s32[10]{0:T(128)} %pad_add_fusion.sc, bf16[1536,2048]{1,0:T(8,128)(2,1)} %w0_ref.9, bf16[512,2048]{1,0:T(8,128)(2,1)} %collective-permute-done.3.w1_ref, bf16[512,2048]{1,0:T(8,128)(2,1)} %bitcast.132, ...), custom_call_target="tpu_custom_call" | custom-call | flops 1 | bytes 1 | tf_op jit(solution)/shard_map/input_near/pallas_call | solution.py:431
  221.0 3.4 %collective-permute-done.30 = bf16[32,2048]{1,0:T(8,128)(2,1)S(1)} collective-permute-done((bf16[32,2048]{1,0:T(8,128)(2,1)S(1)}, bf16[32,2048]{1,0:T(8,128)(2,1)S(1)}, u32[]{:S(2)}, u32[]{:S(2)}) %collective-permute-start.30) | collective-permute-done | bytes 131104 | tf_op jit(solution)/shard_map/ppermute | solution.py:31
  234.0 6.2 %norm_back.2 = (f32[512,2048]{1,0:T(8,128)}, f32[16,2048]{1,0:T(8,128)}) custom-call(bf16[512,2048]{1,0:T(8,128)(2,1)} %get-tuple-element.173.home_ref, bf16[512,2048]{1,0:T(8,128)(2,1)} %collective-permute-done.28.back_ref, bf16[256,2048]{1,0:T(8,128)(2,1)} %copy-done.16, bf16[512,2048]{1,0:T(8,128)(2,1)} %x_ref.6, f32[512,128]{1,0:T(8,128)} %get-tuple-element.179.mean_ref, ...), custom_call_target="tpu_custom_call" | custom-call | flops 1 | bytes 1 | tf_op jit(solution)/shard_map/norm_back/pallas_call | solution.py:490
  243.9 8.4 %collective-permute-done.33.side_ref = bf16[256,2048]{1,0:T(8,128)(2,1)} collective-permute-done((bf16[256,2048]{1,0:T(8,128)(2,1)}, bf16[256,2048]{1,0:T(8,128)(2,1)}, u32[]{:S(2)}, u32[]{:S(2)}) %collective-permute-start.33) | collective-permute-done | bytes 1048608 | tf_op jit(solution)/shard_map/ppermute | solution.py:31
  255.5 6.3 %norm_back.3 = (f32[512,2048]{1,0:T(8,128)}, f32[16,2048]{1,0:T(8,128)}) custom-call(bf16[512,2048]{1,0:T(8,128)(2,1)} %get-tuple-element.173.home_ref, bf16[512,2048]{1,0:T(8,128)(2,1)} %collective-permute-done.28.back_ref, bf16[256,2048]{1,0:T(8,128)(2,1)} %collective-permute-done.33.side_ref, ...), custom_call_target="tpu_custom_call", output_to_operand_aliasing={{0}: (8, {})} | custom-call | flops 1 | bytes 1 | tf_op jit(solution)/shard_map/norm_back/pallas_call | solution.py:490
  266.0 4.8 %collective-permute-done.42.refs_4_ = bf16[3,32,2048]{2,1,0:T(8,128)(2,1)} collective-permute-done((bf16[3,32,2048]{2,1,0:T(8,128)(2,1)}, bf16[3,32,2048]{2,1,0:T(8,128)(2,1)}, u32[]{:S(2)}, u32[]{:S(2)}) %collective-permute-start.42) | collective-permute-done | bytes 393248 | tf_op jit(solution)/shard_map/ppermute | solution.py:572
  272.2 2.9 collective-permute-done.41.refs_1_
  280.5 3.0 collective-permute-done.44.refs_2_
  284.8 2.8 collective-permute-done.47.refs_6_
  288.9 3.0 collective-permute-done.46.refs_3_
  295.9 5.1 %collective-permute-done.51 = f32[4,2048]{1,0:T(4,128)S(1)} collective-permute-done((f32[4,2048]{1,0:T(4,128)S(1)}, f32[4,2048]{1,0:T(4,128)S(1)}, u32[]{:S(2)}, u32[]{:S(2)}) %collective-permute-start.51) | collective-permute-done | bytes 32800 | tf_op jit(solution)/shard_map/ppermute | solution.py:848
  303.2 5.9 %collective-permute-done.52.refs_5_ = bf16[3,32,2048]{2,1,0:T(8,128)(2,1)} collective-permute-done((bf16[3,32,2048]{2,1,0:T(8,128)(2,1)}, bf16[3,32,2048]{2,1,0:T(8,128)(2,1)}, u32[]{:S(2)}, u32[]{:S(2)}) %collective-permute-start.52) | collective-permute-done | bytes 393248 | tf_op jit(solution)/shard_map/ppermute | solution.py:572
  312.6 5.6 %place.2.refs_8_ = f32[3,16,32,2048]{3,2,1,0:T(8,128)} custom-call(s32[11]{0:T(128)} %pad_add_fusion.1.sc, bf16[3,32,2048]{2,1,0:T(8,128)(2,1)} %copy-done.12, bf16[3,32,2048]{2,1,0:T(8,128)(2,1)} %collective-permute-done.31.refs_1_, bf16[3,32,2048]{2,1,0:T(8,128)(2,1)} %collective-permute-done.36.refs_2_, ...), custom_call_target="tpu_custom_call" | custom-call | flops 1 | bytes 1 | tf_op jit(solution)/shard_map/place/pallas_call | solution.py:615
  319.7 5.5 %output.1 = bf16[512,2048]{1,0:T(8,128)(2,1)} custom-call(s32[10]{0:T(128)} %pad_add_fusion.sc, bf16[512,2048]{1,0:T(8,128)(2,1)} %x_ref.6, bf16[2,512,512]{2,1,0:T(8,128)(2,1)} %get-tuple-element.154.own_ref, bf16[2,512,512]{2,1,0:T(8,128)(2,1)} %copy-done.6, bf16[2,512,512]{2,1,0:T(8,128)(2,1)} %collective-permute-done.43.side_ref), custom_call_target="tpu_custom_call" | custom-call | flops 1 | bytes 1 | tf_op jit(solution)/shard_map/output/pallas_call | solution.py:531
  327.0 5.6 %place.3 = f32[3,16,32,2048]{3,2,1,0:T(8,128)} custom-call(s32[11]{0:T(128)} %pad_add_fusion.1.sc, bf16[3,32,2048]{2,1,0:T(8,128)(2,1)} %copy-done.13, bf16[3,32,2048]{2,1,0:T(8,128)(2,1)} %collective-permute-done.41.refs_1_, bf16[3,32,2048]{2,1,0:T(8,128)(2,1)} %collective-permute-done.44.refs_2_, ...), custom_call_target="tpu_custom_call", output_to_operand_aliasing={{}: (9, {})} | custom-call | flops 1 | bytes 1 | tf_op jit(solution)/shard_map/place/pallas_call | solution.py:615
  (246 shorter events, 114.4 us)
Async XLA Ops:
  1.8 15.0 %collective-permute-start = (bf16[128,2048]{1,0:T(8,128)(2,1)S(1)}, bf16[128,2048]{1,0:T(8,128)(2,1)S(1)}, u32[]{:S(2)}, u32[]{:S(2)}) collective-permute-start(bf16[128,2048]{1,0:T(8,128)(2,1)S(1)} %constant_dynamic-slice_fusion.8), channel_id=1, source_target_pairs={{0,2},{1,3},{2,0},{3,1},{4,6},{5,7},{6,4},{7,5},{8,10},{9,11},{10,... | collective-permute-start | bytes 1572872 | tf_op jit(solution)/shard_map/ppermute | solution.py:31
  8.0 17.9 %collective-permute-start.3 = (bf16[512,2048]{1,0:T(8,128)(2,1)}, bf16[512,2048]{1,0:T(8,128)(2,1)}, u32[]{:S(2)}, u32[]{:S(2)}) collective-permute-start(bf16[512,2048]{1,0:T(8,128)(2,1)} %slice.204), channel_id=1, source_target_pairs={{0,1},{1,0},{2,3},{3,2},{4,5},{5,4},{6,7},{7,6},{8,9},{9,8},{10,11... | collective-permute-start | bytes 6291464 | tf_op jit(solution)/shard_map/ppermute | solution.py:31
  16.7 10.7 %collective-permute-start.2 = (bf16[512,2048]{1,0:T(8,128)(2,1)}, bf16[512,2048]{1,0:T(8,128)(2,1)}, u32[]{:S(2)}, u32[]{:S(2)}) collective-permute-start(bf16[512,2048]{1,0:T(8,128)(2,1)} %get-tuple-element.121.n0_ref.c0_ref), channel_id=1, source_target_pairs={{0,1},{1,0},{2,3},{3,2},{4,5},{5,4},{6,7},{7,6},{8,9},{9,8},{10,11... | collective-permute-start | bytes 6291464 | tf_op jit(solution)/shard_map/ppermute | solution.py:31
  18.1 53.2 %collective-permute-start.10 = (bf16[512,2048]{1,0:T(8,128)(2,1)}, bf16[512,2048]{1,0:T(8,128)(2,1)}, u32[]{:S(2)}, u32[]{:S(2)}) collective-permute-start(bf16[512,2048]{1,0:T(8,128)(2,1)} %get-tuple-element.121.n0_ref.c0_ref), channel_id=1, source_target_pairs={{0,2},{1,3},{2,0},{3,1},{4,6},{5,7},{6,4},{7,5},{8,10},{9,11},{10,... | collective-permute-start | bytes 6291464 | tf_op jit(solution)/shard_map/ppermute | solution.py:31
  20.3 16.7 %collective-permute-start.4 = (bf16[128,2048]{1,0:T(8,128)(2,1)S(1)}, bf16[128,2048]{1,0:T(8,128)(2,1)S(1)}, u32[]{:S(2)}, u32[]{:S(2)}) collective-permute-start(bf16[128,2048]{1,0:T(8,128)(2,1)S(1)} %collective-permute-done), channel_id=1, source_target_pairs={{0,8},{4,12},{8,0},{12,4},{16,24},{20,28},{24,16},{28,20},{1,9},{5... | collective-permute-start | bytes 1572872 | tf_op jit(solution)/shard_map/ppermute | solution.py:671
  24.4 27.9 %collective-permute-start.7 = (bf16[512,512]{1,0:T(8,128)(2,1)}, bf16[512,512]{1,0:T(8,128)(2,1)}, u32[]{:S(2)}, u32[]{:S(2)}) collective-permute-start(bf16[512,512]{1,0:T(8,128)(2,1)} %get-tuple-element.230), channel_id=1, source_target_pairs={{0,1},{1,0},{2,3},{3,2},{4,5},{5,4},{6,7},{7,6},{8,9},{9,8},{10,11... | collective-permute-start | bytes 1572872 | tf_op jit(solution)/shard_map/ppermute | solution.py:31
  25.9 24.6 %collective-permute-start.5 = (bf16[128,2048]{1,0:T(8,128)(2,1)S(1)}, bf16[128,2048]{1,0:T(8,128)(2,1)}, u32[]{:S(2)}, u32[]{:S(2)}) collective-permute-start(bf16[128,2048]{1,0:T(8,128)(2,1)S(1)} %collective-permute-done), channel_id=1, source_target_pairs={{0,4},{4,0},{8,12},{12,8},{16,20},{20,16},{24,28},{28,24},{1,5},{5... | collective-permute-start | bytes 1572872 | tf_op jit(solution)/shard_map/ppermute | solution.py:670
  36.7 15.5 %collective-permute-start.6 = (bf16[128,2048]{1,0:T(8,128)(2,1)S(1)}, bf16[128,2048]{1,0:T(8,128)(2,1)S(1)}, u32[]{:S(2)}, u32[]{:S(2)}) collective-permute-start(bf16[128,2048]{1,0:T(8,128)(2,1)S(1)} %collective-permute-done), channel_id=1, source_target_pairs={{0,12},{4,8},{8,4},{12,0},{16,28},{20,24},{24,20},{28,16},{1,13},{... | collective-permute-start | bytes 1572872 | tf_op jit(solution)/shard_map/ppermute | solution.py:714
  51.5 18.9 %collective-permute-start.9 = (f32[8,2048]{1,0:T(8,128)S(1)}, f32[8,2048]{1,0:T(8,128)S(1)}, u32[]{:S(2)}, u32[]{:S(2)}) collective-permute-start(f32[8,2048]{1,0:T(8,128)S(1)} %pad_maximum_fusion.4), channel_id=1, source_target_pairs={{0,3},{1,2},{2,1},{3,0},{4,7},{5,6},{6,5},{7,4},{8,11},{9,10},{10,... | collective-permute-start | bytes 196616 | tf_op jit(solution)/shard_map/ppermute | solution.py:31
  51.6 18.8 %collective-permute-start.8 = (f32[8,2048]{1,0:T(8,128)S(1)}, f32[8,2048]{1,0:T(8,128)S(1)}, u32[]{:S(2)}, u32[]{:S(2)}) collective-permute-start(f32[8,2048]{1,0:T(8,128)S(1)} %pad_maximum_fusion.4), channel_id=1, source_target_pairs={{0,2},{1,3},{2,0},{3,1},{4,6},{5,7},{6,4},{7,5},{8,10},{9,11},{10,... | collective-permute-start | bytes 196616 | tf_op jit(solution)/shard_map/ppermute | solution.py:31
  71.3 11.9 %collective-permute-start.11 = (bf16[512,2048]{1,0:T(8,128)(2,1)}, bf16[512,2048]{1,0:T(8,128)(2,1)S(1)}, u32[]{:S(2)}, u32[]{:S(2)}) collective-permute-start(bf16[512,2048]{1,0:T(8,128)(2,1)} %collective-permute-done.10.n_ref.c0_ref.n2_ref), channel_id=1, source_target_pairs={{0,1},{1,0},{2,3},{3,2},{4,5},{5,4},{6,7},{7,6},{8,9},{9,8},{10,11... | collective-permute-start | bytes 6291464 | tf_op jit(solution)/shard_map/ppermute | solution.py:31
  72.5 20.1 %collective-permute-start.12 = (bf16[512,512]{1,0:T(8,128)(2,1)}, bf16[512,512]{1,0:T(8,128)(2,1)S(1)}, u32[]{:S(2)}, u32[]{:S(2)}) collective-permute-start(bf16[512,512]{1,0:T(8,128)(2,1)} %get-tuple-element.133), channel_id=1, source_target_pairs={{0,2},{1,3},{2,0},{3,1},{4,6},{5,7},{6,4},{7,5},{8,10},{9,11},{10,... | collective-permute-start | bytes 1572872 | tf_op jit(solution)/shard_map/ppermute | solution.py:31
  73.1 23.8 %collective-permute-start.13 = (bf16[512,512]{1,0:T(8,128)(2,1)}, bf16[512,512]{1,0:T(8,128)(2,1)S(1)}, u32[]{:S(2)}, u32[]{:S(2)}) collective-permute-start(bf16[512,512]{1,0:T(8,128)(2,1)} %get-tuple-element.134), channel_id=1, source_target_pairs={{0,3},{1,2},{2,1},{3,0},{4,7},{5,6},{6,5},{7,4},{8,11},{9,10},{10,... | collective-permute-start | bytes 1572872 | tf_op jit(solution)/shard_map/ppermute | solution.py:31
  128.3 13.6 %collective-permute-start.15 = (bf16[3,32,2048]{2,1,0:T(8,128)(2,1)S(1)}, bf16[3,32,2048]{2,1,0:T(8,128)(2,1)S(1)}, u32[]{:S(2)}, u32[]{:S(2)}) collective-permute-start(bf16[3,32,2048]{2,1,0:T(8,128)(2,1)S(1)} %fusion.13), channel_id=1, source_target_pairs={{0,8},{1,5},{2,10},{3,7},{8,16},{9,1},{10,18},{11,3},{16,24},{17,9... | collective-permute-start | bytes 1179656 | tf_op jit(solution)/shard_map/ppermute | solution.py:572
  141.7 24.1 %collective-permute-start.17 = (bf16[512,2048]{1,0:T(8,128)(2,1)}, bf16[512,2048]{1,0:T(8,128)(2,1)}, u32[]{:S(2)}, u32[]{:S(2)}) collective-permute-start(bf16[512,2048]{1,0:T(8,128)(2,1)} %get-tuple-element.147), channel_id=1, source_target_pairs={{0,1},{1,0},{2,3},{3,2},{4,5},{5,4},{6,7},{7,6},{8,9},{9,8},{10,11... | collective-permute-start | bytes 6291464 | tf_op jit(solution)/shard_map/ppermute | solution.py:31
  143.1 17.5 %collective-permute-start.16 = (bf16[3,32,2048]{2,1,0:T(8,128)(2,1)S(1)}, bf16[3,32,2048]{2,1,0:T(8,128)(2,1)S(1)}, u32[]{:S(2)}, u32[]{:S(2)}) collective-permute-start(bf16[3,32,2048]{2,1,0:T(8,128)(2,1)S(1)} %fusion.12), channel_id=1, source_target_pairs={{0,8},{1,5},{2,10},{3,7},{8,16},{9,1},{10,18},{11,3},{16,24},{17,9... | collective-permute-start | bytes 1179656 | tf_op jit(solution)/shard_map/ppermute | solution.py:572
  162.8 13.6 %collective-permute-start.19 = (bf16[3,32,2048]{2,1,0:T(8,128)(2,1)S(1)}, bf16[3,32,2048]{2,1,0:T(8,128)(2,1)S(1)}, u32[]{:S(2)}, u32[]{:S(2)}) collective-permute-start(bf16[3,32,2048]{2,1,0:T(8,128)(2,1)S(1)} %slice_bitcast_fusion.8), channel_id=1, source_target_pairs={{0,8},{1,5},{2,10},{3,7},{8,16},{9,1},{10,18},{11,3},{16,24},{17,9... | collective-permute-start | bytes 1179656 | tf_op jit(solution)/shard_map/ppermute | solution.py:572
  164.3 10.6 %collective-permute-start.20 = (bf16[3,32,2048]{2,1,0:T(8,128)(2,1)S(1)}, bf16[3,32,2048]{2,1,0:T(8,128)(2,1)S(1)}, u32[]{:S(2)}, u32[]{:S(2)}) collective-permute-start(bf16[3,32,2048]{2,1,0:T(8,128)(2,1)S(1)} %fusion.11), channel_id=1, source_target_pairs={{0,8},{1,5},{2,10},{3,7},{8,16},{9,1},{10,18},{11,3},{16,24},{17,9... | collective-permute-start | bytes 1179656 | tf_op jit(solution)/shard_map/ppermute | solution.py:572
  167.6 29.4 %collective-permute-start.27 = (bf16[256,2048]{1,0:T(8,128)(2,1)S(1)}, bf16[256,2048]{1,0:T(8,128)(2,1)S(1)}, u32[]{:S(2)}, u32[]{:S(2)}) collective-permute-start(bf16[256,2048]{1,0:T(8,128)(2,1)S(1)} %add_convert_fusion.1), channel_id=1, source_target_pairs={{0,2},{1,3},{2,0},{3,1},{4,6},{5,7},{6,4},{7,5},{8,10},{9,11},{10,... | collective-permute-start | bytes 3145736 | tf_op jit(solution)/shard_map/ppermute | solution.py:31
  176.5 10.4 %collective-permute-start.21 = (bf16[3,32,2048]{2,1,0:T(8,128)(2,1)S(1)}, bf16[3,32,2048]{2,1,0:T(8,128)(2,1)S(1)}, u32[]{:S(2)}, u32[]{:S(2)}) collective-permute-start(bf16[3,32,2048]{2,1,0:T(8,128)(2,1)S(1)} %fusion.9), channel_id=1, source_target_pairs={{0,8},{1,5},{2,10},{3,7},{8,16},{9,1},{10,18},{11,3},{16,24},{17,9... | collective-permute-start | bytes 1179656 | tf_op jit(solution)/shard_map/ppermute | solution.py:572
  216.4 17.6 %collective-permute-start.28 = (bf16[512,2048]{1,0:T(8,128)(2,1)}, bf16[512,2048]{1,0:T(8,128)(2,1)}, u32[]{:S(2)}, u32[]{:S(2)}) collective-permute-start(bf16[512,2048]{1,0:T(8,128)(2,1)} %get-tuple-element.174), channel_id=1, source_target_pairs={{0,1},{1,0},{2,3},{3,2},{4,5},{5,4},{6,7},{7,6},{8,9},{9,8},{10,11... | collective-permute-start | bytes 6291464 | tf_op jit(solution)/shard_map/ppermute | solution.py:31
  227.0 13.2 %collective-permute-start.34 = (bf16[3,32,2048]{2,1,0:T(8,128)(2,1)}, bf16[3,32,2048]{2,1,0:T(8,128)(2,1)}, u32[]{:S(2)}, u32[]{:S(2)}) collective-permute-start(bf16[3,32,2048]{2,1,0:T(8,128)(2,1)} %fusion.2), channel_id=1, source_target_pairs={{0,8},{1,5},{2,10},{3,7},{8,16},{9,1},{10,18},{11,3},{16,24},{17,9... | collective-permute-start | bytes 1179656 | tf_op jit(solution)/shard_map/ppermute | solution.py:572
  228.7 23.6 %collective-permute-start.33 = (bf16[256,2048]{1,0:T(8,128)(2,1)}, bf16[256,2048]{1,0:T(8,128)(2,1)}, u32[]{:S(2)}, u32[]{:S(2)}) collective-permute-start(bf16[256,2048]{1,0:T(8,128)(2,1)} %add_convert_fusion), channel_id=1, source_target_pairs={{0,2},{1,3},{2,0},{3,1},{4,6},{5,7},{6,4},{7,5},{8,10},{9,11},{10,... | collective-permute-start | bytes 3145736 | tf_op jit(solution)/shard_map/ppermute | solution.py:31
  232.4 20.0 %collective-permute-start.36 = (bf16[3,32,2048]{2,1,0:T(8,128)(2,1)}, bf16[3,32,2048]{2,1,0:T(8,128)(2,1)}, u32[]{:S(2)}, u32[]{:S(2)}) collective-permute-start(bf16[3,32,2048]{2,1,0:T(8,128)(2,1)} %collective-permute-done.31.refs_1_), channel_id=1, source_target_pairs={{0,8},{1,5},{2,10},{3,7},{8,16},{9,1},{10,18},{11,3},{16,24},{17,9... | collective-permute-start | bytes 1179656 | tf_op jit(solution)/shard_map/ppermute | solution.py:572
  241.3 12.3 %collective-permute-start.35 = (bf16[3,32,2048]{2,1,0:T(8,128)(2,1)S(1)}, bf16[3,32,2048]{2,1,0:T(8,128)(2,1)S(1)}, u32[]{:S(2)}, u32[]{:S(2)}) collective-permute-start(bf16[3,32,2048]{2,1,0:T(8,128)(2,1)S(1)} %fusion.1), channel_id=1, source_target_pairs={{0,8},{1,5},{2,10},{3,7},{8,16},{9,1},{10,18},{11,3},{16,24},{17,9... | collective-permute-start | bytes 1179656 | tf_op jit(solution)/shard_map/ppermute | solution.py:572
  252.3 10.4 %collective-permute-start.37 = (bf16[3,32,2048]{2,1,0:T(8,128)(2,1)}, bf16[3,32,2048]{2,1,0:T(8,128)(2,1)}, u32[]{:S(2)}, u32[]{:S(2)}) collective-permute-start(bf16[3,32,2048]{2,1,0:T(8,128)(2,1)} %collective-permute-done.36.refs_2_), channel_id=1, source_target_pairs={{0,8},{1,5},{2,10},{3,7},{8,16},{9,1},{10,18},{11,3},{16,24},{17,9... | collective-permute-start | bytes 1179656 | tf_op jit(solution)/shard_map/ppermute | solution.py:572
  253.7 10.4 %collective-permute-start.38 = (bf16[32,2048]{1,0:T(8,128)(2,1)S(1)}, bf16[32,2048]{1,0:T(8,128)(2,1)S(1)}, u32[]{:S(2)}, u32[]{:S(2)}) collective-permute-start(bf16[32,2048]{1,0:T(8,128)(2,1)S(1)} %get-tuple-element.238), channel_id=1, source_target_pairs={{0,1},{1,0},{2,3},{3,2},{4,5},{5,4},{6,7},{7,6},{8,9},{9,8},{10,11... | collective-permute-start | bytes 393224 | tf_op jit(solution)/shard_map/ppermute | solution.py:31
  255.3 23.0 %collective-permute-start.18 = (bf16[2,512,512]{2,1,0:T(8,128)(2,1)}, bf16[2,512,512]{2,1,0:T(8,128)(2,1)S(1)}, u32[]{:S(2)}, u32[]{:S(2)}) collective-permute-start(bf16[2,512,512]{2,1,0:T(8,128)(2,1)} %pad_maximum_fusion), channel_id=1, source_target_pairs={{0,1},{1,0},{2,3},{3,2},{4,5},{5,4},{6,7},{7,6},{8,9},{9,8},{10,11... | collective-permute-start | bytes 3145736 | tf_op jit(solution)/shard_map/ppermute | solution.py:31
  264.2 10.9 %collective-permute-start.41 = (bf16[3,32,2048]{2,1,0:T(8,128)(2,1)S(1)}, bf16[3,32,2048]{2,1,0:T(8,128)(2,1)}, u32[]{:S(2)}, u32[]{:S(2)}) collective-permute-start(bf16[3,32,2048]{2,1,0:T(8,128)(2,1)S(1)} %pad_maximum_fusion.3.refs_0_), channel_id=1, source_target_pairs={{0,8},{1,5},{2,10},{3,7},{8,16},{9,1},{10,18},{11,3},{16,24},{17,9... | collective-permute-start | bytes 1179656 | tf_op jit(solution)/shard_map/ppermute | solution.py:572
  265.9 10.5 %collective-permute-start.40 = (f32[8,2048]{1,0:T(8,128)S(1)}, f32[8,2048]{1,0:T(8,128)S(1)}, u32[]{:S(2)}, u32[]{:S(2)}) collective-permute-start(f32[8,2048]{1,0:T(8,128)S(1)} %pad_maximum_fusion.5), channel_id=1, source_target_pairs={{0,1},{1,0},{2,3},{3,2},{4,5},{5,4},{6,7},{7,6},{8,9},{9,8},{10,11... | collective-permute-start | bytes 196616 | tf_op jit(solution)/shard_map/ppermute | solution.py:31
  287.6 13.4 %collective-permute-start.50 = (bf16[3,32,2048]{2,1,0:T(8,128)(2,1)S(1)}, bf16[3,32,2048]{2,1,0:T(8,128)(2,1)S(1)}, u32[]{:S(2)}, u32[]{:S(2)}) collective-permute-start(bf16[3,32,2048]{2,1,0:T(8,128)(2,1)S(1)} %collective-permute-done.47.refs_6_), channel_id=1, source_target_pairs={{0,8},{1,5},{2,10},{3,7},{8,16},{9,1},{10,18},{11,3},{16,24},{17,9... | collective-permute-start | bytes 1179656 | tf_op jit(solution)/shard_map/ppermute | solution.py:572
  293.8 25.3 %collective-permute-start.43 = (bf16[2,512,512]{2,1,0:T(8,128)(2,1)S(1)}, bf16[2,512,512]{2,1,0:T(8,128)(2,1)}, u32[]{:S(2)}, u32[]{:S(2)}) collective-permute-start(bf16[2,512,512]{2,1,0:T(8,128)(2,1)S(1)} %pad_maximum_fusion.1), channel_id=1, source_target_pairs={{0,2},{1,3},{2,0},{3,1},{4,6},{5,7},{6,4},{7,5},{8,10},{9,11},{10,... | collective-permute-start | bytes 3145736 | tf_op jit(solution)/shard_map/ppermute | solution.py:31
  (55 other events, 558.7 us)
